TPU v7x, 32 devices: a whole 2x2x4 slice. The times are simulated.
32 devices in a mesh: heads: 4 (over x, core), batch: 8 (over z, y).
Axes of the slice: x: 2, y: 2, z: 4, core: 2. Of those that a mesh axis runs over, the one named last changes fastest.
Arguments:
- tokens: bfloat16 [8192, 2048], P('batch'), may hold values from -6 to 6
- lengths: int32 [8], P('batch'), may hold values from 256 to 1024, as said below
- cotangent: bfloat16 [8192, 2048], P('batch'), may hold values from -6 to 6
- attn_norm_gain: bfloat16 [2048], P('batch'), may hold values from 0.5 to 1.5
- query_norm_gain: bfloat16 [128], replicated, may hold values from 0.5 to 1.5
- key_norm_gain: bfloat16 [128], replicated, may hold values from 0.5 to 1.5
- w_query: bfloat16 [2048, 2048], P('batch', 'heads'), may hold values from -0.125 to 0.125
- w_gate_attn: bfloat16 [2048, 2048], P('batch', 'heads'), may hold values from -0.125 to 0.125
- w_key: bfloat16 [2048, 1024], P('batch', 'heads'), may hold values from -0.125 to 0.125
- w_value: bfloat16 [2048, 1024], P('batch', 'heads'), may hold values from -0.125 to 0.125
- w_out: bfloat16 [2048, 2048], P('batch', 'heads'), may hold values from -2 to 2
- mlp_norm_gain: bfloat16 [2048], P('batch'), may hold values from 0.5 to 1.5
- w_gate: bfloat16 [2048, 6144], P('batch', 'heads'), may hold values from -0.125 to 0.125
- w_up: bfloat16 [2048, 6144], P('batch', 'heads'), may hold values from -0.125 to 0.125
- w_down: bfloat16 [2048, 6144], P('batch', 'heads'), may hold values from -0.078125 to 0.078125
Outputs:
- output: bfloat16 [8192, 2048], P('batch')
- grad_tokens: bfloat16 [8192, 2048], P('batch')
- grad_attn_norm_gain: float32 [2048], P('batch')
- grad_query_norm_gain: float32 [128], replicated
- grad_key_norm_gain: float32 [128], replicated
- grad_w_query: float32 [2048, 2048], P('batch', 'heads')
- grad_w_gate_attn: float32 [2048, 2048], P('batch', 'heads')
- grad_w_key: float32 [2048, 1024], P('batch', 'heads')
- grad_w_value: float32 [2048, 1024], P('batch', 'heads')
- grad_w_out: float32 [2048, 2048], P('batch', 'heads')
- grad_mlp_norm_gain: float32 [2048], P('batch')
- grad_w_gate: float32 [2048, 6144], P('batch', 'heads')
- grad_w_up: float32 [2048, 6144], P('batch', 'heads')
- grad_w_down: float32 [2048, 6144], P('batch', 'heads')
- block_rms: float32 [5], replicated
Inputs may be any that keep to these rules, and one draw needn't show every extreme that they name: The sequence of slot s takes the first lengths[s] rows of its 1024 rows, the rest are padding; some sequence fills its slot.
All inputs are finite; a program needn't handle non-finite values.
Results may differ from a plain program's by a relative error of at most 0.024.
Values may be sent and summed in bfloat16 or wider, within the bound.
A program may use at most 256 MiB of HBM per device.

v0:
```python
import jax
import jax.numpy as jnp
from jax import lax
from jax.sharding import PartitionSpec as P

SLOT_LEN = 1024


NORM_EPS = 1e-06
ROPE_THETA = 1000000.0
MASKED = -1e30


def matmul(left_side, right_side):
    return jnp.dot(left_side, right_side, preferred_element_type=jnp.float32)


def contract_last(left_side, right_side):
    return lax.dot_general(
        left_side, right_side, (((1,), (1,)), ((), ())), preferred_element_type=jnp.float32
    )


def contract_rows(left_side, right_side):
    return lax.dot_general(
        left_side, right_side, (((0,), (0,)), ((), ())), preferred_element_type=jnp.float32
    )


def norm_rows(in_value, gain):
    scale_rows = lax.rsqrt(jnp.mean(in_value * in_value, axis=-1, keepdims=True) + NORM_EPS)
    return (in_value * scale_rows * gain, scale_rows)


def norm_back(in_value, scale_rows, gain, grad_normed):
    normed = in_value * scale_rows
    grad_gain = jnp.sum(grad_normed * normed, axis=tuple(range(in_value.ndim - 1)))
    grad_scaled = grad_normed * gain
    grad_value = scale_rows * (
        grad_scaled - normed * jnp.mean(grad_scaled * normed, axis=-1, keepdims=True)
    )
    return (grad_value, grad_gain)


def rotary_tables(row_count, head_width):
    half_width = head_width // 2
    positions = (lax.iota(jnp.int32, row_count) % SLOT_LEN).astype(jnp.float32)
    inverse = ROPE_THETA ** (
        -(lax.iota(jnp.int32, half_width).astype(jnp.float32) * 2.0 / head_width)
    )
    angles = positions[:, None] * inverse[None, :]
    angles = jnp.concatenate([angles, angles], axis=1)
    return (jnp.cos(angles), jnp.sin(angles))


def turn_half(in_value):
    half_width = in_value.shape[-1] // 2
    return jnp.concatenate([-in_value[..., half_width:], in_value[..., :half_width]], axis=-1)


def rotate_rows(in_value, cos_table, sin_table):
    return in_value * cos_table[:, None, :] + turn_half(in_value) * sin_table[:, None, :]


def unrotate_rows(in_value, cos_table, sin_table):
    return in_value * cos_table[:, None, :] - turn_half(in_value) * sin_table[:, None, :]


def block_scores(block_queries, slot_keys, block_index, block_rows, seq_length, scale_factor):
    scores = (
        jnp.einsum("qkgd,ckd->kgqc", block_queries, slot_keys, preferred_element_type=jnp.float32)
        * scale_factor
    )
    key_places = lax.iota(jnp.int32, SLOT_LEN)
    query_places = block_index * block_rows + lax.iota(jnp.int32, block_rows)
    allowed = (key_places[None, :] <= query_places[:, None]) & (key_places[None, :] < seq_length)
    return jnp.where(allowed, scores, MASKED)


def attend_forward(query_rot, key_rot, value_heads, lengths):
    row_count, head_count, head_width = query_rot.shape
    kv_count = key_rot.shape[1]
    group_size = head_count // kv_count
    block_rows = min(512, SLOT_LEN)
    block_count = SLOT_LEN // block_rows
    slot_count = row_count // SLOT_LEN
    scale_factor = head_width ** (-0.5)

    def one_slot(operands):
        slot_queries, slot_keys, slot_values, seq_length = operands
        grouped = slot_queries.reshape(SLOT_LEN, kv_count, group_size, head_width)
        outputs = []
        totals = []
        for block_index in range(block_count):
            lower = block_index * block_rows
            scores = block_scores(
                grouped[lower : lower + block_rows],
                slot_keys,
                block_index,
                block_rows,
                seq_length,
                scale_factor,
            )
            largest = jnp.max(scores, axis=-1, keepdims=True)
            exponent = jnp.exp(scores - largest)
            denominator = jnp.sum(exponent, axis=-1, keepdims=True)
            soft_weights = (exponent / denominator).astype(jnp.bfloat16)
            outputs.append(
                jnp.einsum(
                    "kgqc,ckd->qkgd", soft_weights, slot_values, preferred_element_type=jnp.float32
                )
            )
            totals.append(largest + jnp.log(denominator))
        return (jnp.concatenate(outputs, axis=0), jnp.concatenate(totals, axis=2))

    attended, log_totals = lax.map(
        one_slot,
        (
            query_rot.reshape(slot_count, SLOT_LEN, head_count, head_width),
            key_rot.reshape(slot_count, SLOT_LEN, kv_count, head_width),
            value_heads.reshape(slot_count, SLOT_LEN, kv_count, head_width),
            lengths,
        ),
    )
    return (attended.reshape(row_count, head_count, head_width), log_totals)


def attend_backward(query_rot, key_rot, value_heads, grad_attended, log_totals, lengths):
    row_count, head_count, head_width = query_rot.shape
    kv_count = key_rot.shape[1]
    group_size = head_count // kv_count
    block_rows = min(512, SLOT_LEN)
    block_count = SLOT_LEN // block_rows
    slot_count = row_count // SLOT_LEN
    scale_factor = head_width ** (-0.5)

    def one_slot(operands):
        slot_queries, slot_keys, slot_values, slot_grads, slot_totals, seq_length = operands
        grouped = slot_queries.reshape(SLOT_LEN, kv_count, group_size, head_width)
        grouped_grads = slot_grads.reshape(SLOT_LEN, kv_count, group_size, head_width)
        grad_keys = jnp.zeros((SLOT_LEN, kv_count, head_width), jnp.float32)
        grad_values = jnp.zeros((SLOT_LEN, kv_count, head_width), jnp.float32)
        query_parts = []
        for block_index in range(block_count):
            lower = block_index * block_rows
            block_queries = grouped[lower : lower + block_rows]
            block_grads = grouped_grads[lower : lower + block_rows]
            scores = block_scores(
                block_queries, slot_keys, block_index, block_rows, seq_length, scale_factor
            )
            probs_true = jnp.exp(scores - slot_totals[:, :, lower : lower + block_rows])
            grad_probs = jnp.einsum(
                "qkgd,ckd->kgqc", block_grads, slot_values, preferred_element_type=jnp.float32
            )
            inner_sum = jnp.sum(grad_probs * probs_true, axis=-1, keepdims=True)
            grad_scores = (probs_true * (grad_probs - inner_sum)).astype(jnp.bfloat16)
            query_parts.append(
                jnp.einsum(
                    "kgqc,ckd->qkgd", grad_scores, slot_keys, preferred_element_type=jnp.float32
                )
                * scale_factor
            )
            grad_keys = (
                grad_keys
                + jnp.einsum(
                    "kgqc,qkgd->ckd", grad_scores, block_queries, preferred_element_type=jnp.float32
                )
                * scale_factor
            )
            grad_values = grad_values + jnp.einsum(
                "kgqc,qkgd->ckd",
                probs_true.astype(jnp.bfloat16),
                block_grads,
                preferred_element_type=jnp.float32,
            )
        return (jnp.concatenate(query_parts, axis=0), grad_keys, grad_values)

    grad_queries, grad_keys, grad_values = lax.map(
        one_slot,
        (
            query_rot.reshape(slot_count, SLOT_LEN, head_count, head_width),
            key_rot.reshape(slot_count, SLOT_LEN, kv_count, head_width),
            value_heads.reshape(slot_count, SLOT_LEN, kv_count, head_width),
            grad_attended.reshape(slot_count, SLOT_LEN, head_count, head_width),
            log_totals,
            lengths,
        ),
    )
    return (
        grad_queries.reshape(row_count, head_count, head_width),
        grad_keys.reshape(row_count, kv_count, head_width),
        grad_values.reshape(row_count, kv_count, head_width),
    )


def local(
    tokens,
    lengths,
    cotangent,
    attn_norm_gain,
    query_norm_gain,
    key_norm_gain,
    w_query,
    w_gate_attn,
    w_key,
    w_value,
    w_out,
    mlp_norm_gain,
    w_gate,
    w_up,
    w_down,
):
    row_count, model_width = tokens.shape
    head_width = query_norm_gain.shape[0]
    attn_full = (
        lax.all_gather(w_query, "batch", axis=0, tiled=True),
        lax.all_gather(w_gate_attn, "batch", axis=0, tiled=True),
        lax.all_gather(w_key, "batch", axis=0, tiled=True),
        lax.all_gather(w_value, "batch", axis=0, tiled=True),
        lax.all_gather(w_out, "batch", axis=0, tiled=True),
        lax.all_gather(attn_norm_gain, "batch", axis=0, tiled=True),
    )
    mlp_full = (
        lax.all_gather(w_gate, "batch", axis=0, tiled=True),
        lax.all_gather(w_up, "batch", axis=0, tiled=True),
        lax.all_gather(w_down, "batch", axis=0, tiled=True),
        lax.all_gather(mlp_norm_gain, "batch", axis=0, tiled=True),
    )
    query_full, gate_attn_full, key_full, value_full, out_full, gain_raw_one = attn_full
    gate_full, up_full, down_full, gain_raw_two = mlp_full
    gain_one = gain_raw_one.astype(jnp.float32)
    gain_two = gain_raw_two.astype(jnp.float32)
    query_gain = query_norm_gain.astype(jnp.float32)
    key_gain = key_norm_gain.astype(jnp.float32)
    valid = (
        (lax.iota(jnp.int32, SLOT_LEN)[None, :] < lengths[:, None])
        .reshape(row_count, 1)
        .astype(jnp.float32)
    )
    tokens_f = tokens.astype(jnp.float32)
    normed_one, scale_one = norm_rows(tokens_f, gain_one)
    input_one = normed_one.astype(jnp.bfloat16)
    queries = matmul(input_one, query_full)
    gate_logit = matmul(input_one, gate_attn_full)
    keys_pre = matmul(input_one, key_full)
    values = matmul(input_one, value_full).astype(jnp.bfloat16)
    head_count = queries.shape[1] // head_width
    kv_count = keys_pre.shape[1] // head_width
    cos_table, sin_table = rotary_tables(row_count, head_width)
    queries = queries.reshape(row_count, head_count, head_width)
    keys_pre = keys_pre.reshape(row_count, kv_count, head_width)
    query_normed, query_scale = norm_rows(queries, query_gain)
    key_normed, key_scale = norm_rows(keys_pre, key_gain)
    query_rot = rotate_rows(query_normed, cos_table, sin_table).astype(jnp.bfloat16)
    key_rot = rotate_rows(key_normed, cos_table, sin_table).astype(jnp.bfloat16)
    value_heads = values.reshape(row_count, kv_count, head_width)
    attended, log_totals = attend_forward(query_rot, key_rot, value_heads, lengths)
    gate_sig = jax.nn.sigmoid(gate_logit.reshape(row_count, head_count, head_width))
    gated = (attended * gate_sig).reshape(row_count, head_count * head_width).astype(jnp.bfloat16)
    attn_out = lax.psum(contract_last(gated, out_full).astype(jnp.bfloat16), "heads").astype(
        jnp.float32
    )
    hidden_res = tokens_f + attn_out
    normed_two, scale_two = norm_rows(hidden_res, gain_two)
    input_two = normed_two.astype(jnp.bfloat16)
    gate_pre = matmul(input_two, gate_full)
    up_pre = matmul(input_two, up_full)
    gate_act = jax.nn.sigmoid(gate_pre)
    activated = (gate_pre * gate_act * up_pre).astype(jnp.bfloat16)
    mlp_out = lax.psum(contract_last(activated, down_full).astype(jnp.bfloat16), "heads").astype(
        jnp.float32
    )
    summed = hidden_res + mlp_out
    output = (summed * valid).astype(jnp.bfloat16)

    def masked_square(field):
        return jnp.sum(valid * field * field)

    squares = jnp.stack(
        [
            masked_square(tokens_f),
            masked_square(hidden_res),
            masked_square(summed),
            masked_square(attn_out),
            masked_square(mlp_out),
        ]
    )
    token_count = jnp.sum(lengths).astype(jnp.float32)
    grad_out = cotangent.astype(jnp.float32) * valid
    grad_mlp = grad_out.astype(jnp.bfloat16)
    grad_activated = matmul(grad_mlp, down_full)
    grad_w_down = contract_rows(grad_mlp, activated)
    grad_gate_pre = (
        grad_activated * up_pre * gate_act * (1.0 + gate_pre * (1.0 - gate_act))
    ).astype(jnp.bfloat16)
    grad_up_pre = (grad_activated * gate_pre * gate_act).astype(jnp.bfloat16)
    grad_w_gate = contract_rows(input_two, grad_gate_pre)
    grad_w_up = contract_rows(input_two, grad_up_pre)
    grad_input_two = lax.psum(
        (contract_last(grad_gate_pre, gate_full) + contract_last(grad_up_pre, up_full)).astype(
            jnp.bfloat16
        ),
        "heads",
    ).astype(jnp.float32)
    grad_norm_two, grad_gain_two = norm_back(hidden_res, scale_two, gain_two, grad_input_two)
    grad_hidden = grad_out + grad_norm_two
    grad_attn = grad_hidden.astype(jnp.bfloat16)
    grad_gated = matmul(grad_attn, out_full).reshape(row_count, head_count, head_width)
    grad_w_out = contract_rows(grad_attn, gated)
    grad_attended = (grad_gated * gate_sig).astype(jnp.bfloat16)
    grad_gate_logit = (
        (grad_gated * attended * gate_sig * (1.0 - gate_sig))
        .astype(jnp.bfloat16)
        .reshape(row_count, head_count * head_width)
    )
    grad_query_rot, grad_key_rot, grad_value_heads = attend_backward(
        query_rot, key_rot, value_heads, grad_attended, log_totals, lengths
    )
    grad_values = grad_value_heads.reshape(row_count, kv_count * head_width).astype(jnp.bfloat16)
    grad_query_pre, grad_query_gain = norm_back(
        queries, query_scale, query_gain, unrotate_rows(grad_query_rot, cos_table, sin_table)
    )
    grad_key_pre, grad_key_gain = norm_back(
        keys_pre, key_scale, key_gain, unrotate_rows(grad_key_rot, cos_table, sin_table)
    )
    grad_queries = grad_query_pre.reshape(row_count, head_count * head_width).astype(jnp.bfloat16)
    grad_keys = grad_key_pre.reshape(row_count, kv_count * head_width).astype(jnp.bfloat16)
    grad_w_query = contract_rows(input_one, grad_queries)
    grad_w_gate_attn = contract_rows(input_one, grad_gate_logit)
    grad_w_key = contract_rows(input_one, grad_keys)
    grad_w_value = contract_rows(input_one, grad_values)
    grad_input_part = (
        contract_last(grad_queries, query_full)
        + contract_last(grad_gate_logit, gate_attn_full)
        + contract_last(grad_keys, key_full)
        + contract_last(grad_values, value_full)
    )
    grad_input_one, query_gain_heads, key_gain_heads = (
        lax.psum(grad_input_part.astype(jnp.bfloat16), "heads").astype(jnp.float32),
        lax.psum(grad_query_gain.astype(jnp.bfloat16), "heads").astype(jnp.float32),
        lax.psum(grad_key_gain.astype(jnp.bfloat16), "heads").astype(jnp.float32),
    )
    grad_norm_one, grad_gain_one = norm_back(tokens_f, scale_one, gain_one, grad_input_one)
    grad_tokens = (grad_hidden + grad_norm_one).astype(jnp.bfloat16)
    everything = (
        lax.psum_scatter(
            grad_w_query.astype(jnp.bfloat16), "batch", scatter_dimension=0, tiled=True
        ).astype(jnp.float32),
        lax.psum_scatter(
            grad_w_gate_attn.astype(jnp.bfloat16), "batch", scatter_dimension=0, tiled=True
        ).astype(jnp.float32),
        lax.psum_scatter(
            grad_w_key.astype(jnp.bfloat16), "batch", scatter_dimension=0, tiled=True
        ).astype(jnp.float32),
        lax.psum_scatter(
            grad_w_value.astype(jnp.bfloat16), "batch", scatter_dimension=0, tiled=True
        ).astype(jnp.float32),
        lax.psum_scatter(
            grad_w_out.astype(jnp.bfloat16), "batch", scatter_dimension=0, tiled=True
        ).astype(jnp.float32),
        lax.psum_scatter(
            grad_gain_one.astype(jnp.bfloat16), "batch", scatter_dimension=0, tiled=True
        ).astype(jnp.float32),
        lax.psum_scatter(
            grad_w_gate.astype(jnp.bfloat16), "batch", scatter_dimension=0, tiled=True
        ).astype(jnp.float32),
        lax.psum_scatter(
            grad_w_up.astype(jnp.bfloat16), "batch", scatter_dimension=0, tiled=True
        ).astype(jnp.float32),
        lax.psum_scatter(
            grad_w_down.astype(jnp.bfloat16), "batch", scatter_dimension=0, tiled=True
        ).astype(jnp.float32),
        lax.psum_scatter(
            grad_gain_two.astype(jnp.bfloat16), "batch", scatter_dimension=0, tiled=True
        ).astype(jnp.float32),
    )
    attn_grads = everything[:6]
    mlp_grads = everything[6:]
    squares_all, count_all, query_gain_all, key_gain_all = lax.psum(
        (squares, token_count, query_gain_heads, key_gain_heads), "batch"
    )
    block_rms = jnp.sqrt(squares_all / (count_all * model_width))
    return (
        output,
        grad_tokens,
        attn_grads[5],
        query_gain_all,
        key_gain_all,
        attn_grads[0],
        attn_grads[1],
        attn_grads[2],
        attn_grads[3],
        attn_grads[4],
        mlp_grads[3],
        mlp_grads[0],
        mlp_grads[1],
        mlp_grads[2],
        block_rms,
    )


def solution(mesh):
    return jax.shard_map(
        local,
        mesh=mesh,
        in_specs=(
            P("batch", None),
            P("batch"),
            P("batch", None),
            P("batch"),
            P(),
            P(),
            P("batch", "heads"),
            P("batch", "heads"),
            P("batch", "heads"),
            P("batch", "heads"),
            P("batch", "heads"),
            P("batch"),
            P("batch", "heads"),
            P("batch", "heads"),
            P("batch", "heads"),
        ),
        out_specs=(
            P("batch", None),
            P("batch", None),
            P("batch"),
            P(),
            P(),
            P("batch", "heads"),
            P("batch", "heads"),
            P("batch", "heads"),
            P("batch", "heads"),
            P("batch", "heads"),
            P("batch"),
            P("batch", "heads"),
            P("batch", "heads"),
            P("batch", "heads"),
            P(),
        ),
        check_vma=False,
    )
```

profile of v0, /device:TPU:0, one launch (start us, length us, event | category | flops | bytes accessed | tf_op | source)
XLA Modules:
  0.0 1691.6 jit_solution(17954588877183765486)
XLA Ops:
  11.5 22.4 %all-gather = bf16[8,1,256]{2,1,0:T(2,128)(2,1)S(1)} all-gather(bf16[1,1,256]{2,1,0:T(2,128)(2,1)S(1)} %reshape.312), channel_id=1, replica_groups=mesh['heads'=4,'batch'=8] {'batch'}, dimensions={0}, use_global_device_ids=true | all-gather | bytes 4608 | tf_op jit(solution)/shard_map/all_gather | solution.py:221
  33.9 3.1 fusion.21
  37.2 2.4 fusion.86
  40.3 3.0 fusion.18
  43.9 9.3 all-gather.13.cloned.1.call-done
  53.2 3.8 multiply_reduce_fusion.5
  58.4 35.9 %all-gather.11.cloned.1.call-done = bf16[2048,256]{1,0:T(8,128)(2,1)} async-done(((bf16[256,256]{1,0:T(8,128)(2,1)}), bf16[2048,256]{1,0:T(8,128)(2,1)}) %all-gather.11.cloned.1.call-update) | async-done | bytes 1048592 | tf_op jit(solution)/shard_map/all_gather | solution.py:219
  94.3 3.8 convolution_convert_fusion.10
  98.1 46.2 %all-gather.15.cloned.1.call-done = bf16[2048,512]{1,0:T(8,128)(2,1)} async-done(((bf16[256,512]{1,0:T(8,128)(2,1)}), bf16[2048,512]{1,0:T(8,128)(2,1)}) %all-gather.15.cloned.1.call-update) | async-done | bytes 2097168 | tf_op jit(solution)/shard_map/all_gather | solution.py:216
  144.3 5.3 multiply_reduce_fusion.2
  161.9 32.0 %all-gather.17.cloned.1.call-done = bf16[2048,512]{1,0:T(8,128)(2,1)} async-done(((bf16[256,512]{1,0:T(8,128)(2,1)}), bf16[2048,512]{1,0:T(8,128)(2,1)}) %all-gather.17.cloned.1.call-update) | async-done | bytes 2097168 | tf_op jit(solution)/shard_map/all_gather | solution.py:217
  193.9 7.2 fusion.52
  201.1 42.4 %all-gather.19.cloned.1.call-done = bf16[2048,512]{1,0:T(8,128)(2,1)} async-done(((bf16[256,512]{1,0:T(8,128)(2,1)}), bf16[2048,512]{1,0:T(8,128)(2,1)}) %all-gather.19.cloned.1.call-update) | async-done | bytes 2097168 | tf_op jit(solution)/shard_map/all_gather | solution.py:220
  243.6 6.3 convolution_convert_fusion.4
  252.2 18.1 %all-gather.1 = bf16[8,1,256]{2,1,0:T(2,128)(2,1)S(1)} all-gather(bf16[1,1,256]{2,1,0:T(2,128)(2,1)S(1)} %reshape.314), channel_id=1, replica_groups=mesh['heads'=4,'batch'=8] {'batch'}, dimensions={0}, use_global_device_ids=true | all-gather | bytes 4608 | tf_op jit(solution)/shard_map/all_gather | solution.py:227
  270.4 63.7 %all-reduce.10.cloned.1.call-done = bf16[1024,2048]{1,0:T(8,128)(2,1)} async-done(((bf16[1024,2048]{1,0:T(8,128)(2,1)}), bf16[1024,2048]{1,0:T(8,128)(2,1)}) %all-reduce.10.cloned.1.call-update) | async-done | bytes 4194320 | tf_op jit(solution)/shard_map/psum | solution.py:260
  334.1 5.0 multiply_reduce_fusion
  340.0 4.4 multiply_convert_fusion.1
  344.5 90.7 %all-gather.21.cloned.1.call-done = bf16[2048,1536]{1,0:T(8,128)(2,1)} async-done(((bf16[256,1536]{1,0:T(8,128)(2,1)}), bf16[2048,1536]{1,0:T(8,128)(2,1)}) %all-gather.21.cloned.1.call-update) | async-done | bytes 6291472 | tf_op jit(solution)/shard_map/all_gather | solution.py:224
  435.1 11.8 fusion.97
  446.9 87.3 %all-gather.23.cloned.1.call-done = bf16[2048,1536]{1,0:T(8,128)(2,1)} async-done(((bf16[256,1536]{1,0:T(8,128)(2,1)}), bf16[2048,1536]{1,0:T(8,128)(2,1)}) %all-gather.23.cloned.1.call-update) | async-done | bytes 6291472 | tf_op jit(solution)/shard_map/all_gather | solution.py:225
  534.2 11.7 fusion.98
  546.0 87.4 %all-gather.25.cloned.1.call-done = bf16[2048,1536]{1,0:T(8,128)(2,1)} async-done(((bf16[256,1536]{1,0:T(8,128)(2,1)}), bf16[2048,1536]{1,0:T(8,128)(2,1)}) %all-gather.25.cloned.1.call-update) | async-done | bytes 6291472 | tf_op jit(solution)/shard_map/all_gather | solution.py:226
  633.3 16.9 %multiply_convert_fusion.2 = (bf16[1024,1536]{1,0:T(8,128)(2,1)}, bf16[1024,1536]{1,0:T(8,128)(2,1)S(1)}, bf16[1024,1536]{1,0:T(8,128)(2,1)}) fusion(f32[1024,1536]{1,0:T(8,128)} %fusion.97, f32[1024,1536]{1,0:T(8,128)} %fusion.98, bf16[2048,1536]{1,0:T(8,128)(2,1)} %all-gather.25.cloned.1.call-done, bf16[1024,2048]{1,0:T(8,128)(2,1)} %param.17, ...), kind=kOutput, calls=%fused_computation.69 | convolution fusion | flops 6473908224 | bytes 32509952 | tf_op jit(solution)/shard_map/dot_general | solution.py:15
  650.3 10.0 fusion.99
  660.3 10.3 convolution_convert_fusion.3
  670.6 8.3 add_convert_fusion.1
  679.1 151.1 %all-reduce.14.cloned.1.call-done = (bf16[1024,2048]{1,0:T(8,128)(2,1)}, bf16[1024,2048]{1,0:T(8,128)(2,1)}) async-done(((bf16[1024,2048]{1,0:T(8,128)(2,1)}, bf16[1024,2048]{1,0:T(8,128)(2,1)}), (bf16[1024,2048]{1,0:T(8,128)(2,1)}, bf16[1024,2048]{1,0:T(8,128)(2,1)})) %all-reduce.14.cloned.1.call-update) | async-done | bytes 8388624 | tf_op jit(solution)/shard_map/psum | solution.py:270
  830.2 15.1 fusion.14
  845.3 5.4 fusion.12
  850.7 6.9 fusion.55
  860.0 2.5 fusion.25
  863.7 2.5 convolution_bitcast_fusion
  868.2 2.5 fusion.66
  870.7 2.4 fusion.28
  880.3 5.3 fusion.78
  886.5 2.4 convolution_convert_fusion.8
  889.0 4.3 fusion.74
  900.4 4.8 fusion.50
  905.2 5.6 fusion.100
  912.8 5.6 fusion.101
  918.4 9.3 add_convert_fusion
  928.9 5.9 convolution_convert_fusion.7
  935.1 7.1 convolution_convert_fusion.5
  942.3 5.9 convolution_convert_fusion.6
  948.3 11.5 convolution_convert_fusion.2
  961.7 11.1 convolution_convert_fusion.1
  974.7 11.8 convolution_convert_fusion
  988.4 3.3 stack.23
  991.7 6.0 all-reduce.4
  997.7 22.5 %all-reduce.2 = (f32[128]{0:T(128)}, f32[128]{0:T(128)}, f32[5]{0:T(128)S(1)}, f32[]{:T(128)}) all-reduce(bf16[128]{0:T(256)(128)(2,1)S(1)} %get-tuple-element.85, bf16[128]{0:T(256)(128)(2,1)S(1)} %get-tuple-element.86, f32[5]{0:T(128)S(1)} %stack.23, f32[]{:T(128)S(6)} %convert_element_type.299), channel_id=1, replica_groups=mesh['heads'=4,'batch'=8] {'batch'}, use_global_device_ids=true, to_apply=%region_23.24 | all-reduce | flops 262 | bytes 1584 | tf_op jit(solution)/shard_map/psum | solution.py:379
  1024.6 82.2 %all-reduce.12.cloned.1.call-done = bf16[1024,2048]{1,0:T(8,128)(2,1)} async-done(((bf16[1024,2048]{1,0:T(8,128)(2,1)}), bf16[1024,2048]{1,0:T(8,128)(2,1)}) %all-reduce.12.cloned.1.call-update) | async-done | bytes 4194320 | tf_op jit(solution)/shard_map/psum | solution.py:339
  1106.9 5.0 fusion.20
  1111.8 22.1 %all-reduce.3 = (bf16[2048]{0:T(1024)(128)(2,1)S(1)}, bf16[2048]{0:T(1024)(128)(2,1)S(1)}) all-reduce(bf16[2048]{0:T(1024)(128)(2,1)S(1)} %get-tuple-element.70, bf16[2048]{0:T(1024)(128)(2,1)S(1)} %get-tuple-element.73), channel_id=2, replica_groups=mesh['heads'=4,'batch'=8] {'batch'}, use_global_device_ids=true, to_apply=%region_19.20.clone | all-reduce | flops 4096 | bytes 16384
  1134.6 9.0 fusion.9
  1143.6 35.3 %reduce-scatter.9.cloned.1.call-done = bf16[256,512]{1,0:T(8,128)(2,1)} async-done(((bf16[2048,512]{1,0:T(8,128)(2,1)}), bf16[256,512]{1,0:T(8,128)(2,1)}) %reduce-scatter.9.cloned.1.call-update) | async-done | bytes 262160 | tf_op jit(solution)/shard_map/reduce_scatter | solution.py:346
  1180.7 68.9 %reduce-scatter.17.cloned.1.call-done = bf16[256,512]{1,0:T(8,128)(2,1)} async-done(((bf16[2048,512]{1,0:T(8,128)(2,1)}), bf16[256,512]{1,0:T(8,128)(2,1)}) %reduce-scatter.17.cloned.1.call-update) | async-done | bytes 262160 | tf_op jit(solution)/shard_map/reduce_scatter | solution.py:358
  1251.4 68.9 %reduce-scatter.11.cloned.1.call-done = bf16[256,512]{1,0:T(8,128)(2,1)} async-done(((bf16[2048,512]{1,0:T(8,128)(2,1)}), bf16[256,512]{1,0:T(8,128)(2,1)}) %reduce-scatter.11.cloned.1.call-update) | async-done | bytes 262160 | tf_op jit(solution)/shard_map/reduce_scatter | solution.py:349
  1322.1 118.7 %reduce-scatter.19.cloned.1.call-done = bf16[256,1536]{1,0:T(8,128)(2,1)} async-done(((bf16[2048,1536]{1,0:T(8,128)(2,1)}), bf16[256,1536]{1,0:T(8,128)(2,1)}) %reduce-scatter.19.cloned.1.call-update) | async-done | bytes 786448 | tf_op jit(solution)/shard_map/reduce_scatter | solution.py:364
  1440.8 2.5 convert_element_type.294
  1443.2 118.3 %reduce-scatter.21.cloned.1.call-done = bf16[256,1536]{1,0:T(8,128)(2,1)} async-done(((bf16[2048,1536]{1,0:T(8,128)(2,1)}), bf16[256,1536]{1,0:T(8,128)(2,1)}) %reduce-scatter.21.cloned.1.call-update) | async-done | bytes 786448 | tf_op jit(solution)/shard_map/reduce_scatter | solution.py:367
  1561.5 2.5 convert_element_type.296
  1564.0 118.4 %reduce-scatter.23.cloned.1.call-done = bf16[256,1536]{1,0:T(8,128)(2,1)} async-done(((bf16[2048,1536]{1,0:T(8,128)(2,1)}), bf16[256,1536]{1,0:T(8,128)(2,1)}) %reduce-scatter.23.cloned.1.call-update) | async-done | bytes 786448 | tf_op jit(solution)/shard_map/reduce_scatter | solution.py:370
  1682.4 2.5 convert_element_type.298
  (248 shorter events, 60.5 us)
Async XLA Ops:
  7.2 29.9 %copy-start.56 = (bf16[128]{0:T(256)(128)(2,1)S(1)}, bf16[128]{0:T(256)(128)(2,1)}, u32[]{:S(2)}) copy-start(bf16[128]{0:T(256)(128)(2,1)} %param.20) | copy-start | bytes 772
  7.2 32.4 %copy-start.57 = (bf16[128]{0:T(256)(128)(2,1)S(1)}, bf16[128]{0:T(256)(128)(2,1)}, u32[]{:S(2)}) copy-start(bf16[128]{0:T(256)(128)(2,1)} %param.19) | copy-start | bytes 772
  7.2 46.0 %all-gather.13.cloned.1.call-start = ((), (), s32[]{:S(2)}) async-start(), calls=%async_computation.9 | async-start | bytes 1179648 | tf_op jit(solution)/shard_map/all_gather | solution.py:218
  7.9 86.4 %all-gather.11.cloned.1.call-start = ((), (), s32[]{:S(2)}) async-start(), calls=%async_computation.8 | async-start | bytes 1179648 | tf_op jit(solution)/shard_map/all_gather | solution.py:219
  8.7 135.6 %all-gather.15.cloned.1.call-start = ((), (), s32[]{:S(2)}) async-start(), calls=%async_computation.10 | async-start | bytes 2359296 | tf_op jit(solution)/shard_map/all_gather | solution.py:216
  9.4 184.5 %all-gather.17.cloned.1.call-start = ((), (), s32[]{:S(2)}) async-start(), calls=%async_computation.11 | async-start | bytes 2359296 | tf_op jit(solution)/shard_map/all_gather | solution.py:217
  10.0 233.6 %all-gather.19.cloned.1.call-start = ((), (), s32[]{:S(2)}) async-start(), calls=%async_computation.12 | async-start | bytes 2359296 | tf_op jit(solution)/shard_map/all_gather | solution.py:220
  10.6 323.5 %all-reduce.10.cloned.1.call-start = ((), (), s32[]{:S(2)}) async-start(), calls=%async_computation.13 | async-start | bytes 8388608 | tf_op jit(solution)/shard_map/psum | solution.py:260
  10.6 29.7 %copy-start = (bf16[1024,2048]{1,0:T(8,128)(2,1)S(1)}, bf16[1024,2048]{1,0:T(8,128)(2,1)}, u32[]{:S(2)}) copy-start(bf16[1024,2048]{1,0:T(8,128)(2,1)} %param.15) | copy-start | bytes 12582916
  33.9 9.4 copy-start.47
  37.0 6.3 copy-start.49
  37.1 20.2 %copy-start.51 = (f32[128]{0:T(128)}, f32[128]{0:T(128)S(1)}, u32[]{:S(2)}) copy-start(f32[128]{0:T(128)S(1)} %convert_element_type.235) | copy-start | bytes 1540
  39.6 110.6 %copy-start.13 = (f32[1024,128]{0,1:T(8,128)}, f32[1024,128]{0,1:T(8,128)S(1)}, u32[]{:S(2)}) copy-start(f32[1024,128]{0,1:T(8,128)S(1)} %get-tuple-element.112) | copy-start | bytes 1572868
  39.6 110.6 %copy-start.18 = (f32[1024,128]{0,1:T(8,128)}, f32[1024,128]{0,1:T(8,128)S(1)}, u32[]{:S(2)}) copy-start(f32[1024,128]{0,1:T(8,128)S(1)} %get-tuple-element.113) | copy-start | bytes 1572868
  58.4 96.3 %copy-start.24 = (bf16[1024,2,128,1]{0,2,3,1:T(8,128)(2,1)}, bf16[1024,2,128,1]{0,2,3,1:T(8,128)(2,1)S(1)}, u32[]{:S(2)}) copy-start(bf16[1024,2,128,1]{0,2,3,1:T(8,128)(2,1)S(1)} %fusion.84) | copy-start | bytes 1572868
  153.5 4.3 copy-start.4
  249.9 185.2 %all-gather.21.cloned.1.call-start = ((), (), s32[]{:S(2)}) async-start(), calls=%async_computation.14 | async-start | bytes 7077888 | tf_op jit(solution)/shard_map/all_gather | solution.py:224
  250.7 283.6 %all-gather.23.cloned.1.call-start = ((), (), s32[]{:S(2)}) async-start(), calls=%async_computation.15 | async-start | bytes 7077888 | tf_op jit(solution)/shard_map/all_gather | solution.py:225
  251.4 381.9 %all-gather.25.cloned.1.call-start = ((), (), s32[]{:S(2)}) async-start(), calls=%async_computation.16 | async-start | bytes 7077888 | tf_op jit(solution)/shard_map/all_gather | solution.py:226
  252.2 578.0 %all-reduce.14.cloned.1.call-start = ((), (), s32[]{:S(2)}) async-start(), calls=%async_computation.26 | async-start | bytes 16777216 | tf_op jit(solution)/shard_map/psum | solution.py:270
  334.1 5.0 copy-start.1
  334.1 5.9 copy-start.6
  650.3 10.0 copy-start.61
  650.3 10.0 copy-start.53
  650.3 20.3 %slice-start.4 = ((s8[6291456]{0:T(1024)(128)(4,1)}), s8[4194304]{0:T(1024)(128)(4,1)S(1)}, s32[]{:S(2)}) async-start(s8[6291456]{0:T(1024)(128)(4,1)} %bitcast.267), calls=%async_computation.31 | async-start | bytes 8388608
  660.3 10.3 slice-start.5
  660.3 10.3 copy-start.63
  679.0 342.4 %reduce-scatter.15.cloned.1.call-start = ((), (), s32[]{:S(2)}) async-start(), calls=%async_computation.21 | async-start | bytes 1179648 | tf_op jit(solution)/shard_map/reduce_scatter | solution.py:355
  830.2 15.1 copy-start.2
  830.2 15.1 copy-start.7
  830.2 15.1 copy-start.21
  845.3 5.5 copy-start.39
  850.7 6.9 copy-start.5
  850.7 7.0 slice-start
  850.7 7.5 slice-start.1
  860.0 6.1 slice-start.2
  860.0 6.1 slice-start.3
  863.7 11.9 copy-start.22
  875.3 5.0 copy-start.17
  875.5 4.8 copy-start.26
  875.5 4.8 copy-start.28
  880.3 6.2 copy-start.33
  888.9 4.5 copy-start.12
  888.9 4.5 copy-start.46
  889.0 4.5 copy-start.52
  889.0 134.0 %reduce-scatter.13.cloned.1.call-start = ((), (), s32[]{:S(2)}) async-start(), calls=%async_computation.20 | async-start | bytes 1179648 | tf_op jit(solution)/shard_map/reduce_scatter | solution.py:352
  889.0 4.4 copy-start.15
  889.0 4.4 copy-start.20
  899.9 206.9 %all-reduce.12.cloned.1.call-start = ((), (), s32[]{:S(2)}) async-start(), calls=%async_computation.17 | async-start | bytes 8388608 | tf_op jit(solution)/shard_map/psum | solution.py:339
  900.4 4.8 copy-start.54
  905.2 5.7 copy-start.42
  905.2 5.7 copy-start.36
  905.2 5.7 copy-start.40
  912.8 5.6 copy-start.38
  912.8 5.6 copy-start.44
  927.7 7.4 copy-start.60
  927.7 251.1 %reduce-scatter.9.cloned.1.call-start = ((), (), s32[]{:S(2)}) async-start(), calls=%async_computation.18 | async-start | bytes 2359296 | tf_op jit(solution)/shard_map/reduce_scatter | solution.py:346
  934.9 314.7 %reduce-scatter.17.cloned.1.call-start = ((), (), s32[]{:S(2)}) async-start(), calls=%async_computation.22 | async-start | bytes 2359296 | tf_op jit(solution)/shard_map/reduce_scatter | solution.py:358
  942.3 378.0 %reduce-scatter.11.cloned.1.call-start = ((), (), s32[]{:S(2)}) async-start(), calls=%async_computation.19 | async-start | bytes 2359296 | tf_op jit(solution)/shard_map/reduce_scatter | solution.py:349
  948.2 492.5 %reduce-scatter.19.cloned.1.call-start = ((), (), s32[]{:S(2)}) async-start(), calls=%async_computation.23 | async-start | bytes 7077888 | tf_op jit(solution)/shard_map/reduce_scatter | solution.py:364
  959.8 601.7 %reduce-scatter.21.cloned.1.call-start = ((), (), s32[]{:S(2)}) async-start(), calls=%async_computation.24 | async-start | bytes 7077888 | tf_op jit(solution)/shard_map/reduce_scatter | solution.py:367
  972.8 709.6 %reduce-scatter.23.cloned.1.call-start = ((), (), s32[]{:S(2)}) async-start(), calls=%async_computation.25 | async-start | bytes 7077888 | tf_op jit(solution)/shard_map/reduce_scatter | solution.py:370
  986.4 120.4 %copy-start.48 = (f32[8,1,256]{2,1,0:T(1,128)S(1)}, f32[8,1,256]{2,1,0:T(1,128)}, u32[]{:S(2)}) copy-start(f32[8,1,256]{2,1,0:T(1,128)} %copy-done.47) | copy-start | bytes 24580
  986.4 120.4 %copy-start.50 = (f32[1024]{0:T(1024)S(1)}, f32[1024]{0:T(1024)}, u32[]{:S(2)}) copy-start(f32[1024]{0:T(1024)} %copy-done.49) | copy-start | bytes 12292
  (26 other events, 51.3 us)
Sparse Core Ops, SparseCore 0:
  10.1 43.0 all-gather.12
  55.3 38.9 all-gather.10
  96.5 47.7 all-gather.14
  146.3 47.6 all-gather.16
  195.9 47.6 all-gather.18
  250.0 84.0 all-reduce.9
  336.3 98.8 all-gather.20
  437.3 96.8 all-gather.22
  536.4 96.8 all-gather.24
  679.1 151.0 all-reduce.13
  889.1 64.3 reduce-scatter.14
  956.7 63.2 reduce-scatter.12
  1022.4 84.3 all-reduce.11
  1110.2 68.6 reduce-scatter.8
  1182.3 67.2 reduce-scatter.16
  1253.0 67.2 reduce-scatter.10
  1323.7 116.9 reduce-scatter.18
  1444.2 117.2 reduce-scatter.20
  1565.1 117.2 reduce-scatter.22
where the time goes:
time: 1690 us
  waiting for transfers between devices  1260 us (75%)
  matrix products  209 us (12%)
  blocking collectives  91.2 us (5%)
  other arithmetic  89.9 us (5%)
  local copies, waits for them, and re-layouts  20.2 us (1%)
  between operations  17.3 us (1%)
    psum x1, waiting for transfers between devices, local(): lax.psum(contract_last(activated, down_full).astype(jnp.bfloat16), 'heads')  151 us
    reduce_scatter x1, waiting for transfers between devices, local(): lax.psum_scatter(grad_w_gate.astype(jnp.bfloat16), 'batch', scatter_dimen...  119 us
    reduce_scatter x1, waiting for transfers between devices, local(): lax.psum_scatter(grad_w_down.astype(jnp.bfloat16), 'batch', scatter_dimen...  118 us
    reduce_scatter x1, waiting for transfers between devices, local(): lax.psum_scatter(grad_w_up.astype(jnp.bfloat16), 'batch', scatter_dimensi...  118 us
    all_gather x1, waiting for transfers between devices, local(): lax.all_gather(w_gate, 'batch', axis=0, tiled=True)  90.7 us
    all_gather x1, waiting for transfers between devices, local(): lax.all_gather(w_down, 'batch', axis=0, tiled=True)  87.4 us
    all_gather x1, waiting for transfers between devices, local(): lax.all_gather(w_up, 'batch', axis=0, tiled=True)  87.3 us
    psum x1, waiting for transfers between devices, local(): lax.psum(grad_input_part.astype(jnp.bfloat16), 'heads').astype(jnp.float32)  82.2 us
  transfers between devices with their start and end apart: 19, of which 17 were waited for; matrix products, arithmetic and copies ran while one was open for 12% of the time, Pallas kernels for 0%

commit v1 on v0

--- a/solution.py
+++ b/solution.py
@@ -1,9 +1,14 @@
+import functools
+
 import jax
 import jax.numpy as jnp
 from jax import lax
+from jax.experimental import pallas as pl
+from jax.experimental.pallas import tpu as pltpu
 from jax.sharding import PartitionSpec as P
 
 SLOT_LEN = 1024
+MESH = pl.DeviceIdType.MESH
 
 
 NORM_EPS = 1e-06
@@ -193,6 +198,356 @@
     )
 
 
+def grid_of(n):
+    inner = 2 if n <= 8 else 4
+    return (n // inner, inner)
+
+def gather_kernel(plan, rows_n, cols_n, *refs):
+    count = plan["count"]
+    ins, outs = refs[:count], refs[count:2*count]
+    send_up, send_down, send_side, recv, local_sem = refs[2*count:]
+    A, B = rows_n, cols_n
+    me = lax.axis_index("batch")
+    a, b = me // B, me % B
+    units = plan["units"]
+
+    def block(u, blk):
+        i, lo, width = units[u][:3]
+        ref = outs[i].at[blk]
+        return ref if lo is None else ref.at[:, pl.ds(lo, width)]
+
+    def own(u):
+        i, lo, width = units[u][:3]
+        return ins[i] if lo is None else ins[i].at[:, pl.ds(lo, width)]
+
+    def put(u, src, blk, sem, target):
+        pltpu.make_async_remote_copy(src, block(u, blk), sem, recv.at[u, blk], device_id={"batch": target}, device_id_type=pl.DeviceIdType.MESH).start()
+
+    def arrived(u, blk):
+        pltpu.make_async_copy(block(u, blk), block(u, blk), recv.at[u, blk]).wait()
+
+    def sent(u, sem):
+        pltpu.make_async_copy(own(u), own(u), sem).wait()
+
+    barrier = pltpu.get_barrier_semaphore()
+    def greet(target):
+        pl.semaphore_signal(barrier, inc=1, device_id={"batch": target}, device_id_type=pl.DeviceIdType.MESH)
+    up_ok, down_ok = a < A - 1, a > 0
+    pl.when(up_ok)(lambda: greet(me + B))
+    pl.when(down_ok)(lambda: greet(me - B))
+    for k in range(1, B):
+        greet(a * B + (b + k) % B)
+    pl.semaphore_wait(barrier, up_ok.astype(jnp.int32) + down_ok.astype(jnp.int32) + (B - 1))
+
+    nu = len(units)
+    def up(u, src, blk, slot):
+        @pl.when(up_ok)
+        def _():
+            put(u, src, blk, send_up.at[u, slot], me + B)
+    def down(u, src, blk, slot):
+        @pl.when(down_ok)
+        def _():
+            put(u, src, blk, send_down.at[u, slot], me - B)
+    def side(u, src, blk, step):
+        for k in range(1, B):
+            put(u, src, blk, send_side.at[u, step * (B - 1) + k - 1], a * B + (b + k) % B)
+
+    for u in range(nu):
+        up(u, own(u), me, b)
+        down(u, own(u), me, b)
+        side(u, own(u), me, 0)
+    for i in range(count):
+        pltpu.make_async_copy(ins[i], outs[i].at[me], local_sem.at[i]).start()
+
+    for u in range(nu):
+        if units[u][3]:
+            for k in range(1, B):
+                bb = (b + k) % B
+                blk = a * B + bb
+                arrived(u, blk)
+                up(u, block(u, blk), blk, bb)
+                down(u, block(u, blk), blk, bb)
+    for s in range(1, A):
+        for u in range(nu):
+            first = units[u][3]
+            @pl.when(a - s >= 0)
+            def _(u=u, first=first):
+                for k in range(B if first else 1):
+                    bb = (b + k) % B
+                    blk = (a - s) * B + bb
+                    arrived(u, blk)
+                    up(u, block(u, blk), blk, s * B + bb)
+                    if not first:
+                        side(u, block(u, blk), blk, 2 * s - 1)
+            @pl.when(a + s < A)
+            def _(u=u, first=first):
+                for k in range(B if first else 1):
+                    bb = (b + k) % B
+                    blk = (a + s) * B + bb
+                    arrived(u, blk)
+                    down(u, block(u, blk), blk, s * B + bb)
+                    if not first:
+                        side(u, block(u, blk), blk, 2 * s)
+    for u in range(nu):
+        if not units[u][3]:
+            for s in range(A):
+                for k in range(1, B):
+                    bb = (b + k) % B
+                    @pl.when(a - s >= 0)
+                    def _(u=u, s=s, bb=bb):
+                        arrived(u, (a - s) * B + bb)
+                    if s:
+                        @pl.when(a + s < A)
+                        def _(u=u, s=s, bb=bb):
+                            arrived(u, (a + s) * B + bb)
+    for u in range(nu):
+        first = units[u][3]
+        for s in range(A):
+            for k in range(B if first else 1):
+                bb = (b + k) % B
+                @pl.when((a - s >= 0) & up_ok)
+                def _(u=u, s=s, bb=bb):
+                    sent(u, send_up.at[u, s * B + bb])
+                @pl.when((a + s < A) & down_ok)
+                def _(u=u, s=s, bb=bb):
+                    sent(u, send_down.at[u, s * B + bb])
+            if s == 0 or not first:
+                for k in range(1, B):
+                    if s == 0:
+                        sent(u, send_side.at[u, k - 1])
+                    else:
+                        @pl.when(a - s >= 0)
+                        def _(u=u, s=s, k=k):
+                            sent(u, send_side.at[u, (2 * s - 1) * (B - 1) + k - 1])
+                        @pl.when(a + s < A)
+                        def _(u=u, s=s, k=k):
+                            sent(u, send_side.at[u, (2 * s) * (B - 1) + k - 1])
+    for i in range(count):
+        pltpu.make_async_copy(ins[i], outs[i].at[me], local_sem.at[i]).wait()
+
+
+def gather_all(shards, plan_units, cid):
+    n = lax.axis_size("batch")
+    A, B = grid_of(n)
+    nu = len(plan_units)
+    plan = {"count": len(shards), "units": plan_units}
+    outs = [jax.ShapeDtypeStruct((n,) + s.shape, s.dtype) for s in shards]
+    res = pl.pallas_call(
+        functools.partial(gather_kernel, plan, A, B),
+        out_shape=outs,
+        in_specs=[pl.BlockSpec(memory_space=pltpu.VMEM)] * len(shards),
+        out_specs=[pl.BlockSpec(memory_space=pl.ANY)] * len(shards),
+        scratch_shapes=[
+            pltpu.SemaphoreType.DMA((nu, A * B)),
+            pltpu.SemaphoreType.DMA((nu, A * B)),
+            pltpu.SemaphoreType.DMA((nu, (2 * A - 1) * (B - 1))),
+            pltpu.SemaphoreType.DMA((nu, n)),
+            pltpu.SemaphoreType.DMA((len(shards),)),
+        ],
+        compiler_params=pltpu.CompilerParams(collective_id=cid, has_side_effects=True),
+        cost_estimate=pl.CostEstimate(flops=0, bytes_accessed=sum(s.size for s in shards) * 60, transcendentals=0),
+    )(*shards)
+    return [r.reshape((n * r.shape[1],) + r.shape[2:]) if r.shape[1] > 1 else r.reshape(-1) for r in res]
+
+
+def scatter_kernel(units, count, A, B, *refs):
+    nu = len(units)
+    ins, outs = refs[:count], refs[count:2 * count]
+    rest = list(refs[2 * count:])
+    own, side_in, up_in, down_in = (rest[k * nu:(k + 1) * nu] for k in range(4))
+    load_sem, side_send, side_recv, up_send, up_recv, down_send, down_recv = rest[4 * nu:]
+    me = lax.axis_index("batch")
+    a, b = me // B, me % B
+    up_ok, down_ok = a < A - 1, a > 0
+
+    def piece(u, blk):
+        i, lo, width, _ = units[u]
+        return ins[i].at[blk, :, pl.ds(lo, width)]
+
+    barrier = pltpu.get_barrier_semaphore()
+    def greet(target):
+        pl.semaphore_signal(barrier, inc=1, device_id={"batch": target}, device_id_type=MESH)
+    pl.when(up_ok)(lambda: greet(me + B))
+    pl.when(down_ok)(lambda: greet(me - B))
+    for k in range(1, B):
+        greet(a * B + (b + k) % B)
+
+    def at_distance(d, fn):
+        if d == 0:
+            return
+        @pl.when(a + d < A)
+        def _():
+            fn(a + d, True)
+        @pl.when(a - d >= 0)
+        def _():
+            fn(a - d, False)
+
+    def load(u, slot, blk):
+        return pltpu.make_async_copy(piece(u, blk), own[u].at[slot], load_sem.at[u, slot])
+
+    for d in range(A - 1, -1, -1):
+        for u in range(nu):
+            first = units[u][3]
+            def start(dest, _=None, u=u, first=first):
+                if first:
+                    for bb in range(B):
+                        load(u, dest * B + bb, dest * B + bb).start()
+                else:
+                    load(u, dest, dest * B + b).start()
+            at_distance(d, start) if d else start(a)
+    pl.semaphore_wait(barrier, up_ok.astype(jnp.int32) + down_ok.astype(jnp.int32) + (B - 1))
+
+    for d in range(A - 1, -1, -1):
+        for u in range(nu):
+            if units[u][3]:
+                continue
+            def start(dest, _=None, u=u):
+                for k in range(1, B):
+                    bb = (b + k) % B
+                    pltpu.make_async_remote_copy(
+                        piece(u, dest * B + bb), side_in[u].at[k - 1, dest], side_send.at[u, k - 1, dest],
+                        side_recv.at[u, k - 1, dest], device_id={"batch": a * B + bb}, device_id_type=MESH).start()
+            at_distance(d, start) if d else start(a)
+
+    def await_bytes(ref, sem):
+        pltpu.make_async_copy(ref, ref, sem).wait()
+
+    R = own[0].shape[1]
+    step_rows = min(R, 32)
+
+    def add_into(target, terms):
+        def body(t, carry):
+            rows = pl.ds(pl.multiple_of(t * step_rows, step_rows), step_rows)
+            total = terms[0][rows, :].astype(jnp.float32)
+            for term in terms[1:]:
+                total = total + term[rows, :].astype(jnp.float32)
+            target[rows, :] = total.astype(target.dtype)
+            return carry
+        lax.fori_loop(0, R // step_rows, body, 0)
+
+    def local_terms(u, dest, bb):
+        if units[u][3]:
+            slot = dest * B + bb
+            load(u, slot, slot).wait()
+            return [own[u].at[slot]], slot
+        load(u, dest, dest * B + b).wait()
+        for k in range(1, B):
+            await_bytes(side_in[u].at[k - 1, dest], side_recv.at[u, k - 1, dest])
+        return [own[u].at[dest]] + [side_in[u].at[k - 1, dest] for k in range(1, B)], dest
+
+    order = [u for u in range(nu) if units[u][3]] + [u for u in range(nu) if not units[u][3]]
+    for d in range(A - 1, 0, -1):
+        for u in order:
+            def flow(dest, goes_up, u=u):
+                for k in range(B if units[u][3] else 1):
+                    terms, slot = local_terms(u, dest, (b + k) % B)
+                    buf = (up_in if goes_up else down_in)[u].at[slot]
+                    send, recv = (up_send, up_recv) if goes_up else (down_send, down_recv)
+                    fed = down_ok if goes_up else up_ok
+                    @pl.when(fed)
+                    def _():
+                        await_bytes(buf, recv.at[u, slot])
+                        add_into(buf, [buf] + terms)
+                    @pl.when(jnp.logical_not(fed))
+                    def _():
+                        add_into(buf, terms)
+                    pltpu.make_async_remote_copy(
+                        buf, buf, send.at[u, slot], recv.at[u, slot],
+                        device_id={"batch": me + B if goes_up else me - B}, device_id_type=MESH).start()
+            at_distance(d, flow)
+
+    def out_piece(u):
+        i, lo, width, _ = units[u]
+        return outs[i].at[:, pl.ds(lo, width)]
+
+    def arrive_home(u, bb, target):
+        terms, slot = local_terms(u, a, bb)
+        @pl.when(down_ok)
+        def _():
+            await_bytes(up_in[u].at[slot], up_recv.at[u, slot])
+        @pl.when(up_ok)
+        def _():
+            await_bytes(down_in[u].at[slot], down_recv.at[u, slot])
+        @pl.when(down_ok & up_ok)
+        def _():
+            add_into(target, terms + [up_in[u].at[slot], down_in[u].at[slot]])
+        @pl.when(down_ok & jnp.logical_not(up_ok))
+        def _():
+            add_into(target, terms + [up_in[u].at[slot]])
+        @pl.when(up_ok & jnp.logical_not(down_ok))
+        def _():
+            add_into(target, terms + [down_in[u].at[slot]])
+
+    for u in order:
+        if units[u][3]:
+            for k in range(1, B):
+                bb = (b + k) % B
+                slot = a * B + bb
+                arrive_home(u, bb, own[u].at[slot])
+                pltpu.make_async_remote_copy(
+                    own[u].at[slot], side_in[u].at[k - 1, 0], side_send.at[u, k - 1, 0], side_recv.at[u, k - 1, 0],
+                    device_id={"batch": slot}, device_id_type=MESH).start()
+            arrive_home(u, b, own[u].at[a * B + b])
+        else:
+            arrive_home(u, b, out_piece(u))
+    for u in order:
+        if units[u][3]:
+            for k in range(1, B):
+                await_bytes(side_in[u].at[k - 1, 0], side_recv.at[u, k - 1, 0])
+            add_into(out_piece(u), [own[u].at[a * B + b]] + [side_in[u].at[k - 1, 0] for k in range(1, B)])
+
+    for u in range(nu):
+        first = units[u][3]
+        for k in range(1, B):
+            if first:
+                await_bytes(side_in[u].at[k - 1, 0], side_send.at[u, k - 1, 0])
+            else:
+                for dest in range(A):
+                    await_bytes(side_in[u].at[k - 1, dest], side_send.at[u, k - 1, dest])
+        for d in range(A - 1, 0, -1):
+            def done(dest, goes_up, u=u, first=first):
+                send = up_send if goes_up else down_send
+                for k in range(B if first else 1):
+                    slot = dest * B + k if first else dest
+                    await_bytes(up_in[u].at[slot], send.at[u, slot])
+            at_distance(d, done)
+
+
+def scatter_all(grads, units, cid, out_dtype=jnp.bfloat16):
+    n = lax.axis_size("batch")
+    A, B = grid_of(n)
+    nu = len(units)
+    R = grads[0].shape[0] // n
+    views = [g.reshape(n, R, g.shape[1]) for g in grads]
+    def slots(u):
+        return n if units[u][3] else A
+    scratch = []
+    scratch += [pltpu.VMEM((slots(u), R, units[u][2]), jnp.bfloat16) for u in range(nu)]
+    scratch += [pltpu.VMEM((B - 1, 1 if units[u][3] else A, R, units[u][2]), jnp.bfloat16) for u in range(nu)]
+    scratch += [pltpu.VMEM((slots(u), R, units[u][2]), jnp.bfloat16) for u in range(nu)]
+    scratch += [pltpu.VMEM((slots(u), R, units[u][2]), jnp.bfloat16) for u in range(nu)]
+    dma = pltpu.SemaphoreType.DMA
+    scratch += [dma((nu, n)), dma((nu, B - 1, A)), dma((nu, B - 1, A)), dma((nu, n)), dma((nu, n)), dma((nu, n)), dma((nu, n))]
+    res = pl.pallas_call(
+        functools.partial(scatter_kernel, units, len(grads), A, B),
+        out_shape=[jax.ShapeDtypeStruct((R, g.shape[1]), out_dtype) for g in grads],
+        in_specs=[pl.BlockSpec(memory_space=pl.ANY)] * len(grads),
+        out_specs=[pl.BlockSpec(memory_space=pltpu.VMEM)] * len(grads),
+        scratch_shapes=scratch,
+        compiler_params=pltpu.CompilerParams(collective_id=cid, has_side_effects=True, vmem_limit_bytes=64 * 1024 * 1024 - 65536),
+        cost_estimate=pl.CostEstimate(flops=0, bytes_accessed=sum(g.size for g in grads) * 8, transcendentals=0),
+    )(*views)
+    return list(res)
+
+
+def column_units(widths, side_first, chunk=512):
+    units = []
+    for index, width in enumerate(widths):
+        for low in range(0, width, chunk):
+            units.append((index, low, min(chunk, width - low), (index, low) in side_first))
+    return units
+
+
 def local(
     tokens,
     lengths,
@@ -212,22 +567,15 @@
 ):
     row_count, model_width = tokens.shape
     head_width = query_norm_gain.shape[0]
-    attn_full = (
-        lax.all_gather(w_query, "batch", axis=0, tiled=True),
-        lax.all_gather(w_gate_attn, "batch", axis=0, tiled=True),
-        lax.all_gather(w_key, "batch", axis=0, tiled=True),
-        lax.all_gather(w_value, "batch", axis=0, tiled=True),
-        lax.all_gather(w_out, "batch", axis=0, tiled=True),
-        lax.all_gather(attn_norm_gain, "batch", axis=0, tiled=True),
-    )
-    mlp_full = (
-        lax.all_gather(w_gate, "batch", axis=0, tiled=True),
-        lax.all_gather(w_up, "batch", axis=0, tiled=True),
-        lax.all_gather(w_down, "batch", axis=0, tiled=True),
-        lax.all_gather(mlp_norm_gain, "batch", axis=0, tiled=True),
-    )
-    query_full, gate_attn_full, key_full, value_full, out_full, gain_raw_one = attn_full
-    gate_full, up_full, down_full, gain_raw_two = mlp_full
+    shard_rows = w_query.shape[0]
+    attn_shards = [w_query, w_gate_attn, w_key, w_value, w_out]
+    attn_units = column_units([w.shape[1] for w in attn_shards], {(2, 0)})
+    gain_shards = [attn_norm_gain.reshape(1, -1), mlp_norm_gain.reshape(1, -1)]
+    query_full, gate_attn_full, key_full, value_full, out_full, gain_raw_one, gain_raw_two = gather_all(
+        attn_shards + gain_shards,
+        [(5, None, None, False), (6, None, None, False)] + attn_units,
+        0,
+    )
     gain_one = gain_raw_one.astype(jnp.float32)
     gain_two = gain_raw_two.astype(jnp.float32)
     query_gain = query_norm_gain.astype(jnp.float32)
@@ -257,8 +605,13 @@
     attended, log_totals = attend_forward(query_rot, key_rot, value_heads, lengths)
     gate_sig = jax.nn.sigmoid(gate_logit.reshape(row_count, head_count, head_width))
     gated = (attended * gate_sig).reshape(row_count, head_count * head_width).astype(jnp.bfloat16)
-    attn_out = lax.psum(contract_last(gated, out_full).astype(jnp.bfloat16), "heads").astype(
-        jnp.float32
+    attn_part = contract_last(gated, out_full).astype(jnp.bfloat16)
+    attn_part, w_gate, w_up, w_down = lax.optimization_barrier((attn_part, w_gate, w_up, w_down))
+    attn_out = lax.psum(attn_part, "heads").astype(jnp.float32)
+    mlp_shards = [w_gate, w_up, w_down]
+    mlp_widths = [w.shape[1] for w in mlp_shards]
+    gate_full, up_full, down_full = gather_all(
+        mlp_shards, column_units(mlp_widths, {(2, 0), (2, 512)}), 1
     )
     hidden_res = tokens_f + attn_out
     normed_two, scale_two = norm_rows(hidden_res, gain_two)
@@ -267,8 +620,26 @@
     up_pre = matmul(input_two, up_full)
     gate_act = jax.nn.sigmoid(gate_pre)
     activated = (gate_pre * gate_act * up_pre).astype(jnp.bfloat16)
-    mlp_out = lax.psum(contract_last(activated, down_full).astype(jnp.bfloat16), "heads").astype(
-        jnp.float32
+    mlp_part = contract_last(activated, down_full).astype(jnp.bfloat16)
+    grad_out = cotangent.astype(jnp.float32) * valid
+    grad_mlp = grad_out.astype(jnp.bfloat16)
+    grad_activated = matmul(grad_mlp, down_full)
+    grad_w_down = contract_rows(grad_mlp, activated).astype(jnp.bfloat16)
+    grad_gate_pre = (
+        grad_activated * up_pre * gate_act * (1.0 + gate_pre * (1.0 - gate_act))
+    ).astype(jnp.bfloat16)
+    grad_up_pre = (grad_activated * gate_pre * gate_act).astype(jnp.bfloat16)
+    grad_w_gate = contract_rows(input_two, grad_gate_pre).astype(jnp.bfloat16)
+    grad_w_up = contract_rows(input_two, grad_up_pre).astype(jnp.bfloat16)
+    grad_two_part = contract_last(grad_gate_pre, gate_full) + contract_last(grad_up_pre, up_full)
+    gain_two_part = jnp.sum(grad_two_part * (hidden_res * scale_two), axis=0)
+    grad_two_send, mlp_part, grad_w_gate, grad_w_up, grad_w_down = lax.optimization_barrier(
+        (grad_two_part.astype(jnp.bfloat16), mlp_part, grad_w_gate, grad_w_up, grad_w_down)
+    )
+    mlp_out = lax.psum(mlp_part, "heads").astype(jnp.float32)
+    grad_input_two = lax.psum(grad_two_send, "heads").astype(jnp.float32)
+    mlp_grads = scatter_all(
+        [grad_w_gate, grad_w_up, grad_w_down], column_units(mlp_widths, {(2, 512), (2, 1024)}), 2
     )
     summed = hidden_res + mlp_out
     output = (summed * valid).astype(jnp.bfloat16)
@@ -283,30 +654,14 @@
             masked_square(summed),
             masked_square(attn_out),
             masked_square(mlp_out),
+            jnp.sum(lengths).astype(jnp.float32),
         ]
     )
-    token_count = jnp.sum(lengths).astype(jnp.float32)
-    grad_out = cotangent.astype(jnp.float32) * valid
-    grad_mlp = grad_out.astype(jnp.bfloat16)
-    grad_activated = matmul(grad_mlp, down_full)
-    grad_w_down = contract_rows(grad_mlp, activated)
-    grad_gate_pre = (
-        grad_activated * up_pre * gate_act * (1.0 + gate_pre * (1.0 - gate_act))
-    ).astype(jnp.bfloat16)
-    grad_up_pre = (grad_activated * gate_pre * gate_act).astype(jnp.bfloat16)
-    grad_w_gate = contract_rows(input_two, grad_gate_pre)
-    grad_w_up = contract_rows(input_two, grad_up_pre)
-    grad_input_two = lax.psum(
-        (contract_last(grad_gate_pre, gate_full) + contract_last(grad_up_pre, up_full)).astype(
-            jnp.bfloat16
-        ),
-        "heads",
-    ).astype(jnp.float32)
-    grad_norm_two, grad_gain_two = norm_back(hidden_res, scale_two, gain_two, grad_input_two)
+    grad_norm_two, _ = norm_back(hidden_res, scale_two, gain_two, grad_input_two)
     grad_hidden = grad_out + grad_norm_two
     grad_attn = grad_hidden.astype(jnp.bfloat16)
     grad_gated = matmul(grad_attn, out_full).reshape(row_count, head_count, head_width)
-    grad_w_out = contract_rows(grad_attn, gated)
+    grad_w_out = contract_rows(grad_attn, gated).astype(jnp.bfloat16)
     grad_attended = (grad_gated * gate_sig).astype(jnp.bfloat16)
     grad_gate_logit = (
         (grad_gated * attended * gate_sig * (1.0 - gate_sig))
@@ -325,65 +680,48 @@
     )
     grad_queries = grad_query_pre.reshape(row_count, head_count * head_width).astype(jnp.bfloat16)
     grad_keys = grad_key_pre.reshape(row_count, kv_count * head_width).astype(jnp.bfloat16)
-    grad_w_query = contract_rows(input_one, grad_queries)
-    grad_w_gate_attn = contract_rows(input_one, grad_gate_logit)
-    grad_w_key = contract_rows(input_one, grad_keys)
-    grad_w_value = contract_rows(input_one, grad_values)
-    grad_input_part = (
+    attn_locals = [
+        contract_rows(input_one, grad_queries).astype(jnp.bfloat16),
+        contract_rows(input_one, grad_gate_logit).astype(jnp.bfloat16),
+        contract_rows(input_one, grad_keys).astype(jnp.bfloat16),
+        contract_rows(input_one, grad_values).astype(jnp.bfloat16),
+        grad_w_out,
+    ]
+    grad_one_part = (
         contract_last(grad_queries, query_full)
         + contract_last(grad_gate_logit, gate_attn_full)
         + contract_last(grad_keys, key_full)
         + contract_last(grad_values, value_full)
     )
-    grad_input_one, query_gain_heads, key_gain_heads = (
-        lax.psum(grad_input_part.astype(jnp.bfloat16), "heads").astype(jnp.float32),
-        lax.psum(grad_query_gain.astype(jnp.bfloat16), "heads").astype(jnp.float32),
-        lax.psum(grad_key_gain.astype(jnp.bfloat16), "heads").astype(jnp.float32),
-    )
-    grad_norm_one, grad_gain_one = norm_back(tokens_f, scale_one, gain_one, grad_input_one)
+    gain_one_part = jnp.sum(grad_one_part * (tokens_f * scale_one), axis=0)
+    grad_one_send, *attn_locals = lax.optimization_barrier(
+        (grad_one_part.astype(jnp.bfloat16), *attn_locals)
+    )
+    grad_input_one = lax.psum(grad_one_send, "heads").astype(jnp.float32)
+    attn_grads = scatter_all(attn_locals, attn_units, 3)
+    once = (lax.axis_index("heads") == 0).astype(jnp.float32)
+    sums = lax.psum(
+        jnp.concatenate(
+            [gain_one_part, gain_two_part, grad_query_gain, grad_key_gain, squares * once]
+        ),
+        ("heads", "batch"),
+    )
+    mine = lax.axis_index("batch") * shard_rows
+    gain_one_grad = lax.dynamic_slice(sums, (mine,), (shard_rows,))
+    gain_two_grad = lax.dynamic_slice(sums, (model_width + mine,), (shard_rows,))
+    low = 2 * model_width
+    query_gain_all = sums[low : low + head_width]
+    key_gain_all = sums[low + head_width : low + 2 * head_width]
+    squares_all = sums[low + 2 * head_width :]
+    block_rms = jnp.sqrt(squares_all[:5] / (squares_all[5] * model_width))
+    grad_norm_one, _ = norm_back(tokens_f, scale_one, gain_one, grad_input_one)
     grad_tokens = (grad_hidden + grad_norm_one).astype(jnp.bfloat16)
-    everything = (
-        lax.psum_scatter(
-            grad_w_query.astype(jnp.bfloat16), "batch", scatter_dimension=0, tiled=True
-        ).astype(jnp.float32),
-        lax.psum_scatter(
-            grad_w_gate_attn.astype(jnp.bfloat16), "batch", scatter_dimension=0, tiled=True
-        ).astype(jnp.float32),
-        lax.psum_scatter(
-            grad_w_key.astype(jnp.bfloat16), "batch", scatter_dimension=0, tiled=True
-        ).astype(jnp.float32),
-        lax.psum_scatter(
-            grad_w_value.astype(jnp.bfloat16), "batch", scatter_dimension=0, tiled=True
-        ).astype(jnp.float32),
-        lax.psum_scatter(
-            grad_w_out.astype(jnp.bfloat16), "batch", scatter_dimension=0, tiled=True
-        ).astype(jnp.float32),
-        lax.psum_scatter(
-            grad_gain_one.astype(jnp.bfloat16), "batch", scatter_dimension=0, tiled=True
-        ).astype(jnp.float32),
-        lax.psum_scatter(
-            grad_w_gate.astype(jnp.bfloat16), "batch", scatter_dimension=0, tiled=True
-        ).astype(jnp.float32),
-        lax.psum_scatter(
-            grad_w_up.astype(jnp.bfloat16), "batch", scatter_dimension=0, tiled=True
-        ).astype(jnp.float32),
-        lax.psum_scatter(
-            grad_w_down.astype(jnp.bfloat16), "batch", scatter_dimension=0, tiled=True
-        ).astype(jnp.float32),
-        lax.psum_scatter(
-            grad_gain_two.astype(jnp.bfloat16), "batch", scatter_dimension=0, tiled=True
-        ).astype(jnp.float32),
-    )
-    attn_grads = everything[:6]
-    mlp_grads = everything[6:]
-    squares_all, count_all, query_gain_all, key_gain_all = lax.psum(
-        (squares, token_count, query_gain_heads, key_gain_heads), "batch"
-    )
-    block_rms = jnp.sqrt(squares_all / (count_all * model_width))
+    attn_grads = [g.astype(jnp.float32) for g in attn_grads]
+    mlp_grads = [g.astype(jnp.float32) for g in mlp_grads]
     return (
         output,
         grad_tokens,
-        attn_grads[5],
+        gain_one_grad,
         query_gain_all,
         key_gain_all,
         attn_grads[0],
@@ -391,7 +729,7 @@
         attn_grads[2],
         attn_grads[3],
         attn_grads[4],
-        mlp_grads[3],
+        gain_two_grad,
         mlp_grads[0],
         mlp_grads[1],
         mlp_grads[2],

time: 1690 us -> 1080 us (0.64)
  waiting for transfers between devices: 1260 us -> 150 us
  Pallas kernels: 0 us -> 569 us
  blocking collectives: 91.2 us -> 40.4 us
  matrix products: 209 us -> 182 us
    pallas_call x0 -> x4, Pallas kernels: none -> 569 us  [the longest x2 288 us: gather_all(): pl.pallas_call(functools.partial(gather_kernel, plan, A, B), out_shape=ou...]
    reduce_scatter x8 -> x0, waiting for transfers between devices: 528 us -> none  [the longest x1 119 us: local(): lax.psum_scatter(grad_w_gate.astype(jnp.bfloat16), 'batch', scatter_dimen...]
    all_gather x8 -> x0, waiting for transfers between devices: 431 us -> none  [the longest x1 90.7 us: local(): lax.all_gather(w_gate, 'batch', axis=0, tiled=True)]
    psum x3, waiting for transfers between devices: 297 us -> 150 us  [the longest x1 150 us: local(): mlp_out = lax.psum(mlp_part, 'heads').astype(jnp.float32)]
    all_gather x2 -> x0, blocking collectives: 40.6 us -> none  [the longest x1 22.4 us: local(): lax.all_gather(attn_norm_gain, 'batch', axis=0, tiled=True)]
    unnamed x1 -> x0, blocking collectives: 22.1 us -> none
    psum x2 -> x1, blocking collectives: 28.5 us -> 40.4 us  [local(): lax.psum(jnp.concatenate([gain_one_part, gain_two_part, grad_query_gain,...]
  transfers between devices with their start and end apart: 19 -> 3, of which waited for: 17 -> 1; matrix products, arithmetic and copies ran while one was open for 12% -> 3% of each run, Pallas kernels for 0% -> 44%
where the time goes in v1:
time: 1080 us
  Pallas kernels  569 us (53%)
  matrix products  182 us (17%)
  waiting for transfers between devices  150 us (14%)
  other arithmetic  86 us (8%)
  blocking collectives  40.4 us (4%)
  local copies, waits for them, and re-layouts  30.9 us (3%)
  between operations  16.5 us (2%)
    pallas_call x2, Pallas kernels, gather_all(): pl.pallas_call(functools.partial(gather_kernel, plan, A, B), out_shape=ou...  288 us
    pallas_call x2, Pallas kernels, scatter_all(): pl.pallas_call(functools.partial(scatter_kernel, units, len(grads), A, B)...  281 us
    psum x1, waiting for transfers between devices, local(): mlp_out = lax.psum(mlp_part, 'heads').astype(jnp.float32)  150 us
    dot_general x8, matrix products, contract_last(): lax.dot_general(left_side, right_side, (((1,), (1,)), ((), ())), preferre...  58.9 us
    dot_general x8, matrix products, matmul(): return jnp.dot(left_side, right_side, preferred_element_type=jnp.float32)  52.7 us
    dot_general x8, matrix products, contract_rows(): lax.dot_general(left_side, right_side, (((0,), (0,)), ((), ())), preferre...  46.6 us
    psum x1, blocking collectives, local(): lax.psum(jnp.concatenate([gain_one_part, gain_two_part, grad_query_gain,...  40.4 us
  transfers between devices with their start and end apart: 3, of which 1 were waited for; matrix products, arithmetic and copies ran while one was open for 3% of the time, Pallas kernels for 44%

profile of v1, /device:TPU:0, one launch (start us, length us, event | category | flops | bytes accessed | tf_op | source)
XLA Modules:
  0.0 1075.0 jit_solution(2055923341371661430)
XLA Ops:
  11.7 3.1 fusion.15
  14.9 1.9 fusion.85
  16.8 92.1 %shard_map.262 = (bf16[8,256,512]{2,1,0:T(8,128)(2,1)}, bf16[8,256,512]{2,1,0:T(8,128)(2,1)}, bf16[8,256,256]{2,1,0:T(8,128)(2,1)}, bf16[8,256,256]{2,1,0:T(8,12...) custom-call(bf16[256,512]{1,0:T(8,128)(2,1)} %refs_0_.1, ...), custom_call_target="tpu_custom_call" | custom-call | bytes 31488000 | tf_op jit(solution)/shard_map/pallas_call | solution.py:335
  109.6 2.7 copy.30
  112.3 4.2 convolution_convert_fusion.10
  119.1 3.9 copy.38
  123.0 3.9 copy.31
  126.9 5.3 multiply_reduce_fusion.5
  134.9 1.8 fusion.106
  137.8 2.0 fusion.61
  140.0 1.8 fusion.107
  143.0 1.8 fusion.62
  145.6 2.1 copy-done.3
  148.3 4.0 fusion.48
  152.3 4.4 convolution_convert_fusion.4
  156.8 196.0 %shard_map.263 = (bf16[8,256,1536]{2,1,0:T(8,128)(2,1)}, bf16[8,256,1536]{2,1,0:T(8,128)(2,1)}, bf16[8,256,1536]{2,1,0:T(8,128)(2,1)}) custom-call(bf16[256,1536]{1,0:T(8,128)(2,1)} %refs_0_.2, bf16[256,1536]{1,0:T(8,128)(2,1)} %refs_1_.2, bf16[256,1536]{1,0:T(8,128)(2,1)} %refs_2_.2), custom_call_target="tpu_custom_call" | custom-call | bytes 70778880 | tf_op jit(solution)/shard_map/pallas_call | solution.py:335
  352.8 12.2 %fusion.57 = f32[1024,1536]{1,0:T(8,128)} fusion(bf16[2048,1536]{1,0:T(8,128)(2,1)} %bitcast.278, bf16[1024,2048]{1,0:T(8,128)(2,1)} %param.17, f32[1024]{0:T(1024)S(1)} %fusion.91), kind=kOutput, calls=%fused_computation.116 | convolution fusion | flops 6448742400 | bytes 16781312 | tf_op jit(solution)/shard_map/dot_general | solution.py:20
  365.1 5.0 multiply_reduce_fusion.2
  371.0 2.7 multiply_convert_fusion.1
  373.8 8.5 fusion.110
  382.3 13.3 %multiply_convert_fusion.2 = (bf16[1024,1536]{1,0:T(8,128)(2,1)}, bf16[1024,1536]{1,0:T(8,128)(2,1)S(1)}, bf16[1024,1536]{1,0:T(8,128)(2,1)}) fusion(f32[1024,1536]{1,0:T(8,128)} %fusion.110, f32[1024,1536]{1,0:T(8,128)} %fusion.57, bf16[1024,2048]{1,0:T(8,128)(2,1)S(1)} %multiply_convert_fusion.1, bf16[2048,1536]{1,0:T(8,128)(2,1)S(1)} %bitcast.276), kind=kOutput, calls=%fused_computation.64 | convolution fusion | flops 6467616768 | bytes 32505856 | tf_op jit(solution)/shard_map/dot_general | solution.py:20
  395.6 1.6 copy-done.67
  397.3 11.2 %fusion.111 = f32[1024,2048]{1,0:T(8,128)} fusion(bf16[1024,1536]{1,0:T(8,128)(2,1)S(1)} %get-tuple-element.153, bf16[2048,1536]{1,0:T(8,128)(2,1)} %bitcast.282), kind=kOutput, calls=%fused_computation.188 | convolution fusion | flops 6442450944 | bytes 17825792 | tf_op jit(solution)/shard_map/dot_general | solution.py:24
  408.4 10.7 convolution_convert_fusion.2
  419.2 8.2 convolution_convert_fusion.3
  427.5 8.9 convolution_convert_fusion
  436.4 8.8 convolution_convert_fusion.1
  445.2 11.8 %fusion.108 = (bf16[1024,2048]{1,0:T(8,128)(2,1)}, f32[1024,2048]{1,0:T(8,128)}) fusion(f32[1024,2048]{1,0:T(8,128)} %fusion.111, bf16[1024,1536]{1,0:T(8,128)(2,1)S(1)} %copy-done.68, bf16[2048,1536]{1,0:T(8,128)(2,1)S(1)} %bitcast.277), kind=kOutput, calls=%fused_computation.185 | convolution fusion | flops 6446645248 | bytes 30408704 | tf_op jit(solution)/shard_map/dot_general | solution.py:24
  457.0 3.3 copy.39
  460.5 149.6 %all-reduce.9.cloned.1.call-done = (bf16[1024,2048]{1,0:T(8,128)(2,1)}, bf16[1024,2048]{1,0:T(8,128)(2,1)}) async-done(((bf16[1024,2048]{1,0:T(8,128)(2,1)}, bf16[1024,2048]{1,0:T(8,128)(2,1)}), (bf16[1024,2048]{1,0:T(8,128)(2,1)}, bf16[1024,2048]{1,0:T(8,128)(2,1)})) %all-reduce.9.cloned.1.call-update) | async-done | bytes 8388624 | tf_op jit(solution)/shard_map/psum | solution.py:639
  610.1 16.1 %fusion.4 = (f32[]{:T(128)}, f32[]{:T(128)}, f32[1024]{0:T(1024)S(1)}, f32[2048]{0:T(1024)}, f32[]{:T(128)}, /*index=5*/f32[]{:T(128)}, f32[]{:T(128)}, bf16[1024,2048]{1,0:T(8,128)(2,1)}) fusion(bf16[1024,2048]{1,0:T(8,128)(2,1)} %get-tuple-element.147, bf16[1024,2048]{1,0:T(8,128)(2,1)} %all-reduce.5.cloned.1.call-done, bf16[1024,2048]{1,0:T(8,128)(2,1)} %param.15, ...), kind=kLoop, calls=%fused_computation.15 | loop fusion | flops 58717184 | bytes 29388820 | tf_op jit(solution)/shard_map/reduce_sum | solution.py:648
  626.3 3.9 multiply_add_fusion
  630.2 3.8 convolution_convert_fusion.5
  635.5 3.7 fusion.51
  639.3 5.0 fusion.17
  644.4 5.0 fusion.19
  649.3 2.5 convolution_bitcast_fusion
  651.8 1.7 fusion.69
  653.5 1.6 fusion.63
  655.1 1.9 fusion.20
  657.0 1.6 fusion.77
  658.7 2.8 convolution_convert_fusion.8
  661.5 4.3 convolution_convert_fusion.6
  665.9 5.6 fusion.113
  671.5 2.8 fusion.22
  678.5 2.8 convolution_convert_fusion.9
  682.9 1.6 multiply_reduce_fusion.3
  685.2 4.4 convolution_convert_fusion.7
  689.5 5.7 fusion.112
  696.7 10.7 fusion.109
  707.4 192.2 %shard_map.265 = (bf16[256,1536]{1,0:T(8,128)(2,1)}, bf16[256,1536]{1,0:T(8,128)(2,1)}, bf16[256,1536]{1,0:T(8,128)(2,1)}) custom-call(bf16[8,256,1536]{2,1,0:T(8,128)(2,1)} %bitcast.220, bf16[8,256,1536]{2,1,0:T(8,128)(2,1)} %bitcast.222, bf16[8,256,1536]{2,1,0:T(8,128)(2,1)} %bitcast.221), custom_call_target="tpu_custom_call" | custom-call | bytes 75497472 | tf_op jit(solution)/shard_map/pallas_call | solution.py:531
  899.7 2.5 convert_element_type.297
  902.1 2.5 convert_element_type.298
  904.6 2.5 convert_element_type.299
  907.0 89.0 %shard_map.264 = (bf16[256,512]{1,0:T(8,128)(2,1)}, bf16[256,512]{1,0:T(8,128)(2,1)}, bf16[256,256]{1,0:T(8,128)(2,1)}, bf16[256,256]{1,0:T(8,128)(2,1)}, bf16[256,512]{1,0:T(8,128)(2,1)}) custom-call(bf16[8,256,512]{2,1,0:T(8,128)(2,1)} %bitcast.251, bf16[8,256,512]{2,1,0:T(8,128)(2,1)} %bitcast.250, bf16[8,256,256]{2,1,0:T(8,128)(2,1)} %bitcast.260, ...), custom_call_target="tpu_custom_call" | custom-call | bytes 33554432 | tf_op jit(solution)/shard_map/pallas_call | solution.py:531
  996.1 1.8 convert_element_type.292
  997.9 1.6 convert_element_type.294
  999.5 1.6 convert_element_type.295
  1001.1 1.8 convert_element_type.293
  1002.9 1.8 convert_element_type.296
  1004.7 3.4 stack.27
  1008.1 8.1 fusion.14
  1016.3 40.4 %psum.39 = f32[4358]{0:T(1024)S(1)} all-reduce(f32[4358]{0:T(1024)S(1)} %constant_dynamic-update-slice_fusion), channel_id=1, replica_groups=mesh['heads'=4,'batch'=8] {'heads','batch'}, use_global_device_ids=true, to_apply=%region_27.28 | all-reduce | flops 4358 | bytes 34864 | tf_op jit(solution)/shard_map/psum | solution.py:703
  1059.6 8.7 fusion.13
  (219 shorter events, 26.3 us)
Async XLA Ops:
  7.2 357.9 %all-reduce.5.cloned.1.call-start = ((), (), s32[]{:S(2)}) async-start(), calls=%async_computation | async-start | bytes 8388608 | tf_op jit(solution)/shard_map/psum | solution.py:610
  8.6 124.3 %copy-start.58 = (f32[128]{0:T(128)}, f32[128]{0:T(128)S(1)}, u32[]{:S(2)}) copy-start(f32[128]{0:T(128)S(1)} %convert_element_type.243) | copy-start | bytes 1540
  9.2 125.1 %copy-start.60 = (f32[128]{0:T(128)}, f32[128]{0:T(128)S(1)}, u32[]{:S(2)}) copy-start(f32[128]{0:T(128)S(1)} %convert_element_type.239) | copy-start | bytes 1540
  14.8 130.8 %copy-start.51 = (f32[1024]{0:T(1024)}, f32[1024]{0:T(1024)S(1)}, u32[]{:S(2)}) copy-start(f32[1024]{0:T(1024)S(1)} %add_rsqrt_fusion.3) | copy-start | bytes 12292
  16.7 117.6 %copy-start.14 = (f32[1024,128]{0,1:T(8,128)}, f32[1024,128]{0,1:T(8,128)S(1)}, u32[]{:S(2)}) copy-start(f32[1024,128]{0,1:T(8,128)S(1)} %get-tuple-element.169) | copy-start | bytes 1572868
  16.7 117.6 %copy-start.16 = (f32[1024,128]{0,1:T(8,128)}, f32[1024,128]{0,1:T(8,128)S(1)}, u32[]{:S(2)}) copy-start(f32[1024,128]{0,1:T(8,128)S(1)} %get-tuple-element.170) | copy-start | bytes 1572868
  109.6 36.0 %copy-start.46 = (f32[8,1,256]{2,1,0:T(1,128)}, f32[8,1,256]{2,1,0:T(1,128)S(1)}, u32[]{:S(2)}) copy-start(f32[8,1,256]{2,1,0:T(1,128)S(1)} %convert_element_type.300) | copy-start | bytes 24580
  112.3 4.2 copy-start.2
  112.3 4.2 copy-start.41
  116.5 26.5 %copy-start.31 = (bf16[1024,256]{0,1:T(8,128)(2,1)}, bf16[1024,256]{0,1:T(8,128)(2,1)S(1)}, u32[]{:S(2)}) copy-start(bf16[1024,256]{0,1:T(8,128)(2,1)S(1)} %convolution_convert_fusion.10) | copy-start | bytes 1572868
  117.9 16.4 %copy-start.12 = (f32[1024,2,128]{0,2,1:T(8,128)}, f32[1024,2,128]{0,2,1:T(8,128)S(1)}, u32[]{:S(2)}) copy-start(f32[1024,2,128]{0,2,1:T(8,128)S(1)} %get-tuple-element.178) | copy-start | bytes 3145732
  118.0 16.4 %copy-start.44 = (f32[1024,2]{0,1:T(2,128)}, f32[1024,2]{0,1:T(2,128)S(1)}, u32[]{:S(2)}) copy-start(f32[1024,2]{0,1:T(2,128)S(1)} %add_rsqrt_fusion.1) | copy-start | bytes 24580
  133.8 2.9 copy-start.24
  133.8 6.2 copy-start.22
  134.8 5.2 copy-start.18
  136.6 3.3 copy-start.1
  136.6 3.3 copy-start.49
  141.8 3.6 copy-start
  143.0 4.7 copy-start.3
  143.0 5.3 copy-start.36
  145.6 6.7 copy-start.20
  148.3 4.0 copy-start.35
  152.3 4.4 copy-start.65
  152.3 4.5 copy-start.57
  156.7 453.4 %all-reduce.9.cloned.1.call-start = ((), (), s32[]{:S(2)}) async-start(), calls=%async_computation.2 | async-start | bytes 16777216 | tf_op jit(solution)/shard_map/psum | solution.py:639
  365.1 5.0 copy-start.4
  365.1 5.9 copy-start.7
  371.0 11.3 %slice-start.4 = ((s8[6291456]{0:T(1024)(128)(4,1)}), s8[4194304]{0:T(1024)(128)(4,1)S(1)}, s32[]{:S(2)}) async-start(s8[6291456]{0:T(1024)(128)(4,1)} %bitcast.274), calls=%async_computation.7 | async-start | bytes 8388608
  373.8 8.6 slice-start.5
  397.3 21.9 %slice-start.6 = ((s8[6291456]{0:T(1024)(128)(4,1)}), s8[4194304]{0:T(1024)(128)(4,1)S(1)}, s32[]{:S(2)}) async-start(s8[6291456]{0:T(1024)(128)(4,1)} %bitcast.279), calls=%async_computation.9 | async-start | bytes 8388608
  408.4 10.7 slice-start.7
  408.4 10.7 copy-start.69
  419.2 8.3 copy-start.27
  427.5 8.9 copy-start.68
  457.0 3.4 copy-start.50
  457.0 3.4 copy-start.56
  457.0 551.1 %all-reduce.7.cloned.1.call-start = ((), (), s32[]{:S(2)}) async-start(), calls=%async_computation.1 | async-start | bytes 8388608 | tf_op jit(solution)/shard_map/psum | solution.py:700
  610.1 16.1 %copy-start.5 = (bf16[1024,2048]{1,0:T(8,128)(2,1)S(1)}, bf16[1024,2048]{1,0:T(8,128)(2,1)}, u32[]{:S(2)}) copy-start(bf16[1024,2048]{1,0:T(8,128)(2,1)} %param.15) | copy-start | bytes 12582916
  610.1 16.1 %copy-start.8 = (bf16[1024,2048]{1,0:T(8,128)(2,1)S(1)}, bf16[1024,2048]{1,0:T(8,128)(2,1)}, u32[]{:S(2)}) copy-start(bf16[1024,2048]{1,0:T(8,128)(2,1)} %all-reduce.5.cloned.1.call-done) | copy-start | bytes 12582916
  610.1 16.1 %copy-start.11 = (bf16[1024,2048]{1,0:T(8,128)(2,1)S(1)}, bf16[1024,2048]{1,0:T(8,128)(2,1)}, u32[]{:S(2)}) copy-start(bf16[1024,2048]{1,0:T(8,128)(2,1)} %get-tuple-element.148) | copy-start | bytes 12582916
  610.1 16.1 %copy-start.28 = (bf16[1024,2048]{1,0:T(8,128)(2,1)S(1)}, bf16[1024,2048]{1,0:T(8,128)(2,1)}, u32[]{:S(2)}) copy-start(bf16[1024,2048]{1,0:T(8,128)(2,1)} %param.17) | copy-start | bytes 12582916
  626.3 3.9 copy-start.66
  630.2 5.3 copy-start.6
  630.2 5.2 copy-start.21
  630.2 5.3 copy-start.38
  634.0 5.2 slice-start.2
  635.5 3.8 slice-start.3
  635.5 3.8 copy-start.32
  639.3 14.2 %slice-start = ((s8[8388608]{0:T(1024)(128)(4,1)}), s8[4194304]{0:T(1024)(128)(4,1)S(1)}, s32[]{:S(2)}) async-start(s8[8388608]{0:T(1024)(128)(4,1)} %bitcast.214), calls=%async_computation.3 | async-start | bytes 8388608
  644.3 5.0 copy-start.25
  644.3 7.5 copy-start.19
  644.3 9.2 slice-start.1
  658.7 2.9 copy-start.40
  661.5 4.3 copy-start.34
  671.5 3.6 copy-start.23
  674.3 2.8 copy-start.13
  678.5 2.8 copy-start.29
  685.2 4.4 copy-start.33
  689.5 5.7 copy-start.26
  1008.1 8.1 copy-start.54
  1008.1 8.1 copy-start.63
  1008.1 8.1 copy-start.62
  1008.1 51.5 %copy-start.48 = (f32[8,1,256]{2,1,0:T(1,128)S(1)}, f32[8,1,256]{2,1,0:T(1,128)}, u32[]{:S(2)}) copy-start(f32[8,1,256]{2,1,0:T(1,128)} %copy-done.46) | copy-start | bytes 24580
  1008.1 51.5 %copy-start.53 = (f32[1024]{0:T(1024)S(1)}, f32[1024]{0:T(1024)}, u32[]{:S(2)}) copy-start(f32[1024]{0:T(1024)} %copy-done.51) | copy-start | bytes 12292
  (17 other events, 33.1 us)
Sparse Core Ops, SparseCore 0:
  156.9 84.6 all-reduce.4
  457.1 152.9 all-reduce.8
  707.5 85.6 all-reduce.6

commit v2 on v1

v2 whole, which is shorter than its diff:
```python
import functools

import jax
import jax.numpy as jnp
from jax import lax
from jax.experimental import pallas as pl
from jax.experimental.pallas import tpu as pltpu
from jax.sharding import PartitionSpec as P

SLOT_LEN = 1024
MESH = pl.DeviceIdType.MESH


NORM_EPS = 1e-06
ROPE_THETA = 1000000.0
MASKED = -1e30


def contract_rows(left_side, right_side):
    return lax.dot_general(
        left_side, right_side, (((0,), (0,)), ((), ())), preferred_element_type=jnp.float32
    )


def rotary_tables(row_count, head_width):
    half_width = head_width // 2
    positions = (lax.iota(jnp.int32, row_count) % SLOT_LEN).astype(jnp.float32)
    inverse = ROPE_THETA ** (
        -(lax.iota(jnp.int32, half_width).astype(jnp.float32) * 2.0 / head_width)
    )
    angles = positions[:, None] * inverse[None, :]
    angles = jnp.concatenate([angles, angles], axis=1)
    return (jnp.cos(angles), jnp.sin(angles))


VMEM_LIMIT = 64 * 1024 * 1024 - 65536


def grid_of(n):
    inner = 2 if n <= 8 else 4
    return (n // inner, inner)


class HeadSum:
    def __init__(self, refs):
        (self.src, self.out, self.core_in, self.mid, self.far_in,
         self.load_sem, self.core_send, self.core_recv, self.far_send, self.far_recv,
         self.back_send, self.back_recv, self.keep_sem) = refs
        head = lax.axis_index("heads")
        self.core = head % 2
        self.near = head + 1 - 2 * self.core
        self.far = (head + 2) % 4
        self.pieces, self.rows = self.mid.shape[0], self.mid.shape[1]

    def greet(self, barrier):
        for other in (self.near, self.far):
            pl.semaphore_signal(barrier, inc=1, device_id={"heads": other}, device_id_type=MESH)

    def part(self, ref, half, k):
        return ref.at[pl.ds(pl.multiple_of((half * self.pieces + k) * self.rows, self.rows), self.rows), :]

    def load(self, k):
        return pltpu.make_async_copy(self.part(self.src, self.core, k), self.mid.at[k], self.load_sem.at[k])

    def to_core(self, k):
        return pltpu.make_async_remote_copy(
            self.part(self.src, 1 - self.core, k), self.core_in.at[k], self.core_send.at[k], self.core_recv.at[k],
            device_id={"heads": self.near}, device_id_type=MESH)

    def to_far(self, k):
        return pltpu.make_async_remote_copy(
            self.mid.at[k], self.far_in.at[k], self.far_send.at[k], self.far_recv.at[k],
            device_id={"heads": self.far}, device_id_type=MESH)

    def keep(self, k):
        return pltpu.make_async_copy(self.far_in.at[k], self.part(self.out, self.core, k), self.keep_sem.at[k])

    def back(self, k):
        return pltpu.make_async_remote_copy(
            self.far_in.at[k], self.part(self.out, self.core, k), self.back_send.at[k], self.back_recv.at[k],
            device_id={"heads": self.near}, device_id_type=MESH)

    def start(self):
        for k in range(self.pieces):
            self.to_core(k).start()
            self.load(k).start()

    def add(self, target, other):
        tile = min(self.rows, 16)

        def body(t, carry):
            rows = pl.ds(pl.multiple_of(t * tile, tile), tile)
            total = target[rows, :].astype(jnp.float32) + other[rows, :].astype(jnp.float32)
            target[rows, :] = total.astype(target.dtype)
            return carry

        lax.fori_loop(0, self.rows // tile, body, 0)

    def cross(self):
        for k in range(self.pieces):
            self.load(k).wait()
            pltpu.make_async_copy(self.core_in.at[k], self.core_in.at[k], self.core_recv.at[k]).wait()
            self.add(self.mid.at[k], self.core_in.at[k])
            self.to_far(k).start()

    def settle(self):
        for k in range(self.pieces):
            pltpu.make_async_copy(self.far_in.at[k], self.far_in.at[k], self.far_recv.at[k]).wait()
            self.add(self.far_in.at[k], self.mid.at[k])
            self.keep(k).start()
            self.back(k).start()

    def finish(self):
        for k in range(self.pieces):
            other = self.part(self.out, 1 - self.core, k)
            pltpu.make_async_copy(other, other, self.back_recv.at[k]).wait()
            self.keep(k).wait()
            self.to_core(k).wait_send()
            self.to_far(k).wait_send()
            self.back(k).wait_send()


SUM_REFS = 13
SUM_PIECES = 4


def head_sum_scratch(array):
    rows, width = array.shape
    shape = (SUM_PIECES, rows // 2 // SUM_PIECES, width)
    return [pltpu.VMEM(shape, array.dtype)] * 3 + [pltpu.SemaphoreType.DMA((SUM_PIECES,))] * 8


def gather_kernel(plan, rows_n, cols_n, *refs):
    count, sums = plan["count"], plan["sums"]
    ins, sum_ins, refs = refs[:count], refs[count : count + sums], refs[count + sums :]
    outs, sum_outs, refs = refs[:count], refs[count : count + sums], refs[count + sums :]
    send_up, send_down, send_side, recv, local_sem = refs[:5]
    each = SUM_REFS - 2
    totals = [
        HeadSum((sum_ins[i], sum_outs[i]) + tuple(refs[5 + i * each : 5 + (i + 1) * each])) for i in range(sums)
    ]
    A, B = rows_n, cols_n
    me = lax.axis_index("batch")
    a, b = me // B, me % B
    units = plan["units"]

    def block(u, blk):
        i, lo, width = units[u][:3]
        ref = outs[i].at[blk]
        return ref if lo is None else ref.at[:, pl.ds(lo, width)]

    def own(u):
        i, lo, width = units[u][:3]
        return ins[i] if lo is None else ins[i].at[:, pl.ds(lo, width)]

    def put(u, src, blk, sem, target):
        pltpu.make_async_remote_copy(src, block(u, blk), sem, recv.at[u, blk], device_id={"batch": target}, device_id_type=pl.DeviceIdType.MESH).start()

    def arrived(u, blk):
        pltpu.make_async_copy(block(u, blk), block(u, blk), recv.at[u, blk]).wait()

    def sent(u, sem):
        pltpu.make_async_copy(own(u), own(u), sem).wait()

    barrier = pltpu.get_barrier_semaphore()

    def greet(target):
        pl.semaphore_signal(barrier, inc=1, device_id={"batch": target}, device_id_type=pl.DeviceIdType.MESH)

    up_ok, down_ok = a < A - 1, a > 0
    pl.when(up_ok)(lambda: greet(me + B))
    pl.when(down_ok)(lambda: greet(me - B))
    for k in range(1, B):
        greet(a * B + (b + k) % B)
    if totals:
        totals[0].greet(barrier)
    pl.semaphore_wait(barrier, up_ok.astype(jnp.int32) + down_ok.astype(jnp.int32) + (B - 1) + (2 if totals else 0))
    for total in totals:
        total.start()

    nu = len(units)

    def up(u, src, blk, slot):
        @pl.when(up_ok)
        def _():
            put(u, src, blk, send_up.at[u, slot], me + B)

    def down(u, src, blk, slot):
        @pl.when(down_ok)
        def _():
            put(u, src, blk, send_down.at[u, slot], me - B)

    def side(u, src, blk, step):
        for k in range(1, B):
            put(u, src, blk, send_side.at[u, step * (B - 1) + k - 1], a * B + (b + k) % B)

    for u in range(nu):
        up(u, own(u), me, b)
        down(u, own(u), me, b)
        side(u, own(u), me, 0)
    for i in range(count):
        pltpu.make_async_copy(ins[i], outs[i].at[me], local_sem.at[i]).start()

    for total in totals:
        total.cross()
    for u in range(nu):
        if units[u][3]:
            for k in range(1, B):
                bb = (b + k) % B
                blk = a * B + bb
                arrived(u, blk)
                up(u, block(u, blk), blk, bb)
                down(u, block(u, blk), blk, bb)
    for s in range(1, A):
        if s == A - 1:
            for total in totals:
                total.settle()
        for u in range(nu):
            first = units[u][3]

            @pl.when(a - s >= 0)
            def _(u=u, first=first):
                for k in range(B if first else 1):
                    bb = (b + k) % B
                    blk = (a - s) * B + bb
                    arrived(u, blk)
                    up(u, block(u, blk), blk, s * B + bb)
                    if not first:
                        side(u, block(u, blk), blk, 2 * s - 1)

            @pl.when(a + s < A)
            def _(u=u, first=first):
                for k in range(B if first else 1):
                    bb = (b + k) % B
                    blk = (a + s) * B + bb
                    arrived(u, blk)
                    down(u, block(u, blk), blk, s * B + bb)
                    if not first:
                        side(u, block(u, blk), blk, 2 * s)
    for total in totals:
        total.finish()
    for u in range(nu):
        if not units[u][3]:
            for s in range(A):
                for k in range(1, B):
                    bb = (b + k) % B

                    @pl.when(a - s >= 0)
                    def _(u=u, s=s, bb=bb):
                        arrived(u, (a - s) * B + bb)

                    if s:
                        @pl.when(a + s < A)
                        def _(u=u, s=s, bb=bb):
                            arrived(u, (a + s) * B + bb)
    for u in range(nu):
        first = units[u][3]
        for s in range(A):
            for k in range(B if first else 1):
                bb = (b + k) % B

                @pl.when((a - s >= 0) & up_ok)
                def _(u=u, s=s, bb=bb):
                    sent(u, send_up.at[u, s * B + bb])

                @pl.when((a + s < A) & down_ok)
                def _(u=u, s=s, bb=bb):
                    sent(u, send_down.at[u, s * B + bb])
            if s == 0 or not first:
                for k in range(1, B):
                    if s == 0:
                        sent(u, send_side.at[u, k - 1])
                    else:
                        @pl.when(a - s >= 0)
                        def _(u=u, s=s, k=k):
                            sent(u, send_side.at[u, (2 * s - 1) * (B - 1) + k - 1])

                        @pl.when(a + s < A)
                        def _(u=u, s=s, k=k):
                            sent(u, send_side.at[u, (2 * s) * (B - 1) + k - 1])
    for i in range(count):
        pltpu.make_async_copy(ins[i], outs[i].at[me], local_sem.at[i]).wait()


def gather_all(shards, plan_units, cid, sums=()):
    n = lax.axis_size("batch")
    A, B = grid_of(n)
    nu = len(plan_units)
    plan = {"count": len(shards), "units": plan_units, "sums": len(sums)}
    outs = [jax.ShapeDtypeStruct((n,) + s.shape, s.dtype) for s in shards]
    outs += [jax.ShapeDtypeStruct(s.shape, s.dtype) for s in sums]
    sum_scratch = [ref for s in sums for ref in head_sum_scratch(s)]
    res = pl.pallas_call(
        functools.partial(gather_kernel, plan, A, B),
        out_shape=outs,
        in_specs=[pl.BlockSpec(memory_space=pltpu.VMEM)] * len(shards) + [pl.BlockSpec(memory_space=pl.ANY)] * len(sums),
        out_specs=[pl.BlockSpec(memory_space=pl.ANY)] * len(outs),
        scratch_shapes=[
            pltpu.SemaphoreType.DMA((nu, A * B)),
            pltpu.SemaphoreType.DMA((nu, A * B)),
            pltpu.SemaphoreType.DMA((nu, (2 * A - 1) * (B - 1))),
            pltpu.SemaphoreType.DMA((nu, n)),
            pltpu.SemaphoreType.DMA((len(shards),)),
        ] + sum_scratch,
        compiler_params=pltpu.CompilerParams(collective_id=cid, has_side_effects=True, vmem_limit_bytes=VMEM_LIMIT),
        cost_estimate=pl.CostEstimate(flops=0, bytes_accessed=sum(s.size for s in shards) * 60, transcendentals=0),
    )(*shards, *sums)
    full = [r.reshape((n * r.shape[1],) + r.shape[2:]) if r.shape[1] > 1 else r.reshape(-1) for r in res[: len(shards)]]
    return full + list(res[len(shards) :])


TILE = 256


def nt(left_side, right_side):
    return lax.dot_general(left_side, right_side, (((1,), (1,)), ((), ())), preferred_element_type=jnp.float32)


def nn(left_side, right_side):
    return lax.dot_general(left_side, right_side, (((1,), (0,)), ((), ())), preferred_element_type=jnp.float32)


def rms_scale(value):
    return lax.rsqrt(jnp.mean(value * value, axis=-1, keepdims=True) + NORM_EPS)


def gain_row(gains, which):
    return jnp.concatenate(
        [gains[blk, which : which + 1, :].astype(jnp.float32) for blk in range(gains.shape[0])], axis=1
    )


def allowed_keys(key_count, lane_count, first_query, seq_length):
    keys = lax.broadcasted_iota(jnp.int32, (key_count, lane_count), 0)
    queries = first_query + lax.broadcasted_iota(jnp.int32, (key_count, lane_count), 1) % TILE
    return (keys <= queries) & (keys < seq_length)


def attn_forward_kernel(
    lengths, x, gain, query_gain, key_gain, cos, sin, wq, wg, wk, wv, wo,
    a1_out, qr_out, kr_out, v_out, q_out, k_out, gate_out, o_out, lse_out, part_out,
    kr_all, vt_all,
):
    step = pl.program_id(0)
    hd = query_gain.shape[1]
    heads, kv = wq.shape[1] // hd, wk.shape[1] // hd
    group = heads // kv
    xf = x[...].astype(jnp.float32)
    a1 = (xf * rms_scale(xf) * gain_row(gain, 0)).astype(jnp.bfloat16)
    a1_out[...] = a1
    k = nn(a1, wk[...])
    k_out[...] = k
    v = nn(a1, wv[...])
    v_out[...] = v.astype(jnp.bfloat16)
    q = nn(a1, wq[...])
    q_out[...] = q
    gate = nn(a1, wg[...])
    gate_out[...] = gate

    def rope(u, g):
        n = u * rms_scale(u) * g
        return (n * cos[...] + pltpu.roll(n, hd // 2, 1) * sin[...]).astype(jnp.bfloat16)

    rows = pl.ds(pl.multiple_of(step * TILE, TILE), TILE)
    for j in range(kv):
        cols = slice(j * hd, (j + 1) * hd)
        kr = rope(k[:, cols], key_gain[...])
        kr_out[:, cols] = kr
        kr_all[rows, cols] = kr
    vt_all[:, rows] = v.T.astype(jnp.bfloat16)
    qr = [rope(q[:, h * hd : (h + 1) * hd], query_gain[...]) for h in range(heads)]
    for h in range(heads):
        qr_out[:, h * hd : (h + 1) * hd] = qr[h]
    seq_length = lengths[0]
    scale = hd ** -0.5
    for i in range(SLOT_LEN // TILE):
        @pl.when(step == i)
        def _(i=i):
            count = (i + 1) * TILE
            mask = allowed_keys(count, group * TILE, i * TILE, seq_length)
            for j in range(kv):
                cols = slice(j * hd, (j + 1) * hd)
                stack = jnp.concatenate(qr[j * group : (j + 1) * group], axis=0)
                scores = jnp.where(mask, nt(kr_all[:count, cols], stack) * scale, MASKED)
                top = jnp.max(scores, axis=0, keepdims=True)
                weights = jnp.exp(scores - top)
                total = jnp.sum(weights, axis=0, keepdims=True)
                lse_out[0, j : j + 1, :] = top + jnp.log(total)
                probs = (weights * (1.0 / total)).astype(jnp.bfloat16)
                ot = nn(vt_all[cols, :count], probs)
                o = ot.T
                for g in range(group):
                    h = j * group + g
                    o_out[:, h * hd : (h + 1) * hd] = o[g * TILE : (g + 1) * TILE, :]
    og = (o_out[...] * jax.nn.sigmoid(gate)).astype(jnp.bfloat16)
    part_out[...] = nt(og, wo[...]).astype(jnp.bfloat16)


def whole(shape):
    return pl.BlockSpec(shape, lambda i: (0,) * len(shape), pipeline_mode=pl.Buffered(1))


def attn_forward(lengths, x, gain, query_gain, key_gain, cos, sin, wq, wg, wk, wv, wo):
    rows, width = x.shape
    steps = rows // TILE
    q_width, k_width = wq.shape[1], wk.shape[1]
    hd = query_gain.shape[1]
    tile = lambda w: pl.BlockSpec((TILE, w), lambda i: (i, 0))
    kv = k_width // hd
    lanes = q_width // k_width * TILE
    bf, f32 = jnp.bfloat16, jnp.float32
    shapes = [
        ((rows, width), bf), ((rows, q_width), bf), ((rows, k_width), bf), ((rows, k_width), bf),
        ((rows, q_width), f32), ((rows, k_width), f32), ((rows, q_width), f32), ((rows, q_width), f32),
        ((steps, kv, lanes), f32), ((rows, width), bf),
    ]
    out_specs = [tile(s[1]) for s, _ in shapes]
    out_specs[8] = pl.BlockSpec((1, kv, lanes), lambda i: (i, 0, 0))
    return pl.pallas_call(
        attn_forward_kernel,
        grid=(steps,),
        out_shape=[jax.ShapeDtypeStruct(*s) for s in shapes],
        in_specs=[pl.BlockSpec(memory_space=pltpu.SMEM), tile(width), whole(gain.shape), whole((1, hd)), whole((1, hd)),
                  tile(hd), tile(hd)] + [whole(w.shape) for w in (wq, wg, wk, wv, wo)],
        out_specs=out_specs,
        scratch_shapes=[pltpu.VMEM((rows, k_width), bf), pltpu.VMEM((k_width, rows), bf)],
        compiler_params=pltpu.CompilerParams(vmem_limit_bytes=60 * 1024 * 1024),
        cost_estimate=pl.CostEstimate(flops=2 * rows * width * (3 * q_width + 2 * k_width), bytes_accessed=40 << 20, transcendentals=4 << 20),
        name="attn_forward",
    )(lengths, x, gain, query_gain, key_gain, cos, sin, wq, wg, wk, wv, wo)


def mlp_forward_kernel(lengths, x, attn, cot, gain, wg, wu, a2_out, gm_out, hid_out, gu_out, up_out):
    t, c = pl.program_id(0), pl.program_id(1)
    rows = x.shape[0]

    @pl.when(c == 0)
    def _():
        h = x[...].astype(jnp.float32) + attn[...].astype(jnp.float32)
        a2_out[...] = (h * rms_scale(h) * gain_row(gain, 1)).astype(jnp.bfloat16)
        places = t * rows + lax.broadcasted_iota(jnp.int32, (rows, 1), 0)
        gm_out[...] = jnp.where(places < lengths[0], cot[...], 0.0).astype(jnp.bfloat16)

    a2 = a2_out[...]
    gu = nn(a2, wg[...])
    up = nn(a2, wu[...])
    gu_out[...] = gu.astype(jnp.bfloat16)
    up_out[...] = up.astype(jnp.bfloat16)
    hid_out[...] = (gu * jax.nn.sigmoid(gu) * up).astype(jnp.bfloat16)


def mlp_backward_kernel(
    x, attn, gm, hid, gu_in, up_in, wg, wu, wd_first, wd_last,
    ggu_out, gup_first, gup_last, part_out, ga2_out, gain_out, part_s, ga2_s,
):
    t, c = pl.program_id(0), pl.program_id(1)

    def half(wd, gup_out):
        gu, up = gu_in[...].astype(jnp.float32), up_in[...].astype(jnp.float32)
        sg = jax.nn.sigmoid(gu)
        g_hid = nn(gm[...], wd[...])
        g_gu = (g_hid * up * sg * (1.0 + gu * (1.0 - sg))).astype(jnp.bfloat16)
        g_up = (g_hid * (gu * sg)).astype(jnp.bfloat16)
        ggu_out[...] = g_gu
        gup_out[...] = g_up
        return nt(hid[...], wd[...]), nt(g_gu, wg[...]) + nt(g_up, wu[...])

    @pl.when(c == 0)
    def _():
        part_s[...], ga2_s[...] = half(wd_first, gup_first)

    @pl.when(c == 1)
    def _():
        part, ga2 = half(wd_last, gup_last)
        part_out[...] = (part_s[...] + part).astype(jnp.bfloat16)
        ga2 = ga2_s[...] + ga2
        ga2_out[...] = ga2.astype(jnp.bfloat16)
        h = x[...].astype(jnp.float32) + attn[...].astype(jnp.float32)
        mine = jnp.sum(ga2 * (h * rms_scale(h)), axis=0, keepdims=True)

        @pl.when(t == 0)
        def _():
            gain_out[...] = mine

        @pl.when(t > 0)
        def _():
            gain_out[...] += mine


def mlp_specs(width, row_tile, col_tile):
    wide = pl.BlockSpec((row_tile, width), lambda t, c: (t, 0))
    wcol = pl.BlockSpec((width, col_tile), lambda t, c: (0, c))
    narrow = pl.BlockSpec((row_tile, col_tile), lambda t, c: (t, c))
    one = pl.BlockSpec((1, width), lambda t, c: (0, 0))
    return wide, wcol, narrow, one


def mlp_forward(lengths, x, attn, cot, gain, wg, wu, row_tile=512, col_tile=512):
    rows, width = x.shape
    ff = wg.shape[1]
    wide, wcol, narrow, _ = mlp_specs(width, row_tile, col_tile)
    return pl.pallas_call(
        mlp_forward_kernel,
        grid=(rows // row_tile, ff // col_tile),
        out_shape=[jax.ShapeDtypeStruct((rows, width), jnp.bfloat16)] * 2
        + [jax.ShapeDtypeStruct((rows, ff), jnp.bfloat16)] * 3,
        in_specs=[pl.BlockSpec(memory_space=pltpu.SMEM), wide, wide, wide,
                  pl.BlockSpec(gain.shape, lambda t, c: (0, 0, 0)), wcol, wcol],
        out_specs=[wide, wide, narrow, narrow, narrow],
        compiler_params=pltpu.CompilerParams(vmem_limit_bytes=60 * 1024 * 1024),
        cost_estimate=pl.CostEstimate(flops=4 * rows * width * ff, bytes_accessed=50 << 20, transcendentals=rows * ff),
        name="mlp_forward",
    )(lengths, x, attn, cot, gain, wg, wu)


def mlp_backward(x, attn, gm, hid, gu, up, wg, wu, wd_first, wd_last, row_tile=512):
    rows, width = x.shape
    ff = wg.shape[1]
    col_tile = ff // 2
    wide, wcol, narrow, one = mlp_specs(width, row_tile, col_tile)
    alone = pl.BlockSpec((row_tile, col_tile), lambda t, c: (t, 0))
    fixed = pl.BlockSpec((width, col_tile), lambda t, c: (0, 0), pipeline_mode=pl.Buffered(1))
    bf, f32 = jnp.bfloat16, jnp.float32
    return pl.pallas_call(
        mlp_backward_kernel,
        grid=(rows // row_tile, 2),
        out_shape=[jax.ShapeDtypeStruct((rows, ff), bf)] + [jax.ShapeDtypeStruct((rows, col_tile), bf)] * 2
        + [jax.ShapeDtypeStruct((rows, width), bf)] * 2 + [jax.ShapeDtypeStruct((1, width), f32)],
        in_specs=[wide, wide, wide, narrow, narrow, narrow, wcol, wcol, fixed, fixed],
        out_specs=[narrow, alone, alone, wide, wide, one],
        scratch_shapes=[pltpu.VMEM((row_tile, width), f32), pltpu.VMEM((row_tile, width), f32)],
        compiler_params=pltpu.CompilerParams(vmem_limit_bytes=VMEM_LIMIT),
        cost_estimate=pl.CostEstimate(flops=8 * rows * width * ff, bytes_accessed=60 << 20, transcendentals=rows * ff),
        name="mlp_backward",
    )(x, attn, gm, hid, gu, up, wg, wu, wd_first, wd_last)


def attn_backward_kernel(
    lengths, g2, x, attn, mlp, cot, gain_two, query_gain, key_gain, cos, sin,
    qr, kr, v, q, k, gate, o, lse, wq, wg, wk, wv, wo,
    y_out, ghb_out, og_out, gall_out, ga1_out, gain_out, small_out,
    krt, gk, gv, gq_s,
):
    step = pl.program_id(0)
    steps = SLOT_LEN // TILE
    tile = steps - 1 - step
    hd = query_gain.shape[1]
    heads, kv = wq.shape[1] // hd, wk.shape[1] // hd
    group = heads // kv
    seq_length = lengths[0]
    scale = hd ** -0.5

    @pl.when(step == 0)
    def _():
        krt[...] = kr[...].astype(jnp.float32).T.astype(jnp.bfloat16)
        gk[...] = jnp.zeros_like(gk)
        gv[...] = jnp.zeros_like(gv)
        gain_out[...] = jnp.zeros_like(gain_out)
        small_out[...] = jnp.zeros_like(small_out)

    places = tile * TILE + lax.broadcasted_iota(jnp.int32, (TILE, 1), 0)
    live = places < seq_length
    xf = x[...].astype(jnp.float32)
    attn_f = attn[...].astype(jnp.float32)
    mlp_f = mlp[...].astype(jnp.float32)
    h = xf + attn_f
    y = h + mlp_f
    y_out[...] = jnp.where(live, y, 0.0).astype(jnp.bfloat16)
    for r, field in enumerate((xf, h, y, attn_f, mlp_f)):
        by_lane = jnp.sum(jnp.where(live, field * field, 0.0), axis=0, keepdims=True)
        folded = by_lane[:, :hd]
        for low in range(hd, by_lane.shape[1], hd):
            folded = folded + by_lane[:, low : low + hd]
        small_out[2 + r : 3 + r, :] += folded
    rho = rms_scale(h)
    n = h * rho
    gs = g2[...].astype(jnp.float32) * gain_row(gain_two, 1)
    g_out = jnp.where(live, cot[...].astype(jnp.float32), 0.0)
    ghb = (g_out + rho * (gs - n * jnp.mean(gs * n, axis=-1, keepdims=True))).astype(jnp.bfloat16)
    ghb_out[...] = ghb
    g_og = nn(ghb, wo[...])
    sig = jax.nn.sigmoid(gate[...])
    of = o[...]
    og_out[...] = (of * sig).astype(jnp.bfloat16)
    g_o = (g_og * sig).astype(jnp.bfloat16)
    q_width, k_width = heads * hd, kv * hd
    gall_out[:, q_width : 2 * q_width] = (g_og * of * sig * (1.0 - sig)).astype(jnp.bfloat16)

    for i in range(steps):
        @pl.when(tile == i)
        def _(i=i):
            count = (i + 1) * TILE
            mask = allowed_keys(count, group * TILE, i * TILE, seq_length)
            for j in range(kv):
                cols = slice(j * hd, (j + 1) * hd)
                mine = [slice((j * group + g) * hd, (j * group + g + 1) * hd) for g in range(group)]
                stack = jnp.concatenate([qr[:, s] for s in mine], axis=0)
                g_stack = jnp.concatenate([g_o[:, s] for s in mine], axis=0)
                scores = nt(kr[:count, cols], stack) * scale
                probs = jnp.where(mask, jnp.exp(jnp.where(mask, scores, MASKED) - lse[0, j : j + 1, :]), 0.0)
                g_p = nt(v[:count, cols], g_stack)
                inner = jnp.sum(probs * g_p, axis=0, keepdims=True)
                g_s = (probs * (g_p - inner)).astype(jnp.bfloat16)
                gk[:count, cols] += nn(g_s, stack) * scale
                gv[:count, cols] += nn(probs.astype(jnp.bfloat16), g_stack)
                gqt = nn(krt[cols, :count], g_s) * scale
                back = gqt.T
                for g in range(group):
                    gq_s[:, mine[g]] = back[g * TILE : (g + 1) * TILE, :]

    def unrope(g, u, gain):
        g = g * cos[...] - pltpu.roll(g, hd // 2, 1) * sin[...]
        r = rms_scale(u)
        nu = u * r
        gain_grad = jnp.sum(g * nu, axis=0, keepdims=True)
        ga = g * gain
        return r * (ga - nu * jnp.mean(ga * nu, axis=-1, keepdims=True)), gain_grad

    for head in range(heads):
        cols = slice(head * hd, (head + 1) * hd)
        g, gain_grad = unrope(gq_s[:, cols], q[:, cols], query_gain[...])
        gall_out[:, cols] = g.astype(jnp.bfloat16)
        small_out[0:1, :] += gain_grad
    rows = pl.ds(pl.multiple_of(tile * TILE, TILE), TILE)
    for j in range(kv):
        cols = slice(j * hd, (j + 1) * hd)
        g, gain_grad = unrope(gk[rows, cols], k[:, cols], key_gain[...])
        gall_out[:, 2 * q_width + j * hd : 2 * q_width + (j + 1) * hd] = g.astype(jnp.bfloat16)
        small_out[1:2, :] += gain_grad
    gall_out[:, 2 * q_width + k_width :] = gv[rows, :].astype(jnp.bfloat16)
    ga1 = (
        nt(gall_out[:, :q_width], wq[...])
        + nt(gall_out[:, q_width : 2 * q_width], wg[...])
        + nt(gall_out[:, 2 * q_width : 2 * q_width + k_width], wk[...])
        + nt(gall_out[:, 2 * q_width + k_width :], wv[...])
    )
    ga1_out[...] = ga1.astype(jnp.bfloat16)
    gain_out[...] += jnp.sum(ga1 * (xf * rms_scale(xf)), axis=0, keepdims=True)


def attn_backward(lengths, g2, x, attn, mlp, cot, gain_two, query_gain, key_gain, cos, sin,
                  qr, kr, v, q, k, gate, o, lse, wq, wg, wk, wv, wo):
    rows, width = x.shape
    steps = rows // TILE
    q_width, k_width = wq.shape[1], wk.shape[1]
    hd = query_gain.shape[1]
    tile = lambda w: pl.BlockSpec((TILE, w), lambda i: (steps - 1 - i, 0))
    bf, f32 = jnp.bfloat16, jnp.float32
    total = 2 * q_width + 2 * k_width
    return pl.pallas_call(
        attn_backward_kernel,
        grid=(steps,),
        out_shape=[
            jax.ShapeDtypeStruct((rows, width), bf), jax.ShapeDtypeStruct((rows, width), bf),
            jax.ShapeDtypeStruct((rows, q_width), bf), jax.ShapeDtypeStruct((rows, total), bf),
            jax.ShapeDtypeStruct((rows, width), bf), jax.ShapeDtypeStruct((1, width), f32),
            jax.ShapeDtypeStruct((8, hd), f32),
        ],
        in_specs=[pl.BlockSpec(memory_space=pltpu.SMEM)] + [tile(width)] * 5
        + [whole(gain_two.shape), whole((1, hd)), whole((1, hd)), tile(hd), tile(hd),
                  tile(q_width), whole((rows, k_width)), whole((rows, k_width)), tile(q_width), tile(k_width),
                  tile(q_width), tile(q_width), pl.BlockSpec((1,) + lse.shape[1:], lambda i: (steps - 1 - i, 0, 0))]
        + [whole(w.shape) for w in (wq, wg, wk, wv, wo)],
        out_specs=[tile(width), tile(width), tile(q_width), tile(total), tile(width), whole((1, width)), whole((8, hd))],
        scratch_shapes=[pltpu.VMEM((k_width, rows), bf), pltpu.VMEM((rows, k_width), f32),
                        pltpu.VMEM((rows, k_width), f32), pltpu.VMEM((TILE, q_width), f32)],
        compiler_params=pltpu.CompilerParams(vmem_limit_bytes=60 * 1024 * 1024),
        cost_estimate=pl.CostEstimate(flops=2 * rows * width * (3 * q_width + 2 * k_width) + (12 << 30), bytes_accessed=50 << 20, transcendentals=4 << 20),
        name="attn_backward",
    )(lengths, g2, x, attn, mlp, cot, gain_two, query_gain, key_gain, cos, sin,
      qr, kr, v, q, k, gate, o, lse, wq, wg, wk, wv, wo)


def finish_kernel(moves, count, x, gain, grad_hidden, grad_sum, *refs):
    ins, tokens_out, outs = refs[:count], refs[count], refs[count + 1 :]
    xf = x[...].astype(jnp.float32)
    rho = rms_scale(xf)
    n = xf * rho
    gs = grad_sum[...].astype(jnp.float32) * gain_row(gain, 0)
    back = rho * (gs - n * jnp.mean(gs * n, axis=-1, keepdims=True))
    tokens_out[...] = (grad_hidden[...].astype(jnp.float32) + back).astype(jnp.bfloat16)
    for source, low, width, target, place in moves:
        outs[target][:, place : place + width] = ins[source][:, low : low + width].astype(jnp.float32)


def finish(x, gain, grad_hidden, grad_sum, grads, moves, widths):
    rows, width = x.shape
    steps = 4
    shard = grads[0].shape[0]
    tile = pl.BlockSpec((rows // steps, width), lambda i: (i, 0))
    part = lambda w: pl.BlockSpec((shard // steps, w), lambda i: (i, 0))
    return pl.pallas_call(
        functools.partial(finish_kernel, moves, len(grads)),
        grid=(steps,),
        out_shape=[jax.ShapeDtypeStruct((rows, width), jnp.bfloat16)]
        + [jax.ShapeDtypeStruct((shard, w), jnp.float32) for w in widths],
        in_specs=[tile, whole(gain.shape), tile, tile] + [part(g.shape[1]) for g in grads],
        out_specs=[tile] + [part(w) for w in widths],
        compiler_params=pltpu.CompilerParams(vmem_limit_bytes=60 * 1024 * 1024),
        cost_estimate=pl.CostEstimate(flops=20 * rows * width, bytes_accessed=30 << 20, transcendentals=0),
        name="finish",
    )(x, gain, grad_hidden, grad_sum, *grads)


def scatter_kernel(units, sources, lefts, count, A, B, H, small_count, sums, *refs):
    nu = len(units)
    left_refs, refs = refs[:lefts], refs[lefts:]
    ins, refs = refs[:count], refs[count:]
    if H:
        pieces, refs = refs[:small_count], refs[small_count:]
    sum_ins, refs = refs[:sums], refs[sums:]
    outs, sum_outs, refs = refs[:count], refs[count : count + sums], refs[count + sums :]
    if H:
        small_out, refs = refs[0], refs[1:]
    rest = list(refs)
    each = SUM_REFS - 2
    totals = [HeadSum((sum_ins[i], sum_outs[i]) + tuple(rest[i * each : (i + 1) * each])) for i in range(sums)]
    rest = rest[sums * each :]
    if H:
        small, row_in, col_in, row_send, row_recv, col_send, col_recv = rest[-7:]
        rest = rest[:-7]
    turned, rest = rest[:lefts], rest[lefts:]
    own, side_in, up_in, down_in, stage = (rest[k * nu:(k + 1) * nu] for k in range(5))
    side_send, side_recv, up_send, up_recv, down_send, down_recv = rest[5 * nu:]
    me = lax.axis_index("batch")
    a, b = me // B, me % B
    up_ok, down_ok = a < A - 1, a > 0

    R = own[0].shape[1]

    def product(u, blk, target):
        i, lo, width, _ = units[u]
        left = turned[sources[i]][pl.ds(pl.multiple_of(blk * R, R), R), :]
        target[...] = nn(left, ins[i][:, lo : lo + width]).astype(jnp.bfloat16)

    def turn(blk):
        for left, flat in zip(left_refs, turned):
            flat[pl.ds(pl.multiple_of(blk * R, R), R), :] = left[:, pl.ds(pl.multiple_of(blk * R, R), R)].T

    barrier = pltpu.get_barrier_semaphore()

    def greet(target):
        pl.semaphore_signal(barrier, inc=1, device_id={"batch": target}, device_id_type=MESH)

    n = A * B
    if H:
        head = lax.axis_index("heads")
        for k in range(1, n):
            greet((me + k) % n)
        for k in range(1, H):
            pl.semaphore_signal(barrier, inc=1, device_id={"heads": (head + k) % H}, device_id_type=MESH)
        guests = n - 1 + H - 1
    else:
        pl.when(up_ok)(lambda: greet(me + B))
        pl.when(down_ok)(lambda: greet(me - B))
        for k in range(1, B):
            greet(a * B + (b + k) % B)
        guests = up_ok.astype(jnp.int32) + down_ok.astype(jnp.int32) + (B - 1)
        if totals:
            totals[0].greet(barrier)
            guests = guests + 2

    def at_distance(d, fn):
        if d == 0:
            return

        @pl.when(a + d < A)
        def _():
            fn(a + d, True)

        @pl.when(a - d >= 0)
        def _():
            fn(a - d, False)

    if R % 128:
        for left, flat in zip(left_refs, turned):
            for low in range(0, flat.shape[0], 256):
                flat[low : low + 256, :] = left[:, low : low + 256].T
    pl.semaphore_wait(barrier, guests)
    for total in totals:
        total.start()

    def to_heads(k):
        return pltpu.make_async_remote_copy(
            small, row_in.at[head], row_send.at[k - 1], row_recv.at[head],
            device_id={"heads": (head + k) % H}, device_id_type=MESH)

    def to_batch(k):
        return pltpu.make_async_remote_copy(
            col_in.at[me], col_in.at[me], col_send.at[k - 1], col_recv.at[me],
            device_id={"batch": (me + k) % n}, device_id_type=MESH)

    if H:
        low = 0
        for piece_ref in pieces:
            rows = piece_ref.shape[0]
            small[low : low + rows, :] = piece_ref[...]
            low += rows
        for k in range(1, H):
            to_heads(k).start()
        row_in[head] = small[...]

    for d in range(A - 1, -1, -1):
        def start(dest, _=None):
            for k in range(1, B):
                bb = (b + k) % B
                if R % 128 == 0:
                    turn(dest * B + bb)
                for u in range(nu):
                    if units[u][3]:
                        continue
                    product(u, dest * B + bb, stage[u].at[k - 1, dest])
                    pltpu.make_async_remote_copy(
                        stage[u].at[k - 1, dest], side_in[u].at[k - 1, dest], side_send.at[u, k - 1, dest],
                        side_recv.at[u, k - 1, dest], device_id={"batch": a * B + bb}, device_id_type=MESH).start()

        at_distance(d, start) if d else start(a)
        if d == A - 1:
            for total in totals:
                total.cross()
    if R % 128 == 0:
        for dest in range(A):
            turn(dest * B + b)

    def await_bytes(ref, sem):
        pltpu.make_async_copy(ref, ref, sem).wait()

    if H:
        for k in range(1, H):
            other = (head + k) % H
            await_bytes(row_in.at[other], row_recv.at[other])
        group_sum = row_in[0]
        for k in range(1, H):
            group_sum = group_sum + row_in[k]
        col_in[me] = group_sum
        for k in range(1, n):
            to_batch(k).start()

    step_rows = min(R, 32)

    def add_into(target, terms):
        def body(t, carry):
            rows = pl.ds(pl.multiple_of(t * step_rows, step_rows), step_rows)
            total = terms[0][rows, :].astype(jnp.float32)
            for term in terms[1:]:
                total = total + term[rows, :].astype(jnp.float32)
            target[rows, :] = total.astype(target.dtype)
            return carry

        lax.fori_loop(0, R // step_rows, body, 0)

    def local_terms(u, dest, bb):
        if units[u][3]:
            slot = dest * B + bb
            product(u, slot, own[u].at[slot])
            return [own[u].at[slot]], slot
        product(u, dest * B + b, own[u].at[dest])
        for k in range(1, B):
            await_bytes(side_in[u].at[k - 1, dest], side_recv.at[u, k - 1, dest])
        return [own[u].at[dest]] + [side_in[u].at[k - 1, dest] for k in range(1, B)], dest

    order = [u for u in range(nu) if units[u][3]] + [u for u in range(nu) if not units[u][3]]
    for d in range(A - 1, 0, -1):
        for u in order:
            def flow(dest, goes_up, u=u):
                for k in range(B if units[u][3] else 1):
                    terms, slot = local_terms(u, dest, (b + k) % B)
                    buf = (up_in if goes_up else down_in)[u].at[slot]
                    send, recv = (up_send, up_recv) if goes_up else (down_send, down_recv)
                    fed = down_ok if goes_up else up_ok

                    @pl.when(fed)
                    def _():
                        await_bytes(buf, recv.at[u, slot])
                        add_into(buf, [buf] + terms)

                    @pl.when(jnp.logical_not(fed))
                    def _():
                        add_into(buf, terms)

                    pltpu.make_async_remote_copy(
                        buf, buf, send.at[u, slot], recv.at[u, slot],
                        device_id={"batch": me + B if goes_up else me - B}, device_id_type=MESH).start()

            at_distance(d, flow)

    def out_piece(u):
        i, lo, width, _ = units[u]
        return outs[i].at[:, pl.ds(lo, width)]

    def arrive_home(u, bb, target):
        terms, slot = local_terms(u, a, bb)

        @pl.when(down_ok)
        def _():
            await_bytes(up_in[u].at[slot], up_recv.at[u, slot])

        @pl.when(up_ok)
        def _():
            await_bytes(down_in[u].at[slot], down_recv.at[u, slot])

        @pl.when(down_ok & up_ok)
        def _():
            add_into(target, terms + [up_in[u].at[slot], down_in[u].at[slot]])

        @pl.when(down_ok & jnp.logical_not(up_ok))
        def _():
            add_into(target, terms + [up_in[u].at[slot]])

        @pl.when(up_ok & jnp.logical_not(down_ok))
        def _():
            add_into(target, terms + [down_in[u].at[slot]])

    for total in totals:
        total.settle()
    for u in order:
        if units[u][3]:
            for k in range(1, B):
                bb = (b + k) % B
                slot = a * B + bb
                arrive_home(u, bb, own[u].at[slot])
                pltpu.make_async_remote_copy(
                    own[u].at[slot], side_in[u].at[k - 1, 0], side_send.at[u, k - 1, 0], side_recv.at[u, k - 1, 0],
                    device_id={"batch": slot}, device_id_type=MESH).start()
            arrive_home(u, b, own[u].at[a * B + b])
        else:
            arrive_home(u, b, out_piece(u))
    for u in order:
        if units[u][3]:
            for k in range(1, B):
                await_bytes(side_in[u].at[k - 1, 0], side_recv.at[u, k - 1, 0])
            add_into(out_piece(u), [own[u].at[a * B + b]] + [side_in[u].at[k - 1, 0] for k in range(1, B)])

    for total in totals:
        total.finish()
    if H:
        for k in range(1, n):
            other = (me + k) % n
            await_bytes(col_in.at[other], col_recv.at[other])
        whole_sum = col_in[0]
        for k in range(1, n):
            whole_sum = whole_sum + col_in[k]
        small_out[...] = whole_sum
        for k in range(1, H):
            to_heads(k).wait_send()
        for k in range(1, n):
            to_batch(k).wait_send()

    for u in range(nu):
        first = units[u][3]
        for k in range(1, B):
            if first:
                await_bytes(side_in[u].at[k - 1, 0], side_send.at[u, k - 1, 0])
            else:
                for dest in range(A):
                    await_bytes(side_in[u].at[k - 1, dest], side_send.at[u, k - 1, dest])
        for d in range(A - 1, 0, -1):
            def done(dest, goes_up, u=u, first=first):
                send = up_send if goes_up else down_send
                for k in range(B if first else 1):
                    slot = dest * B + k if first else dest
                    await_bytes(up_in[u].at[slot], send.at[u, slot])

            at_distance(d, done)


def scatter_all(lefts, rights, sources, units, cid, small=None, sums=(), out_dtype=jnp.bfloat16):
    n = lax.axis_size("batch")
    A, B = grid_of(n)
    nu = len(units)
    R = lefts[0].shape[1] // n

    def slots(u):
        return n if units[u][3] else A

    scratch = [ref for s in sums for ref in head_sum_scratch(s)]
    scratch += [pltpu.VMEM(left.shape[::-1], left.dtype) for left in lefts]
    scratch += [pltpu.VMEM((slots(u), R, units[u][2]), jnp.bfloat16) for u in range(nu)]
    scratch += [pltpu.VMEM((B - 1, 1 if units[u][3] else A, R, units[u][2]), jnp.bfloat16) for u in range(nu)]
    scratch += [pltpu.VMEM((slots(u), R, units[u][2]), jnp.bfloat16) for u in range(nu)]
    scratch += [pltpu.VMEM((slots(u), R, units[u][2]), jnp.bfloat16) for u in range(nu)]
    scratch += [pltpu.VMEM((B - 1, 1 if units[u][3] else A, R, units[u][2]), jnp.bfloat16) for u in range(nu)]
    dma = pltpu.SemaphoreType.DMA
    scratch += [dma((nu, B - 1, A)), dma((nu, B - 1, A)), dma((nu, n)), dma((nu, n)), dma((nu, n)), dma((nu, n))]
    H = 0
    extra, small_outs = [], []
    if small is not None:
        H = lax.axis_size("heads")
        extra = list(small)
        small_shape = (sum(e.shape[0] for e in extra), extra[0].shape[1])
        small_outs = [jax.ShapeDtypeStruct(small_shape, jnp.float32)]
        scratch += [
            pltpu.VMEM(small_shape, jnp.float32),
            pltpu.VMEM((H,) + small_shape, jnp.float32), pltpu.VMEM((n,) + small_shape, jnp.float32),
            dma((H - 1,)), dma((H,)), dma((n - 1,)), dma((n,)),
        ]
    res = pl.pallas_call(
        functools.partial(scatter_kernel, units, sources, len(lefts), len(rights), A, B, H, len(extra), len(sums)),
        out_shape=[jax.ShapeDtypeStruct((R, g.shape[1]), out_dtype) for g in rights]
        + [jax.ShapeDtypeStruct(s.shape, s.dtype) for s in sums]
        + small_outs,
        in_specs=[pl.BlockSpec(memory_space=pltpu.VMEM)] * (len(lefts) + len(rights)) + [pl.BlockSpec(memory_space=pltpu.VMEM)] * len(extra) + [pl.BlockSpec(memory_space=pl.ANY)] * len(sums),
        out_specs=[pl.BlockSpec(memory_space=pltpu.VMEM)] * len(rights) + [pl.BlockSpec(memory_space=pl.ANY)] * len(sums)
        + [pl.BlockSpec(memory_space=pltpu.VMEM)] * len(small_outs),
        scratch_shapes=scratch,
        compiler_params=pltpu.CompilerParams(collective_id=cid, has_side_effects=True, vmem_limit_bytes=VMEM_LIMIT),
        cost_estimate=pl.CostEstimate(flops=0, bytes_accessed=sum(g.size for g in rights) * 16, transcendentals=0),
    )(*lefts, *rights, *extra, *sums)
    return list(res)


def column_units(widths, side_first, chunk=512):
    units = []
    for index, width in enumerate(widths):
        for low in range(0, width, chunk):
            units.append((index, low, min(chunk, width - low), (index, low) in side_first))
    return units


def local(
    tokens,
    lengths,
    cotangent,
    attn_norm_gain,
    query_norm_gain,
    key_norm_gain,
    w_query,
    w_gate_attn,
    w_key,
    w_value,
    w_out,
    mlp_norm_gain,
    w_gate,
    w_up,
    w_down,
):
    row_count, model_width = tokens.shape
    head_width = query_norm_gain.shape[0]
    shard_rows = w_query.shape[0]
    attn_shards = [w_query, w_gate_attn, w_key, w_value, w_out]
    gain_shards = [jnp.stack([attn_norm_gain, mlp_norm_gain])]
    query_full, gate_attn_full, key_full, value_full, out_full, gains = gather_all(
        attn_shards + gain_shards,
        [(5, None, None, False)] + column_units([w.shape[1] for w in attn_shards], {(2, 0)}),
        0,
    )
    cut = w_down.shape[1] // 2
    down_first, down_last = w_down[:, :cut], w_down[:, cut:]
    down_first, query_full = lax.optimization_barrier((down_first, query_full))
    down_first = lax.all_gather(down_first, "batch", axis=0, tiled=True)
    gains = gains.reshape(-1, 2, shard_rows)
    query_gain = query_norm_gain.astype(jnp.float32).reshape(1, -1)
    key_gain = key_norm_gain.astype(jnp.float32).reshape(1, -1)
    cos_table, sin_table = rotary_tables(row_count, head_width)
    turn_sign = jnp.where(lax.iota(jnp.int32, head_width) < head_width // 2, -1.0, 1.0)
    sin_table = sin_table * turn_sign
    attn_weights = (query_full, gate_attn_full, key_full, value_full, out_full)
    input_one, query_rot, key_rot, values, queries, keys_pre, gate_logit, attended, log_totals, attn_part = attn_forward(
        lengths, tokens, gains, query_gain, key_gain, cos_table, sin_table, *attn_weights
    )
    mlp_widths = [w_gate.shape[1], w_up.shape[1]]
    gate_full, up_full, attn_sum = gather_all(
        [w_gate, w_up], column_units(mlp_widths, {(1, 0)}), 1, sums=[attn_part]
    )
    down_last, attn_sum = lax.optimization_barrier((down_last, attn_sum))
    down_last = lax.all_gather(down_last, "batch", axis=0, tiled=True)
    input_two, grad_mlp, activated, gate_pre, up_pre = mlp_forward(
        lengths, tokens, attn_sum, cotangent, gains, gate_full, up_full
    )
    grad_w_down = contract_rows(grad_mlp, activated).astype(jnp.bfloat16)
    grad_w_down, grad_mlp, activated = lax.optimization_barrier((grad_w_down, grad_mlp, activated))
    grad_down = lax.psum_scatter(grad_w_down, "batch", scatter_dimension=0, tiled=True)
    grad_gate_pre, grad_up_first, grad_up_last, mlp_part, grad_two_send, gain_two_part = mlp_backward(
        tokens, attn_sum, grad_mlp, activated, gate_pre, up_pre, gate_full, up_full, down_first, down_last
    )
    grad_w_late = contract_rows(input_two, grad_up_last).astype(jnp.bfloat16)
    input_two, grad_w_late = lax.optimization_barrier((input_two, grad_w_late))
    grad_gate, grad_up, grad_two_sum, mlp_sum = scatter_all(
        [input_two],
        [grad_gate_pre, grad_up_first],
        (0, 0),
        column_units([w_gate.shape[1], cut], {(1, 512)}),
        2,
        sums=[grad_two_send, mlp_part],
    )
    grad_two_sum, grad_w_late = lax.optimization_barrier((grad_two_sum, grad_w_late))
    grad_late = lax.psum_scatter(grad_w_late, "batch", scatter_dimension=0, tiled=True)
    output, grad_hidden, gated, grad_all, grad_one_send, gain_one_part, head_gains = attn_backward(
        lengths, grad_two_sum, tokens, attn_sum, mlp_sum, cotangent, gains, query_gain, key_gain,
        cos_table, sin_table, query_rot, key_rot, values, queries, keys_pre, gate_logit, attended, log_totals,
        *attn_weights,
    )
    counts = jnp.where(lax.iota(jnp.int32, head_width) == 0, jnp.sum(lengths), 0).astype(jnp.float32)
    once = (lax.axis_index("heads") == 0).astype(jnp.float32)
    own_sums = jnp.concatenate([head_gains[2:7], counts.reshape(1, -1)], axis=0) * once
    small = [
        gain_one_part.reshape(-1, head_width), gain_two_part.reshape(-1, head_width), head_gains[:2], own_sums,
    ]
    q_width, k_width = w_query.shape[1], w_key.shape[1]
    attn_units = [
        (0, 0, q_width, False),
        (0, q_width, q_width, False),
        (0, 2 * q_width, k_width, True),
        (0, 2 * q_width + k_width, k_width, False),
        (1, 0, q_width, False),
    ]
    grad_all_sum, grad_out_sum, grad_one_sum, sums = scatter_all(
        [input_one, grad_hidden],
        [grad_all, gated],
        (0, 1),
        attn_units,
        3,
        small,
        sums=[grad_one_send],
    )
    gain_rows = model_width // head_width
    mine = lax.axis_index("batch") * shard_rows
    gain_one_grad = lax.dynamic_slice(sums[:gain_rows].reshape(-1), (mine,), (shard_rows,))
    gain_two_grad = lax.dynamic_slice(sums[gain_rows : 2 * gain_rows].reshape(-1), (mine,), (shard_rows,))
    query_gain_all = sums[2 * gain_rows]
    key_gain_all = sums[2 * gain_rows + 1]
    squares_all = jnp.sum(sums[2 * gain_rows + 2 :], axis=1)
    block_rms = jnp.sqrt(squares_all[:5] / (squares_all[5] * model_width))
    widths = [w.shape[1] for w in attn_shards] + [w_gate.shape[1], w_up.shape[1], w_down.shape[1]]
    moves, low = [], 0
    for index in range(4):
        moves.append((0, low, widths[index], index, 0))
        low += widths[index]
    moves += [
        (1, 0, widths[4], 4, 0),
        (2, 0, widths[5], 5, 0),
        (3, 0, cut, 6, 0),
        (4, 0, widths[6] - cut, 6, cut),
        (5, 0, widths[7], 7, 0),
    ]
    grad_tokens, *weight_grads = finish(
        tokens, gains, grad_hidden, grad_one_sum,
        [grad_all_sum, grad_out_sum, grad_gate, grad_up, grad_late, grad_down], moves, widths,
    )
    return (
        output,
        grad_tokens,
        gain_one_grad,
        query_gain_all,
        key_gain_all,
        *weight_grads[:5],
        gain_two_grad,
        *weight_grads[5:],
        block_rms,
    )


def solution(mesh):
    return jax.shard_map(
        local,
        mesh=mesh,
        in_specs=(
            P("batch", None),
            P("batch"),
            P("batch", None),
            P("batch"),
            P(),
            P(),
            P("batch", "heads"),
            P("batch", "heads"),
            P("batch", "heads"),
            P("batch", "heads"),
            P("batch", "heads"),
            P("batch"),
            P("batch", "heads"),
            P("batch", "heads"),
            P("batch", "heads"),
        ),
        out_specs=(
            P("batch", None),
            P("batch", None),
            P("batch"),
            P(),
            P(),
            P("batch", "heads"),
            P("batch", "heads"),
            P("batch", "heads"),
            P("batch", "heads"),
            P("batch", "heads"),
            P("batch"),
            P("batch", "heads"),
            P("batch", "heads"),
            P("batch", "heads"),
            P(),
        ),
        check_vma=False,
    )
```

time: 1080 us -> 784 us (0.73)
  matrix products: 182 us -> 19.6 us
  Pallas kernels: 569 us -> 660 us
  waiting for transfers between devices: 150 us -> 63.9 us
  other arithmetic: 86 us -> 6.8 us
  blocking collectives: 40.4 us -> 0 us
  local copies, waits for them, and re-layouts: 30.9 us -> 9.14 us
    psum x3 -> x0, waiting for transfers between devices: 150 us -> none  [the longest x1 150 us: local(): mlp_out = lax.psum(mlp_part, 'heads').astype(jnp.float32)]
    dot_general x28 -> x0, matrix products: 135 us -> none  [the longest x8 58.9 us: contract_last(): lax.dot_general(left_side, right_side, (((1,), (1,)), ((), ())), preferre...]
    pallas_call x2 -> x7, Pallas kernels: 281 us -> 415 us  [the longest x2 267 us: scatter_all(): pl.pallas_call(functools.partial(scatter_kernel, units, sources, len(left...]
    pallas_call x2, Pallas kernels: 288 us -> 245 us  [gather_all(): pl.pallas_call(functools.partial(gather_kernel, plan, A, B), out_shape=ou...]
    reduce_scatter x0 -> x2, waiting for transfers between devices: none -> 42.4 us  [the longest x1 42.4 us: local(): lax.psum_scatter(grad_w_down, 'batch', scatter_dimension=0, tiled=True)]
    psum x1 -> x0, blocking collectives: 40.4 us -> none  [local(): lax.psum(jnp.concatenate([gain_one_part, gain_two_part, grad_query_gain,...]
    convert_element_type x21 -> x1, other arithmetic: 39.3 us -> 0.01 us  [local(): jnp.where(lax.iota(jnp.int32, head_width) == 0, jnp.sum(lengths), 0)]
    reduce_sum x8 -> x1, other arithmetic: 37.2 us -> 0.8 us  [local(): squares_all = jnp.sum(sums[2 * gain_rows + 2:], axis=1)]
  transfers between devices with their start and end apart: 3 -> 4, of which waited for: 1 -> 2; matrix products, arithmetic and copies ran while one was open for 3% -> 3% of each run, Pallas kernels for 44% -> 53%
where the time goes in v2:
time: 784 us; the launch traced here: 775 us
  Pallas kernels  660 us (84%)
  waiting for transfers between devices  63.9 us (8%)
  matrix products  19.6 us (3%)
  between operations  15.4 us (2%)
  local copies, waits for them, and re-layouts  9.14 us (1%)
    pallas_call x2, Pallas kernels, scatter_all(): pl.pallas_call(functools.partial(scatter_kernel, units, sources, len(left...  267 us
    pallas_call x2, Pallas kernels, gather_all(): pl.pallas_call(functools.partial(gather_kernel, plan, A, B), out_shape=ou...  245 us
    pallas_call x1, Pallas kernels, attn_backward(): pl.pallas_call(attn_backward_kernel, grid=(steps,), out_shape=[jax.ShapeD...  44.1 us
    reduce_scatter x1, waiting for transfers between devices, local(): lax.psum_scatter(grad_w_down, 'batch', scatter_dimension=0, tiled=True)  42.4 us
    pallas_call x1, Pallas kernels, mlp_backward(): pl.pallas_call(mlp_backward_kernel, grid=(rows // row_tile, 2), out_shape...  39.7 us
    pallas_call x1, Pallas kernels, mlp_forward(): pl.pallas_call(mlp_forward_kernel, grid=(rows // row_tile, ff // col_tile...  27.6 us
    pallas_call x1, Pallas kernels, attn_forward(): pl.pallas_call(attn_forward_kernel, grid=(steps,), out_shape=[jax.ShapeDt...  23.8 us
    all_gather x1, waiting for transfers between devices, local(): down_last = lax.all_gather(down_last, 'batch', axis=0, tiled=True)  20.9 us
  transfers between devices with their start and end apart: 4, of which 2 were waited for; matrix products, arithmetic and copies ran while one was open for 3% of the time, Pallas kernels for 53%

profile of v2, /device:TPU:0, one launch (start us, length us, event | category | flops | bytes accessed | tf_op | source)
XLA Modules:
  0.0 775.0 jit_solution(16564867420864177342)
XLA Ops:
  7.2 0.0 all-gather.3.cloned.1.call-start
  7.2 2.0 fusion.6
  9.3 0.7 stack.10
  9.9 0.7 stack.9
  10.6 0.6 pad_maximum_fusion.1.refs_5_
  11.2 91.3 %shard_map.262 = (bf16[8,256,512]{2,1,0:T(8,128)(2,1)}, bf16[8,256,512]{2,1,0:T(8,128)(2,1)}, bf16[8,256,256]{2,1,0:T(8,128)(2,1)}, bf16[8,256,256]{2,1,0:T(8,12...) custom-call(bf16[256,512]{1,0:T(8,128)(2,1)} %refs_0_.2, bf16[256,512]{1,0:T(8,128)(2,1)} %refs_1_.2, ...), custom_call_target="tpu_custom_call" | custom-call | bytes 31488000 | tf_op jit(solution)/shard_map/pallas_call | solution.py:293
  102.5 0.0 all-gather.3.cloned.1.call-update
  102.5 0.0 all-gather.5.cloned.1.call-start
  103.3 1.2 bitcast_convert_fusion
  104.4 0.2 broadcast_multiply_fusion
  104.7 2.9 sine_multiply_fusion
  107.5 23.8 %attn_forward.1 = (bf16[1024,2048]{1,0:T(8,128)(2,1)}, bf16[1024,512]{1,0:T(8,128)(2,1)}, bf16[1024,256]{1,0:T(8,128)(2,1)}, bf16[1024,256]{1,0:T(8,128)(2,1)}, ...) custom-call(s32[1]{0:T(128)} %copy.30.lengths, ...), custom_call_target="tpu_custom_call" | custom-call | flops 8589934592 | bytes 41943040 | tf_op jit(solution)/shard_map/attn_forward/pallas_call | solution.py:419
  131.3 154.0 %shard_map.263 = (bf16[8,256,1536]{2,1,0:T(8,128)(2,1)}, bf16[8,256,1536]{2,1,0:T(8,128)(2,1)}, bf16[1024,2048]{1,0:T(8,128)(2,1)}) custom-call(bf16[256,1536]{1,0:T(8,128)(2,1)} %refs_0_.3, bf16[256,1536]{1,0:T(8,128)(2,1)} %refs_1_.3, bf16[1024,2048]{1,0:T(8,128)(2,1)} %get-tuple-element.87.refs_2_), custom_call_target="tpu_custom_call" | custom-call | bytes 47185920 | tf_op jit(solution)/shard_map/pallas_call | solution.py:293
  285.3 0.0 all-gather.5.cloned.1.call-update
  285.3 0.0 reduce-scatter.3.cloned.1.call-start
  285.4 27.6 %mlp_forward.1 = (bf16[1024,2048]{1,0:T(8,128)(2,1)}, bf16[1024,2048]{1,0:T(8,128)(2,1)}, bf16[1024,1536]{1,0:T(8,128)(2,1)}, bf16[1024,1536]{1,0:T(8,128)(2,1)}, bf16[1024,1536]{1,0:T(8,128)(2,1)}) custom-call(s32[1]{0:T(128)} %copy.30.lengths, bf16[1024,2048]{1,0:T(8,128)(2,1)} %x.9, bf16[1024,2048]{1,0:T(8,128)(2,1)} %get-tuple-element.89.attn, ...), custom_call_target="tpu_custom_call" | custom-call | flops 12884901888 | bytes 52428800 | tf_op jit(solution)/shard_map/mlp_forward/pallas_call | solution.py:502
  313.0 11.8 %convolution_convert_fusion = bf16[2048,1536]{1,0:T(8,128)(2,1)} fusion(bf16[1024,2048]{1,0:T(8,128)(2,1)} %get-tuple-element.95.gm, bf16[1024,1536]{1,0:T(8,128)(2,1)} %get-tuple-element.96.hid), kind=kOutput, calls=%fused_computation | convolution fusion | flops 6445596672 | bytes 13631488 | tf_op jit(solution)/shard_map/dot_general | solution.py:20
  324.8 0.0 all-gather.3.cloned.1.call-done.wd_first
  324.8 20.9 %all-gather.5.cloned.1.call-done.wd_last = bf16[2048,768]{1,0:T(8,128)(2,1)} async-done(((bf16[256,768]{1,0:T(8,128)(2,1)}), bf16[2048,768]{1,0:T(8,128)(2,1)}) %all-gather.5.cloned.1.call-update) | async-done | bytes 3145744 | tf_op jit(solution)/shard_map/all_gather | solution.py:1066
  345.7 39.7 %mlp_backward.1 = (bf16[1024,1536]{1,0:T(8,128)(2,1)}, bf16[1024,768]{1,0:T(8,128)(2,1)}, bf16[1024,768]{1,0:T(8,128)(2,1)}, bf16[1024,2048]{1,0:T(8,128)(2,1)},...) custom-call(bf16[1024,2048]{1,0:T(8,128)(2,1)} %x.9, bf16[1024,2048]{1,0:T(8,128)(2,1)} %get-tuple-element.89.attn, ...), custom_call_target="tpu_custom_call" | custom-call | flops 25769803776 | bytes 62914560 | tf_op jit(solution)/shard_map/mlp_backward/pallas_call | solution.py:524
  385.4 7.8 %convolution_convert_fusion.1 = bf16[2048,768]{1,0:T(8,128)(2,1)} fusion(bf16[1024,2048]{1,0:T(8,128)(2,1)} %get-tuple-element.102.refs_0_, bf16[1024,768]{1,0:T(8,128)(2,1)} %get-tuple-element.101), kind=kOutput, calls=%fused_computation.1 | convolution fusion | flops 3222798336 | bytes 8912896 | tf_op jit(solution)/shard_map/dot_general | solution.py:20
  393.2 107.7 %shard_map.264 = (bf16[256,1536]{1,0:T(8,128)(2,1)}, bf16[256,768]{1,0:T(8,128)(2,1)}, bf16[1024,2048]{1,0:T(8,128)(2,1)}, bf16[1024,2048]{1,0:T(8,128)(2,1)}) custom-call(bf16[1024,2048]{1,0:T(8,128)(2,1)} %get-tuple-element.102.refs_0_, bf16[1024,1536]{1,0:T(8,128)(2,1)} %get-tuple-element.103.refs_1_, bf16[1024,768]{1,0:T(8,128)(2,1)} %get-tuple-element.104.refs_2_, ...), custom_call_target="tpu_custom_call" | custom-call | bytes 37748736 | tf_op jit(solution)/shard_map/pallas_call | solution.py:997
  500.9 0.0 reduce-scatter.3.cloned.1.call-update
  500.9 0.0 reduce-scatter.5.cloned.1.call-start
  501.0 0.5 reduce-scatter.5.cloned.1.call-update
  501.5 44.1 %attn_backward.1 = (bf16[1024,2048]{1,0:T(8,128)(2,1)}, bf16[1024,2048]{1,0:T(8,128)(2,1)}, bf16[1024,512]{1,0:T(8,128)(2,1)}, bf16[1024,1536]{1,0:T(8,128)(2,1)...) custom-call(s32[1]{0:T(128)} %copy.30.lengths, bf16[1024,2048]{1,0:T(8,128)(2,1)} %get-tuple-element.109.g2, ...), custom_call_target="tpu_custom_call" | custom-call | flops 21474836480 | bytes 52428800 | tf_op jit(solution)/shard_map/attn_backward/pallas_call | solution.py:650
  545.6 1.2 slice.35.refs_6_
  546.9 0.7 slice.36
  547.5 0.6 maximum_multiply_fusion.refs_7_
  548.1 159.6 %shard_map.265 = (bf16[256,1536]{1,0:T(8,128)(2,1)}, bf16[256,512]{1,0:T(8,128)(2,1)}, bf16[1024,2048]{1,0:T(8,128)(2,1)}, f32[40,128]{1,0:T(8,128)}) custom-call(bf16[1024,2048]{1,0:T(8,128)(2,1)} %get-tuple-element.121.refs_0_, bf16[1024,2048]{1,0:T(8,128)(2,1)} %get-tuple-element.120.refs_1_.grad_hidden, bf16[1024,1536]{1,0:T(8,128)(2,1)} %get-tuple-element.122.refs_2_, ...), custom_call_target="tpu_custom_call" | custom-call | bytes 33554432 | tf_op jit(solution)/shard_map/pallas_call | solution.py:997
  707.8 0.7 slice_bitcast_fusion
  708.5 0.6 dynamic_slice.6
  709.2 0.6 dynamic_slice.7
  709.8 0.8 slice_reduce_fusion
  710.6 0.6 slice.43
  711.8 0.5 divide_sqrt_fusion
  712.3 1.3 slice_bitcast_fusion.2
  713.6 0.0 reduce-scatter.3.cloned.1.call-done.refs_4_
  713.6 42.4 %reduce-scatter.5.cloned.1.call-done.refs_5_ = bf16[256,1536]{1,0:T(8,128)(2,1)} async-done(((bf16[2048,1536]{1,0:T(8,128)(2,1)}), bf16[256,1536]{1,0:T(8,128)(2,1)}) %reduce-scatter.5.cloned.1.call-update) | async-done | bytes 786448 | tf_op jit(solution)/shard_map/reduce_scatter | solution.py:1072
  756.0 12.3 %finish.1 = (bf16[1024,2048]{1,0:T(8,128)(2,1)}, f32[256,512]{1,0:T(8,128)}, f32[256,512]{1,0:T(8,128)}, f32[256,256]{1,0:T(8,128)}, f32[256,256]{1,0:T(8,128)},...) custom-call(bf16[1024,2048]{1,0:T(8,128)(2,1)} %x.9, ...), custom_call_target="tpu_custom_call" | custom-call | flops 41943040 | bytes 31457280 | tf_op jit(solution)/shard_map/finish/pallas_call | solution.py:692
  (4 shorter events, 0.0 us)
Async XLA Ops:
  7.2 317.6 %all-gather.3.cloned.1.call-start = ((), (), s32[]{:S(2)}) async-start(), calls=%async_computation.2 | async-start | bytes 3538944 | tf_op jit(solution)/shard_map/all_gather | solution.py:1050
  102.5 243.2 %all-gather.5.cloned.1.call-start = ((), (), s32[]{:S(2)}) async-start(), calls=%async_computation.3 | async-start | bytes 3538944 | tf_op jit(solution)/shard_map/all_gather | solution.py:1066
  285.3 428.3 %reduce-scatter.3.cloned.1.call-start = ((), (), s32[]{:S(2)}) async-start(), calls=%async_computation.4 | async-start | bytes 3538944 | tf_op jit(solution)/shard_map/reduce_scatter | solution.py:1087
  500.9 255.1 %reduce-scatter.5.cloned.1.call-start = ((), (), s32[]{:S(2)}) async-start(), calls=%async_computation.5 | async-start | bytes 7077888 | tf_op jit(solution)/shard_map/reduce_scatter | solution.py:1072
Sparse Core Ops, SparseCore 0:
  102.6 80.7 all-gather.2
  285.4 60.1 all-gather.4
  501.1 82.5 reduce-scatter.2
  587.1 168.9 reduce-scatter.4

commit v3 on v2

--- a/solution.py
+++ b/solution.py
@@ -1,4 +1,5 @@
 import functools
+import math
 
 import jax
 import jax.numpy as jnp
@@ -20,17 +21,6 @@
     return lax.dot_general(
         left_side, right_side, (((0,), (0,)), ((), ())), preferred_element_type=jnp.float32
     )
-
-
-def rotary_tables(row_count, head_width):
-    half_width = head_width // 2
-    positions = (lax.iota(jnp.int32, row_count) % SLOT_LEN).astype(jnp.float32)
-    inverse = ROPE_THETA ** (
-        -(lax.iota(jnp.int32, half_width).astype(jnp.float32) * 2.0 / head_width)
-    )
-    angles = positions[:, None] * inverse[None, :]
-    angles = jnp.concatenate([angles, angles], axis=1)
-    return (jnp.cos(angles), jnp.sin(angles))
 
 
 VMEM_LIMIT = 64 * 1024 * 1024 - 65536
@@ -134,6 +124,8 @@
     count, sums = plan["count"], plan["sums"]
     ins, sum_ins, refs = refs[:count], refs[count : count + sums], refs[count + sums :]
     outs, sum_outs, refs = refs[:count], refs[count : count + sums], refs[count + sums :]
+    if plan["tables"]:
+        cos_out, sin_out, refs = refs[0], refs[1], refs[2:]
     send_up, send_down, send_side, recv, local_sem = refs[:5]
     each = SUM_REFS - 2
     totals = [
@@ -239,6 +231,23 @@
                         side(u, block(u, blk), blk, 2 * s)
     for total in totals:
         total.finish()
+    if plan["tables"]:
+        rows, width = cos_out.shape
+        tile = min(rows, 128)
+        lane = lax.broadcasted_iota(jnp.int32, (1, width), 1)
+        column = (lane % (width // 2)).astype(jnp.float32)
+        inverse = jnp.exp(column * (-2.0 * math.log(ROPE_THETA) / width))
+        sign = jnp.where(lane < width // 2, -1.0, 1.0)
+
+        def fill(t, carry):
+            first = pl.multiple_of(t * tile, tile)
+            place = (first + lax.broadcasted_iota(jnp.int32, (tile, 1), 0)) % SLOT_LEN
+            angles = place.astype(jnp.float32) * inverse
+            cos_out[pl.ds(first, tile), :] = jnp.cos(angles)
+            sin_out[pl.ds(first, tile), :] = jnp.sin(angles) * sign
+            return carry
+
+        lax.fori_loop(0, rows // tile, fill, 0)
     for u in range(nu):
         if not units[u][3]:
             for s in range(A):
@@ -282,19 +291,20 @@
         pltpu.make_async_copy(ins[i], outs[i].at[me], local_sem.at[i]).wait()
 
 
-def gather_all(shards, plan_units, cid, sums=()):
+def gather_all(shards, plan_units, cid, sums=(), tables=None):
     n = lax.axis_size("batch")
     A, B = grid_of(n)
     nu = len(plan_units)
-    plan = {"count": len(shards), "units": plan_units, "sums": len(sums)}
+    plan = {"count": len(shards), "units": plan_units, "sums": len(sums), "tables": tables is not None}
     outs = [jax.ShapeDtypeStruct((n,) + s.shape, s.dtype) for s in shards]
     outs += [jax.ShapeDtypeStruct(s.shape, s.dtype) for s in sums]
+    table_outs = [jax.ShapeDtypeStruct(tables, jnp.float32)] * 2 if tables else []
     sum_scratch = [ref for s in sums for ref in head_sum_scratch(s)]
     res = pl.pallas_call(
         functools.partial(gather_kernel, plan, A, B),
-        out_shape=outs,
+        out_shape=outs + table_outs,
         in_specs=[pl.BlockSpec(memory_space=pltpu.VMEM)] * len(shards) + [pl.BlockSpec(memory_space=pl.ANY)] * len(sums),
-        out_specs=[pl.BlockSpec(memory_space=pl.ANY)] * len(outs),
+        out_specs=[pl.BlockSpec(memory_space=pl.ANY)] * len(outs) + [pl.BlockSpec(memory_space=pltpu.VMEM)] * len(table_outs),
         scratch_shapes=[
             pltpu.SemaphoreType.DMA((nu, A * B)),
             pltpu.SemaphoreType.DMA((nu, A * B)),
@@ -358,17 +368,17 @@
     gate_out[...] = gate
 
     def rope(u, g):
-        n = u * rms_scale(u) * g
+        n = u * rms_scale(u) * g[...].astype(jnp.float32)
         return (n * cos[...] + pltpu.roll(n, hd // 2, 1) * sin[...]).astype(jnp.bfloat16)
 
     rows = pl.ds(pl.multiple_of(step * TILE, TILE), TILE)
     for j in range(kv):
         cols = slice(j * hd, (j + 1) * hd)
-        kr = rope(k[:, cols], key_gain[...])
+        kr = rope(k[:, cols], key_gain)
         kr_out[:, cols] = kr
         kr_all[rows, cols] = kr
     vt_all[:, rows] = v.T.astype(jnp.bfloat16)
-    qr = [rope(q[:, h * hd : (h + 1) * hd], query_gain[...]) for h in range(heads)]
+    qr = [rope(q[:, h * hd : (h + 1) * hd], query_gain) for h in range(heads)]
     for h in range(heads):
         qr_out[:, h * hd : (h + 1) * hd] = qr[h]
     seq_length = lengths[0]
@@ -538,7 +548,7 @@
 def attn_backward_kernel(
     lengths, g2, x, attn, mlp, cot, gain_two, query_gain, key_gain, cos, sin,
     qr, kr, v, q, k, gate, o, lse, wq, wg, wk, wv, wo,
-    y_out, ghb_out, og_out, gall_out, ga1_out, gain_out, small_out,
+    y_out, ghb_out, og_out, gall_out, ga1_out, gain_out, small_out, square_out,
     krt, gk, gv, gq_s,
 ):
     step = pl.program_id(0)
@@ -557,6 +567,7 @@
         gv[...] = jnp.zeros_like(gv)
         gain_out[...] = jnp.zeros_like(gain_out)
         small_out[...] = jnp.zeros_like(small_out)
+        square_out[...] = jnp.zeros_like(square_out)
 
     places = tile * TILE + lax.broadcasted_iota(jnp.int32, (TILE, 1), 0)
     live = places < seq_length
@@ -566,13 +577,20 @@
     h = xf + attn_f
     y = h + mlp_f
     y_out[...] = jnp.where(live, y, 0.0).astype(jnp.bfloat16)
-    for r, field in enumerate((xf, h, y, attn_f, mlp_f)):
+    first_lane = (lax.broadcasted_iota(jnp.int32, (1, hd), 1) == 0).astype(jnp.float32)
+    width = float(xf.shape[1])
+    mean_x = jnp.mean(xf * xf, axis=-1, keepdims=True)
+    mean_h = jnp.mean(h * h, axis=-1, keepdims=True)
+    for r, mean in ((0, mean_x), (1, mean_h)):
+        square_out[r : r + 1, :] += jnp.sum(jnp.where(live, mean, 0.0), axis=0, keepdims=True) * width * first_lane
+    for r, field in ((2, y), (3, attn_f), (4, mlp_f)):
         by_lane = jnp.sum(jnp.where(live, field * field, 0.0), axis=0, keepdims=True)
         folded = by_lane[:, :hd]
         for low in range(hd, by_lane.shape[1], hd):
             folded = folded + by_lane[:, low : low + hd]
-        small_out[2 + r : 3 + r, :] += folded
-    rho = rms_scale(h)
+        square_out[r : r + 1, :] += folded
+    square_out[5:6, :] += jnp.sum(live.astype(jnp.float32), axis=0, keepdims=True) * first_lane
+    rho = lax.rsqrt(mean_h + NORM_EPS)
     n = h * rho
     gs = g2[...].astype(jnp.float32) * gain_row(gain_two, 1)
     g_out = jnp.where(live, cot[...].astype(jnp.float32), 0.0)
@@ -613,18 +631,18 @@
         r = rms_scale(u)
         nu = u * r
         gain_grad = jnp.sum(g * nu, axis=0, keepdims=True)
-        ga = g * gain
+        ga = g * gain[...].astype(jnp.float32)
         return r * (ga - nu * jnp.mean(ga * nu, axis=-1, keepdims=True)), gain_grad
 
     for head in range(heads):
         cols = slice(head * hd, (head + 1) * hd)
-        g, gain_grad = unrope(gq_s[:, cols], q[:, cols], query_gain[...])
+        g, gain_grad = unrope(gq_s[:, cols], q[:, cols], query_gain)
         gall_out[:, cols] = g.astype(jnp.bfloat16)
         small_out[0:1, :] += gain_grad
     rows = pl.ds(pl.multiple_of(tile * TILE, TILE), TILE)
     for j in range(kv):
         cols = slice(j * hd, (j + 1) * hd)
-        g, gain_grad = unrope(gk[rows, cols], k[:, cols], key_gain[...])
+        g, gain_grad = unrope(gk[rows, cols], k[:, cols], key_gain)
         gall_out[:, 2 * q_width + j * hd : 2 * q_width + (j + 1) * hd] = g.astype(jnp.bfloat16)
         small_out[1:2, :] += gain_grad
     gall_out[:, 2 * q_width + k_width :] = gv[rows, :].astype(jnp.bfloat16)
@@ -635,7 +653,12 @@
         + nt(gall_out[:, 2 * q_width + k_width :], wv[...])
     )
     ga1_out[...] = ga1.astype(jnp.bfloat16)
-    gain_out[...] += jnp.sum(ga1 * (xf * rms_scale(xf)), axis=0, keepdims=True)
+
+    @pl.when(step == steps - 1)
+    def _():
+        square_out[...] = square_out[...] * (lax.axis_index("heads") == 0).astype(jnp.float32)
+
+    gain_out[...] += jnp.sum(ga1 * (xf * lax.rsqrt(mean_x + NORM_EPS)), axis=0, keepdims=True)
 
 
 def attn_backward(lengths, g2, x, attn, mlp, cot, gain_two, query_gain, key_gain, cos, sin,
@@ -654,14 +677,14 @@
             jax.ShapeDtypeStruct((rows, width), bf), jax.ShapeDtypeStruct((rows, width), bf),
             jax.ShapeDtypeStruct((rows, q_width), bf), jax.ShapeDtypeStruct((rows, total), bf),
             jax.ShapeDtypeStruct((rows, width), bf), jax.ShapeDtypeStruct((1, width), f32),
-            jax.ShapeDtypeStruct((8, hd), f32),
+            jax.ShapeDtypeStruct((2, hd), f32), jax.ShapeDtypeStruct((6, hd), f32),
         ],
         in_specs=[pl.BlockSpec(memory_space=pltpu.SMEM)] + [tile(width)] * 5
         + [whole(gain_two.shape), whole((1, hd)), whole((1, hd)), tile(hd), tile(hd),
                   tile(q_width), whole((rows, k_width)), whole((rows, k_width)), tile(q_width), tile(k_width),
                   tile(q_width), tile(q_width), pl.BlockSpec((1,) + lse.shape[1:], lambda i: (steps - 1 - i, 0, 0))]
         + [whole(w.shape) for w in (wq, wg, wk, wv, wo)],
-        out_specs=[tile(width), tile(width), tile(q_width), tile(total), tile(width), whole((1, width)), whole((8, hd))],
+        out_specs=[tile(width), tile(width), tile(q_width), tile(total), tile(width), whole((1, width)), whole((2, hd)), whole((6, hd))],
         scratch_shapes=[pltpu.VMEM((k_width, rows), bf), pltpu.VMEM((rows, k_width), f32),
                         pltpu.VMEM((rows, k_width), f32), pltpu.VMEM((TILE, q_width), f32)],
         compiler_params=pltpu.CompilerParams(vmem_limit_bytes=60 * 1024 * 1024),
@@ -685,8 +708,8 @@
 
 def finish(x, gain, grad_hidden, grad_sum, grads, moves, widths):
     rows, width = x.shape
+    shard = grads[0].shape[0]
     steps = 4
-    shard = grads[0].shape[0]
     tile = pl.BlockSpec((rows // steps, width), lambda i: (i, 0))
     part = lambda w: pl.BlockSpec((shard // steps, w), lambda i: (i, 0))
     return pl.pallas_call(
@@ -702,16 +725,18 @@
     )(x, gain, grad_hidden, grad_sum, *grads)
 
 
-def scatter_kernel(units, sources, lefts, count, A, B, H, small_count, sums, *refs):
+def scatter_kernel(units, sources, kept, lefts, count, A, B, H, small_count, sums, *refs):
     nu = len(units)
     left_refs, refs = refs[:lefts], refs[lefts:]
     ins, refs = refs[:count], refs[count:]
+    kept_ins, refs = refs[: len(kept)], refs[len(kept) :]
     if H:
         pieces, refs = refs[:small_count], refs[small_count:]
     sum_ins, refs = refs[:sums], refs[sums:]
     outs, sum_outs, refs = refs[:count], refs[count : count + sums], refs[count + sums :]
     if H:
         small_out, refs = refs[0], refs[1:]
+    kept_outs, refs = refs[: len(kept)], refs[len(kept) :]
     rest = list(refs)
     each = SUM_REFS - 2
     totals = [HeadSum((sum_ins[i], sum_outs[i]) + tuple(rest[i * each : (i + 1) * each])) for i in range(sums)]
@@ -821,6 +846,13 @@
     if R % 128 == 0:
         for dest in range(A):
             turn(dest * B + b)
+    for which, right, whole_out in zip(kept, kept_ins, kept_outs):
+        def keep(blk, carry, which=which, right=right, whole_out=whole_out):
+            rows = pl.ds(pl.multiple_of(blk * R, R), R)
+            whole_out[rows, :] = nn(turned[which][rows, :], right[...]).astype(jnp.bfloat16)
+            return carry
+
+        lax.fori_loop(0, n, keep, 0)
 
     def await_bytes(ref, sem):
         pltpu.make_async_copy(ref, ref, sem).wait()
@@ -964,7 +996,7 @@
             at_distance(d, done)
 
 
-def scatter_all(lefts, rights, sources, units, cid, small=None, sums=(), out_dtype=jnp.bfloat16):
+def scatter_all(lefts, rights, sources, units, cid, small=None, sums=(), kept=(), kept_rights=(), out_dtype=jnp.bfloat16):
     n = lax.axis_size("batch")
     A, B = grid_of(n)
     nu = len(units)
@@ -995,17 +1027,18 @@
             dma((H - 1,)), dma((H,)), dma((n - 1,)), dma((n,)),
         ]
     res = pl.pallas_call(
-        functools.partial(scatter_kernel, units, sources, len(lefts), len(rights), A, B, H, len(extra), len(sums)),
+        functools.partial(scatter_kernel, units, sources, kept, len(lefts), len(rights), A, B, H, len(extra), len(sums)),
         out_shape=[jax.ShapeDtypeStruct((R, g.shape[1]), out_dtype) for g in rights]
         + [jax.ShapeDtypeStruct(s.shape, s.dtype) for s in sums]
-        + small_outs,
-        in_specs=[pl.BlockSpec(memory_space=pltpu.VMEM)] * (len(lefts) + len(rights)) + [pl.BlockSpec(memory_space=pltpu.VMEM)] * len(extra) + [pl.BlockSpec(memory_space=pl.ANY)] * len(sums),
+        + small_outs
+        + [jax.ShapeDtypeStruct((lefts[w].shape[1], g.shape[1]), out_dtype) for w, g in zip(kept, kept_rights)],
+        in_specs=[pl.BlockSpec(memory_space=pltpu.VMEM)] * (len(lefts) + len(rights) + len(kept)) + [pl.BlockSpec(memory_space=pltpu.VMEM)] * len(extra) + [pl.BlockSpec(memory_space=pl.ANY)] * len(sums),
         out_specs=[pl.BlockSpec(memory_space=pltpu.VMEM)] * len(rights) + [pl.BlockSpec(memory_space=pl.ANY)] * len(sums)
-        + [pl.BlockSpec(memory_space=pltpu.VMEM)] * len(small_outs),
+        + [pl.BlockSpec(memory_space=pltpu.VMEM)] * (len(small_outs) + len(kept)),
         scratch_shapes=scratch,
         compiler_params=pltpu.CompilerParams(collective_id=cid, has_side_effects=True, vmem_limit_bytes=VMEM_LIMIT),
         cost_estimate=pl.CostEstimate(flops=0, bytes_accessed=sum(g.size for g in rights) * 16, transcendentals=0),
-    )(*lefts, *rights, *extra, *sums)
+    )(*lefts, *rights, *kept_rights, *extra, *sums)
     return list(res)
 
 
@@ -1039,28 +1072,32 @@
     shard_rows = w_query.shape[0]
     attn_shards = [w_query, w_gate_attn, w_key, w_value, w_out]
     gain_shards = [jnp.stack([attn_norm_gain, mlp_norm_gain])]
-    query_full, gate_attn_full, key_full, value_full, out_full, gains = gather_all(
-        attn_shards + gain_shards,
-        [(5, None, None, False)] + column_units([w.shape[1] for w in attn_shards], {(2, 0)}),
-        0,
+    q_width, k_width = w_query.shape[1], w_key.shape[1]
+    gather_units = [
+        (5, None, None, False),
+        (0, 0, q_width, False),
+        (1, 0, q_width, False),
+        (2, 0, k_width, True),
+        (3, 0, k_width, False),
+        (4, 0, q_width, False),
+    ]
+    query_full, gate_attn_full, key_full, value_full, out_full, gains, cos_table, sin_table = gather_all(
+        attn_shards + gain_shards, gather_units, 0, tables=(row_count, head_width)
     )
     cut = w_down.shape[1] // 2
     down_first, down_last = w_down[:, :cut], w_down[:, cut:]
     down_first, query_full = lax.optimization_barrier((down_first, query_full))
     down_first = lax.all_gather(down_first, "batch", axis=0, tiled=True)
     gains = gains.reshape(-1, 2, shard_rows)
-    query_gain = query_norm_gain.astype(jnp.float32).reshape(1, -1)
-    key_gain = key_norm_gain.astype(jnp.float32).reshape(1, -1)
-    cos_table, sin_table = rotary_tables(row_count, head_width)
-    turn_sign = jnp.where(lax.iota(jnp.int32, head_width) < head_width // 2, -1.0, 1.0)
-    sin_table = sin_table * turn_sign
+    query_gain = query_norm_gain.reshape(1, -1)
+    key_gain = key_norm_gain.reshape(1, -1)
     attn_weights = (query_full, gate_attn_full, key_full, value_full, out_full)
     input_one, query_rot, key_rot, values, queries, keys_pre, gate_logit, attended, log_totals, attn_part = attn_forward(
         lengths, tokens, gains, query_gain, key_gain, cos_table, sin_table, *attn_weights
     )
     mlp_widths = [w_gate.shape[1], w_up.shape[1]]
     gate_full, up_full, attn_sum = gather_all(
-        [w_gate, w_up], column_units(mlp_widths, {(1, 0)}), 1, sums=[attn_part]
+        [w_gate, w_up], column_units(mlp_widths, {(1, 0)}, 384), 1, sums=[attn_part]
     )
     down_last, attn_sum = lax.optimization_barrier((down_last, attn_sum))
     down_last = lax.all_gather(down_last, "batch", axis=0, tiled=True)
@@ -1073,30 +1110,32 @@
     grad_gate_pre, grad_up_first, grad_up_last, mlp_part, grad_two_send, gain_two_part = mlp_backward(
         tokens, attn_sum, grad_mlp, activated, gate_pre, up_pre, gate_full, up_full, down_first, down_last
     )
-    grad_w_late = contract_rows(input_two, grad_up_last).astype(jnp.bfloat16)
-    input_two, grad_w_late = lax.optimization_barrier((input_two, grad_w_late))
-    grad_gate, grad_up, grad_two_sum, mlp_sum = scatter_all(
+    late_units = [
+        (0, 0, 512, False),
+        (0, 512, 512, False),
+        (0, 1024, 512, False),
+        (1, 0, cut // 2, False),
+        (1, cut // 2, cut // 2, False),
+    ]
+    grad_gate, grad_up, grad_two_sum, mlp_sum, grad_w_late = scatter_all(
         [input_two],
         [grad_gate_pre, grad_up_first],
         (0, 0),
-        column_units([w_gate.shape[1], cut], {(1, 512)}),
+        late_units,
         2,
         sums=[grad_two_send, mlp_part],
-    )
-    grad_two_sum, grad_w_late = lax.optimization_barrier((grad_two_sum, grad_w_late))
+        kept=(0,),
+        kept_rights=[grad_up_last],
+    )
     grad_late = lax.psum_scatter(grad_w_late, "batch", scatter_dimension=0, tiled=True)
-    output, grad_hidden, gated, grad_all, grad_one_send, gain_one_part, head_gains = attn_backward(
+    output, grad_hidden, gated, grad_all, grad_one_send, gain_one_part, head_gains, own_sums = attn_backward(
         lengths, grad_two_sum, tokens, attn_sum, mlp_sum, cotangent, gains, query_gain, key_gain,
         cos_table, sin_table, query_rot, key_rot, values, queries, keys_pre, gate_logit, attended, log_totals,
         *attn_weights,
     )
-    counts = jnp.where(lax.iota(jnp.int32, head_width) == 0, jnp.sum(lengths), 0).astype(jnp.float32)
-    once = (lax.axis_index("heads") == 0).astype(jnp.float32)
-    own_sums = jnp.concatenate([head_gains[2:7], counts.reshape(1, -1)], axis=0) * once
     small = [
-        gain_one_part.reshape(-1, head_width), gain_two_part.reshape(-1, head_width), head_gains[:2], own_sums,
+        gain_one_part.reshape(-1, head_width), gain_two_part.reshape(-1, head_width), head_gains, own_sums,
     ]
-    q_width, k_width = w_query.shape[1], w_key.shape[1]
     attn_units = [
         (0, 0, q_width, False),
         (0, q_width, q_width, False),

time: 784 us -> 779 us (level)
  Pallas kernels: 660 us -> 668 us
    pallas_call x2, Pallas kernels: 267 us -> 279 us  [scatter_all(): pl.pallas_call(functools.partial(scatter_kernel, units, sources, kept, le...]
    dot_general x2 -> x1, matrix products: 19.6 us -> 11.8 us  [contract_rows(): lax.dot_general(left_side, right_side, (((0,), (0,)), ((), ())), preferre...]
  transfers between devices with their start and end apart: 4 -> 4, of which waited for: 2 -> 2; matrix products, arithmetic and copies ran while one was open for 3% -> 2% of each run, Pallas kernels for 53% -> 53%
where the time goes in v3:
time: 779 us; the launch traced here: 770 us
  Pallas kernels  668 us (86%)
  waiting for transfers between devices  66.1 us (8%)
  between operations  15.3 us (2%)
  matrix products  11.8 us (2%)
    pallas_call x2, Pallas kernels, scatter_all(): pl.pallas_call(functools.partial(scatter_kernel, units, sources, kept, le...  279 us
    pallas_call x2, Pallas kernels, gather_all(): pl.pallas_call(functools.partial(gather_kernel, plan, A, B), out_shape=ou...  243 us
    reduce_scatter x1, waiting for transfers between devices, local(): lax.psum_scatter(grad_w_down, 'batch', scatter_dimension=0, tiled=True)  44.8 us
    pallas_call x1, Pallas kernels, attn_backward(): pl.pallas_call(attn_backward_kernel, grid=(steps,), out_shape=[jax.ShapeD...  43.5 us
    pallas_call x1, Pallas kernels, mlp_backward(): pl.pallas_call(mlp_backward_kernel, grid=(rows // row_tile, 2), out_shape...  39.5 us
    pallas_call x1, Pallas kernels, mlp_forward(): pl.pallas_call(mlp_forward_kernel, grid=(rows // row_tile, ff // col_tile...  27.7 us
    pallas_call x1, Pallas kernels, attn_forward(): pl.pallas_call(attn_forward_kernel, grid=(steps,), out_shape=[jax.ShapeDt...  23.4 us
    all_gather x1, waiting for transfers between devices, local(): down_last = lax.all_gather(down_last, 'batch', axis=0, tiled=True)  20.8 us
  transfers between devices with their start and end apart: 4, of which 2 were waited for; matrix products, arithmetic and copies ran while one was open for 2% of the time, Pallas kernels for 53%

profile of v3, /device:TPU:0, one launch (start us, length us, event | category | flops | bytes accessed | tf_op | source)
XLA Modules:
  0.0 770.1 jit_solution(4476515833916201993)
XLA Ops:
  7.2 0.0 all-gather.3.cloned.1.call-start
  7.2 2.0 fusion
  9.3 0.7 stack.10
  9.9 0.7 stack.9
  10.6 0.6 pad_maximum_fusion.refs_5_
  11.2 92.3 %shard_map.262 = (bf16[8,256,512]{2,1,0:T(8,128)(2,1)}, bf16[8,256,512]{2,1,0:T(8,128)(2,1)}, bf16[8,256,256]{2,1,0:T(8,128)(2,1)}, bf16[8,256,256]{2,1,0:T(8,12...) custom-call(bf16[256,512]{1,0:T(8,128)(2,1)} %refs_0_.2, ...), custom_call_target="tpu_custom_call" | custom-call | bytes 31488000 | tf_op jit(solution)/shard_map/pallas_call | solution.py:303
  103.5 0.0 all-gather.3.cloned.1.call-update
  103.5 0.0 all-gather.5.cloned.1.call-start
  104.2 23.4 %attn_forward.1 = (bf16[1024,2048]{1,0:T(8,128)(2,1)}, bf16[1024,512]{1,0:T(8,128)(2,1)}, bf16[1024,256]{1,0:T(8,128)(2,1)}, bf16[1024,256]{1,0:T(8,128)(2,1)}, ...) custom-call(s32[1]{0:T(128)S(6)} %copy.30.lengths, ...), custom_call_target="tpu_custom_call" | custom-call | flops 8589934592 | bytes 41943040 | tf_op jit(solution)/shard_map/attn_forward/pallas_call | solution.py:429
  127.6 150.2 %shard_map.263 = (bf16[8,256,1536]{2,1,0:T(8,128)(2,1)}, bf16[8,256,1536]{2,1,0:T(8,128)(2,1)}, bf16[1024,2048]{1,0:T(8,128)(2,1)}) custom-call(bf16[256,1536]{1,0:T(8,128)(2,1)} %refs_0_.3, bf16[256,1536]{1,0:T(8,128)(2,1)} %refs_1_.3, bf16[1024,2048]{1,0:T(8,128)(2,1)} %get-tuple-element.89.refs_2_), custom_call_target="tpu_custom_call" | custom-call | bytes 47185920 | tf_op jit(solution)/shard_map/pallas_call | solution.py:303
  277.8 0.0 all-gather.5.cloned.1.call-update
  277.8 0.0 reduce-scatter.3.cloned.1.call-start
  277.9 27.7 %mlp_forward.1 = (bf16[1024,2048]{1,0:T(8,128)(2,1)}, bf16[1024,2048]{1,0:T(8,128)(2,1)}, bf16[1024,1536]{1,0:T(8,128)(2,1)}, bf16[1024,1536]{1,0:T(8,128)(2,1)}, bf16[1024,1536]{1,0:T(8,128)(2,1)}) custom-call(s32[1]{0:T(128)S(6)} %copy.30.lengths, bf16[1024,2048]{1,0:T(8,128)(2,1)} %x.9, bf16[1024,2048]{1,0:T(8,128)(2,1)} %get-tuple-element.91.attn, ...), custom_call_target="tpu_custom_call" | custom-call | flops 12884901888 | bytes 52428800 | tf_op jit(solution)/shard_map/mlp_forward/pallas_call | solution.py:512
  305.5 11.8 %convolution_convert_fusion = bf16[2048,1536]{1,0:T(8,128)(2,1)} fusion(bf16[1024,2048]{1,0:T(8,128)(2,1)} %get-tuple-element.97.gm, bf16[1024,1536]{1,0:T(8,128)(2,1)} %get-tuple-element.98.hid), kind=kOutput, calls=%fused_computation | convolution fusion | flops 6445596672 | bytes 13631488 | tf_op jit(solution)/shard_map/dot_general | solution.py:21
  317.4 0.0 all-gather.3.cloned.1.call-done.wd_first
  317.4 20.8 %all-gather.5.cloned.1.call-done.wd_last = bf16[2048,768]{1,0:T(8,128)(2,1)} async-done(((bf16[256,768]{1,0:T(8,128)(2,1)}), bf16[2048,768]{1,0:T(8,128)(2,1)}) %all-gather.5.cloned.1.call-update) | async-done | bytes 3145744 | tf_op jit(solution)/shard_map/all_gather | solution.py:1103
  338.2 39.5 %mlp_backward.1 = (bf16[1024,1536]{1,0:T(8,128)(2,1)}, bf16[1024,768]{1,0:T(8,128)(2,1)}, bf16[1024,768]{1,0:T(8,128)(2,1)}, bf16[1024,2048]{1,0:T(8,128)(2,1)},...) custom-call(bf16[1024,2048]{1,0:T(8,128)(2,1)} %x.9, bf16[1024,2048]{1,0:T(8,128)(2,1)} %get-tuple-element.91.attn, ...), custom_call_target="tpu_custom_call" | custom-call | flops 25769803776 | bytes 62914560 | tf_op jit(solution)/shard_map/mlp_backward/pallas_call | solution.py:534
  377.7 112.1 %shard_map.264 = (bf16[256,1536]{1,0:T(8,128)(2,1)}, bf16[256,768]{1,0:T(8,128)(2,1)}, bf16[1024,2048]{1,0:T(8,128)(2,1)}, bf16[1024,2048]{1,0:T(8,128)(2,1)}, bf16[2048,768]{1,0:T(8,128)(2,1)}) custom-call(bf16[1024,2048]{1,0:T(8,128)(2,1)} %get-tuple-element.94.refs_0_, bf16[1024,1536]{1,0:T(8,128)(2,1)} %get-tuple-element.103.refs_1_, ...), custom_call_target="tpu_custom_call" | custom-call | bytes 37748736 | tf_op jit(solution)/shard_map/pallas_call | solution.py:1029
  489.9 0.0 reduce-scatter.3.cloned.1.call-update
  489.9 0.0 reduce-scatter.5.cloned.1.call-start
  489.9 0.5 reduce-scatter.5.cloned.1.call-update
  490.5 43.5 %attn_backward.1 = (bf16[1024,2048]{1,0:T(8,128)(2,1)}, bf16[1024,2048]{1,0:T(8,128)(2,1)}, bf16[1024,512]{1,0:T(8,128)(2,1)}, bf16[1024,1536]{1,0:T(8,128)(2,1)...) custom-call(s32[1]{0:T(128)S(6)} %copy.30.lengths, ...), custom_call_target="tpu_custom_call" | custom-call | flops 21474836480 | bytes 52428800 | tf_op jit(solution)/shard_map/attn_backward/pallas_call | solution.py:673
  534.0 166.6 %shard_map.265 = (bf16[256,1536]{1,0:T(8,128)(2,1)}, bf16[256,512]{1,0:T(8,128)(2,1)}, bf16[1024,2048]{1,0:T(8,128)(2,1)}, f32[40,128]{1,0:T(8,128)}) custom-call(bf16[1024,2048]{1,0:T(8,128)(2,1)} %get-tuple-element.120.refs_0_, bf16[1024,2048]{1,0:T(8,128)(2,1)} %get-tuple-element.119.refs_1_.grad_hidden, bf16[1024,1536]{1,0:T(8,128)(2,1)} %get-tuple-element.121.refs_2_, ...), custom_call_target="tpu_custom_call" | custom-call | bytes 33554432 | tf_op jit(solution)/shard_map/pallas_call | solution.py:1029
  700.6 0.7 slice_bitcast_fusion
  701.4 0.6 dynamic_slice.6
  702.0 0.6 dynamic_slice.7
  702.6 0.8 slice_reduce_fusion
  703.4 0.6 slice.35
  704.7 0.5 divide_sqrt_fusion
  705.2 1.3 slice_bitcast_fusion.2
  706.5 0.0 reduce-scatter.3.cloned.1.call-done.refs_4_
  706.5 44.8 %reduce-scatter.5.cloned.1.call-done.refs_5_ = bf16[256,1536]{1,0:T(8,128)(2,1)} async-done(((bf16[2048,1536]{1,0:T(8,128)(2,1)}), bf16[256,1536]{1,0:T(8,128)(2,1)}) %reduce-scatter.5.cloned.1.call-update) | async-done | bytes 786448 | tf_op jit(solution)/shard_map/reduce_scatter | solution.py:1109
  751.2 12.1 %finish.1 = (bf16[1024,2048]{1,0:T(8,128)(2,1)}, f32[256,512]{1,0:T(8,128)}, f32[256,512]{1,0:T(8,128)}, f32[256,256]{1,0:T(8,128)}, f32[256,256]{1,0:T(8,128)},...) custom-call(bf16[1024,2048]{1,0:T(8,128)(2,1)} %x.9, ...), custom_call_target="tpu_custom_call" | custom-call | flops 41943040 | bytes 31457280 | tf_op jit(solution)/shard_map/finish/pallas_call | solution.py:715
Async XLA Ops:
  7.2 310.2 %all-gather.3.cloned.1.call-start = ((), (), s32[]{:S(2)}) async-start(), calls=%async_computation.2 | async-start | bytes 3538944 | tf_op jit(solution)/shard_map/all_gather | solution.py:1090
  103.5 234.6 %all-gather.5.cloned.1.call-start = ((), (), s32[]{:S(2)}) async-start(), calls=%async_computation.3 | async-start | bytes 3538944 | tf_op jit(solution)/shard_map/all_gather | solution.py:1103
  277.8 428.7 %reduce-scatter.3.cloned.1.call-start = ((), (), s32[]{:S(2)}) async-start(), calls=%async_computation.4 | async-start | bytes 3538944 | tf_op jit(solution)/shard_map/reduce_scatter | solution.py:1130
  489.9 261.4 %reduce-scatter.5.cloned.1.call-start = ((), (), s32[]{:S(2)}) async-start(), calls=%async_computation.5 | async-start | bytes 7077888 | tf_op jit(solution)/shard_map/reduce_scatter | solution.py:1109
Sparse Core Ops, SparseCore 0:
  103.7 82.4 all-gather.2
  277.9 60.1 all-gather.4
  490.0 89.0 reduce-scatter.2
  582.6 168.6 reduce-scatter.4

commit v4 on v3

--- a/solution.py
+++ b/solution.py
@@ -459,42 +459,34 @@
     hid_out[...] = (gu * jax.nn.sigmoid(gu) * up).astype(jnp.bfloat16)
 
 
-def mlp_backward_kernel(
-    x, attn, gm, hid, gu_in, up_in, wg, wu, wd_first, wd_last,
-    ggu_out, gup_first, gup_last, part_out, ga2_out, gain_out, part_s, ga2_s,
-):
-    t, c = pl.program_id(0), pl.program_id(1)
-
-    def half(wd, gup_out):
-        gu, up = gu_in[...].astype(jnp.float32), up_in[...].astype(jnp.float32)
-        sg = jax.nn.sigmoid(gu)
-        g_hid = nn(gm[...], wd[...])
-        g_gu = (g_hid * up * sg * (1.0 + gu * (1.0 - sg))).astype(jnp.bfloat16)
-        g_up = (g_hid * (gu * sg)).astype(jnp.bfloat16)
+def mlp_backward_kernel(last, gm, hid, gu_in, up_in, wg, wu, wd, *refs):
+    gu, up = gu_in[...].astype(jnp.float32), up_in[...].astype(jnp.float32)
+    sg = jax.nn.sigmoid(gu)
+    g_hid = nn(gm[...], wd[...])
+    g_gu = (g_hid * up * sg * (1.0 + gu * (1.0 - sg))).astype(jnp.bfloat16)
+    g_up = (g_hid * (gu * sg)).astype(jnp.bfloat16)
+    part = nt(hid[...], wd[...])
+    ga2 = nt(g_gu, wg[...]) + nt(g_up, wu[...])
+    if not last:
+        ggu_out, gup_out, part_out, ga2_out = refs
         ggu_out[...] = g_gu
         gup_out[...] = g_up
-        return nt(hid[...], wd[...]), nt(g_gu, wg[...]) + nt(g_up, wu[...])
-
-    @pl.when(c == 0)
+        part_out[...] = part
+        ga2_out[...] = ga2
+        return
+    x, attn, part_in, ga2_in, ggu_out, gup_out, part_out, ga2_out, gain_out = refs
+    ggu_out[...] = g_gu
+    gup_out[...] = g_up
+    part_out[...] = (part_in[...] + part).astype(jnp.bfloat16)
+    ga2 = ga2_in[...] + ga2
+    ga2_out[...] = ga2.astype(jnp.bfloat16)
+    h = x[...].astype(jnp.float32) + attn[...].astype(jnp.float32)
+
+    @pl.when(pl.program_id(0) == 0)
     def _():
-        part_s[...], ga2_s[...] = half(wd_first, gup_first)
-
-    @pl.when(c == 1)
-    def _():
-        part, ga2 = half(wd_last, gup_last)
-        part_out[...] = (part_s[...] + part).astype(jnp.bfloat16)
-        ga2 = ga2_s[...] + ga2
-        ga2_out[...] = ga2.astype(jnp.bfloat16)
-        h = x[...].astype(jnp.float32) + attn[...].astype(jnp.float32)
-        mine = jnp.sum(ga2 * (h * rms_scale(h)), axis=0, keepdims=True)
-
-        @pl.when(t == 0)
-        def _():
-            gain_out[...] = mine
-
-        @pl.when(t > 0)
-        def _():
-            gain_out[...] += mine
+        gain_out[...] = jnp.zeros_like(gain_out)
+
+    gain_out[...] += jnp.sum(ga2 * (h * rms_scale(h)), axis=0, keepdims=True)
 
 
 def mlp_specs(width, row_tile, col_tile):
@@ -523,26 +515,30 @@
     )(lengths, x, attn, cot, gain, wg, wu)
 
 
-def mlp_backward(x, attn, gm, hid, gu, up, wg, wu, wd_first, wd_last, row_tile=512):
-    rows, width = x.shape
-    ff = wg.shape[1]
-    col_tile = ff // 2
-    wide, wcol, narrow, one = mlp_specs(width, row_tile, col_tile)
-    alone = pl.BlockSpec((row_tile, col_tile), lambda t, c: (t, 0))
-    fixed = pl.BlockSpec((width, col_tile), lambda t, c: (0, 0), pipeline_mode=pl.Buffered(1))
+def mlp_backward(which, gm, hid, gu, up, wg, wu, wd, rest=()):
+    rows, width = gm.shape
+    half = wd.shape[1]
+    wide = pl.BlockSpec((TILE, width), lambda t: (t, 0))
+    narrow = pl.BlockSpec((TILE, half), lambda t: (t, which))
+    alone = pl.BlockSpec((TILE, half), lambda t: (t, 0))
+    weight = pl.BlockSpec((width, half), lambda t: (0, which), pipeline_mode=pl.Buffered(1))
     bf, f32 = jnp.bfloat16, jnp.float32
+    kind = bf if rest else f32
+    shapes = [((rows, half), bf)] * 2 + [((rows, width), kind)] * 2
+    out_specs = [alone, alone, wide, wide]
+    if rest:
+        shapes.append(((1, width), f32))
+        out_specs.append(whole((1, width)))
     return pl.pallas_call(
-        mlp_backward_kernel,
-        grid=(rows // row_tile, 2),
-        out_shape=[jax.ShapeDtypeStruct((rows, ff), bf)] + [jax.ShapeDtypeStruct((rows, col_tile), bf)] * 2
-        + [jax.ShapeDtypeStruct((rows, width), bf)] * 2 + [jax.ShapeDtypeStruct((1, width), f32)],
-        in_specs=[wide, wide, wide, narrow, narrow, narrow, wcol, wcol, fixed, fixed],
-        out_specs=[narrow, alone, alone, wide, wide, one],
-        scratch_shapes=[pltpu.VMEM((row_tile, width), f32), pltpu.VMEM((row_tile, width), f32)],
-        compiler_params=pltpu.CompilerParams(vmem_limit_bytes=VMEM_LIMIT),
-        cost_estimate=pl.CostEstimate(flops=8 * rows * width * ff, bytes_accessed=60 << 20, transcendentals=rows * ff),
+        functools.partial(mlp_backward_kernel, bool(rest)),
+        grid=(rows // TILE,),
+        out_shape=[jax.ShapeDtypeStruct(*s) for s in shapes],
+        in_specs=[wide, narrow, narrow, narrow, weight, weight, whole(wd.shape)] + [wide] * len(rest),
+        out_specs=out_specs,
+        compiler_params=pltpu.CompilerParams(vmem_limit_bytes=60 * 1024 * 1024),
+        cost_estimate=pl.CostEstimate(flops=8 * rows * width * half, bytes_accessed=40 << 20, transcendentals=rows * half),
         name="mlp_backward",
-    )(x, attn, gm, hid, gu, up, wg, wu, wd_first, wd_last)
+    )(gm, hid, gu, up, wg, wu, wd, *rest)
 
 
 def attn_backward_kernel(
@@ -1107,21 +1103,16 @@
     grad_w_down = contract_rows(grad_mlp, activated).astype(jnp.bfloat16)
     grad_w_down, grad_mlp, activated = lax.optimization_barrier((grad_w_down, grad_mlp, activated))
     grad_down = lax.psum_scatter(grad_w_down, "batch", scatter_dimension=0, tiled=True)
-    grad_gate_pre, grad_up_first, grad_up_last, mlp_part, grad_two_send, gain_two_part = mlp_backward(
-        tokens, attn_sum, grad_mlp, activated, gate_pre, up_pre, gate_full, up_full, down_first, down_last
-    )
-    late_units = [
-        (0, 0, 512, False),
-        (0, 512, 512, False),
-        (0, 1024, 512, False),
-        (1, 0, cut // 2, False),
-        (1, cut // 2, cut // 2, False),
-    ]
-    grad_gate, grad_up, grad_two_sum, mlp_sum, grad_w_late = scatter_all(
+    halves = (activated, gate_pre, up_pre, gate_full, up_full)
+    grad_gate_first, grad_up_first, part_first, grad_two_first = mlp_backward(0, grad_mlp, *halves, down_first)
+    grad_gate_last, grad_up_last, mlp_part, grad_two_send, gain_two_part = mlp_backward(
+        1, grad_mlp, *halves, down_last, (tokens, attn_sum, part_first, grad_two_first)
+    )
+    grad_gate_one, grad_gate_two, grad_up, grad_two_sum, mlp_sum, grad_w_late = scatter_all(
         [input_two],
-        [grad_gate_pre, grad_up_first],
-        (0, 0),
-        late_units,
+        [grad_gate_first, grad_gate_last, grad_up_first],
+        (0, 0, 0),
+        column_units([cut] * 3, ()),
         2,
         sums=[grad_two_send, mlp_part],
         kept=(0,),
@@ -1167,14 +1158,15 @@
         low += widths[index]
     moves += [
         (1, 0, widths[4], 4, 0),
-        (2, 0, widths[5], 5, 0),
-        (3, 0, cut, 6, 0),
-        (4, 0, widths[6] - cut, 6, cut),
-        (5, 0, widths[7], 7, 0),
+        (2, 0, cut, 5, 0),
+        (3, 0, widths[5] - cut, 5, cut),
+        (4, 0, cut, 6, 0),
+        (5, 0, widths[6] - cut, 6, cut),
+        (6, 0, widths[7], 7, 0),
     ]
     grad_tokens, *weight_grads = finish(
         tokens, gains, grad_hidden, grad_one_sum,
-        [grad_all_sum, grad_out_sum, grad_gate, grad_up, grad_late, grad_down], moves, widths,
+        [grad_all_sum, grad_out_sum, grad_gate_one, grad_gate_two, grad_up, grad_late, grad_down], moves, widths,
     )
     return (
         output,

time: 779 us -> 766 us (0.983)
  waiting for transfers between devices: 66.1 us -> 45.7 us
    all_gather x1, waiting for transfers between devices: 20.8 us -> 0.59 us  [local(): down_last = lax.all_gather(down_last, 'batch', axis=0, tiled=True)]
    pallas_call x1 -> x2, Pallas kernels: 39.5 us -> 46.4 us  [mlp_backward(): pl.pallas_call(functools.partial(mlp_backward_kernel, bool(rest)), grid=(...]
  transfers between devices with their start and end apart: 4 -> 4, of which waited for: 2 -> 2; matrix products, arithmetic and copies ran while one was open for 2% -> 2% of each run, Pallas kernels for 53% -> 57%
where the time goes in v4:
time: 766 us; the launch traced here: 757 us
  Pallas kernels  675 us (88%)
  waiting for transfers between devices  45.7 us (6%)
  between operations  15.3 us (2%)
  matrix products  11.9 us (2%)
    pallas_call x2, Pallas kernels, scatter_all(): pl.pallas_call(functools.partial(scatter_kernel, units, sources, kept, le...  279 us
    pallas_call x2, Pallas kernels, gather_all(): pl.pallas_call(functools.partial(gather_kernel, plan, A, B), out_shape=ou...  243 us
    pallas_call x2, Pallas kernels, mlp_backward(): pl.pallas_call(functools.partial(mlp_backward_kernel, bool(rest)), grid=(...  46.4 us
    reduce_scatter x1, waiting for transfers between devices, local(): lax.psum_scatter(grad_w_down, 'batch', scatter_dimension=0, tiled=True)  44.6 us
    pallas_call x1, Pallas kernels, attn_backward(): pl.pallas_call(attn_backward_kernel, grid=(steps,), out_shape=[jax.ShapeD...  43.6 us
    pallas_call x1, Pallas kernels, mlp_forward(): pl.pallas_call(mlp_forward_kernel, grid=(rows // row_tile, ff // col_tile...  27.7 us
    pallas_call x1, Pallas kernels, attn_forward(): pl.pallas_call(attn_forward_kernel, grid=(steps,), out_shape=[jax.ShapeDt...  23.4 us
  transfers between devices with their start and end apart: 4, of which 2 were waited for; matrix products, arithmetic and copies ran while one was open for 2% of the time, Pallas kernels for 57%

profile of v4, /device:TPU:0, one launch (start us, length us, event | category | flops | bytes accessed | tf_op | source)
XLA Modules:
  0.0 757.1 jit_solution(14315919541563664858)
XLA Ops:
  7.2 0.0 all-gather.3.cloned.1.call-start
  7.2 0.7 stack.9
  7.9 0.7 stack.10
  8.5 2.0 fusion
  10.6 0.6 pad_maximum_fusion.refs_5_
  11.2 92.3 %shard_map.262 = (bf16[8,256,512]{2,1,0:T(8,128)(2,1)}, bf16[8,256,512]{2,1,0:T(8,128)(2,1)}, bf16[8,256,256]{2,1,0:T(8,128)(2,1)}, bf16[8,256,256]{2,1,0:T(8,12...) custom-call(bf16[256,512]{1,0:T(8,128)(2,1)} %refs_0_.3, ...), custom_call_target="tpu_custom_call" | custom-call | bytes 31488000 | tf_op jit(solution)/shard_map/pallas_call | solution.py:303
  103.5 0.0 all-gather.3.cloned.1.call-update
  103.5 0.0 all-gather.5.cloned.1.call-start
  104.2 23.4 %attn_forward.1 = (bf16[1024,2048]{1,0:T(8,128)(2,1)}, bf16[1024,512]{1,0:T(8,128)(2,1)}, bf16[1024,256]{1,0:T(8,128)(2,1)}, bf16[1024,256]{1,0:T(8,128)(2,1)}, ...) custom-call(s32[1]{0:T(128)S(6)} %copy.30.lengths, ...), custom_call_target="tpu_custom_call" | custom-call | flops 8589934592 | bytes 41943040 | tf_op jit(solution)/shard_map/attn_forward/pallas_call | solution.py:429
  127.6 150.2 %shard_map.263 = (bf16[8,256,1536]{2,1,0:T(8,128)(2,1)}, bf16[8,256,1536]{2,1,0:T(8,128)(2,1)}, bf16[1024,2048]{1,0:T(8,128)(2,1)}) custom-call(bf16[256,1536]{1,0:T(8,128)(2,1)} %refs_0_.4, bf16[256,1536]{1,0:T(8,128)(2,1)} %refs_1_.3, bf16[1024,2048]{1,0:T(8,128)(2,1)} %get-tuple-element.93.refs_2_), custom_call_target="tpu_custom_call" | custom-call | bytes 47185920 | tf_op jit(solution)/shard_map/pallas_call | solution.py:303
  277.8 0.0 all-gather.5.cloned.1.call-update
  277.8 0.0 reduce-scatter.3.cloned.1.call-start
  277.9 27.7 %mlp_forward.1 = (bf16[1024,2048]{1,0:T(8,128)(2,1)}, bf16[1024,2048]{1,0:T(8,128)(2,1)}, bf16[1024,1536]{1,0:T(8,128)(2,1)}, bf16[1024,1536]{1,0:T(8,128)(2,1)}, bf16[1024,1536]{1,0:T(8,128)(2,1)}) custom-call(s32[1]{0:T(128)S(6)} %copy.30.lengths, bf16[1024,2048]{1,0:T(8,128)(2,1)} %x.7, bf16[1024,2048]{1,0:T(8,128)(2,1)} %get-tuple-element.95.attn.refs_1_, ...), custom_call_target="tpu_custom_call" | custom-call | flops 12884901888 | bytes 52428800 | tf_op jit(solution)/shard_map/mlp_forward/pallas_call | solution.py:504
  305.6 11.9 %convolution_convert_fusion = bf16[2048,1536]{1,0:T(8,128)(2,1)} fusion(bf16[1024,2048]{1,0:T(8,128)(2,1)} %get-tuple-element.101.gm, bf16[1024,1536]{1,0:T(8,128)(2,1)} %get-tuple-element.102.hid), kind=kOutput, calls=%fused_computation | convolution fusion | flops 6445596672 | bytes 13631488 | tf_op jit(solution)/shard_map/dot_general | solution.py:21
  317.5 0.0 all-gather.3.cloned.1.call-done.wd
  317.5 20.1 %mlp_backward.2 = (bf16[1024,768]{1,0:T(8,128)(2,1)}, bf16[1024,768]{1,0:T(8,128)(2,1)}, f32[1024,2048]{1,0:T(8,128)}, f32[1024,2048]{1,0:T(8,128)}) custom-call(bf16[1024,2048]{1,0:T(8,128)(2,1)} %get-tuple-element.101.gm, bf16[1024,1536]{1,0:T(8,128)(2,1)} %get-tuple-element.102.hid, bf16[1024,1536]{1,0:T(8,128)(2,1)} %get-tuple-element.103.gu_in, ...), custom_call_target="tpu_custom_call" | custom-call | flops 12884901888 | bytes 41943040 | tf_op jit(solution)/shard_map/mlp_backward/pallas_call | solution.py:532
  337.6 0.6 all-gather.5.cloned.1.call-done.wd
  338.2 26.3 %mlp_backward.3 = (bf16[1024,768]{1,0:T(8,128)(2,1)}, bf16[1024,768]{1,0:T(8,128)(2,1)}, bf16[1024,2048]{1,0:T(8,128)(2,1)}, bf16[1024,2048]{1,0:T(8,128)(2,1)}, f32[1,2048]{1,0:T(1,128)}) custom-call(bf16[1024,2048]{1,0:T(8,128)(2,1)} %get-tuple-element.101.gm, bf16[1024,1536]{1,0:T(8,128)(2,1)} %get-tuple-element.102.hid, ...), custom_call_target="tpu_custom_call" | custom-call | flops 12884901888 | bytes 41943040 | tf_op jit(solution)/shard_map/mlp_backward/pallas_call | solution.py:532
  364.5 113.1 %shard_map.264 = (bf16[256,768]{1,0:T(8,128)(2,1)}, bf16[256,768]{1,0:T(8,128)(2,1)}, bf16[256,768]{1,0:T(8,128)(2,1)}, bf16[1024,2048]{1,0:T(8,128)(2,1)}, bf16...) custom-call(bf16[1024,2048]{1,0:T(8,128)(2,1)} %get-tuple-element.98.refs_0_, ...), custom_call_target="tpu_custom_call" | custom-call | bytes 37748736 | tf_op jit(solution)/shard_map/pallas_call | solution.py:1025
  477.6 0.0 reduce-scatter.3.cloned.1.call-update
  477.6 0.0 reduce-scatter.5.cloned.1.call-start
  477.7 0.5 reduce-scatter.5.cloned.1.call-update
  478.2 43.6 %attn_backward.1 = (bf16[1024,2048]{1,0:T(8,128)(2,1)}, bf16[1024,2048]{1,0:T(8,128)(2,1)}, bf16[1024,512]{1,0:T(8,128)(2,1)}, bf16[1024,1536]{1,0:T(8,128)(2,1)...) custom-call(s32[1]{0:T(128)S(6)} %copy.30.lengths, ...), custom_call_target="tpu_custom_call" | custom-call | flops 21474836480 | bytes 52428800 | tf_op jit(solution)/shard_map/attn_backward/pallas_call | solution.py:669
  521.8 166.0 %shard_map.265 = (bf16[256,1536]{1,0:T(8,128)(2,1)}, bf16[256,512]{1,0:T(8,128)(2,1)}, bf16[1024,2048]{1,0:T(8,128)(2,1)}, f32[40,128]{1,0:T(8,128)}) custom-call(bf16[1024,2048]{1,0:T(8,128)(2,1)} %get-tuple-element.127.refs_0_, bf16[1024,2048]{1,0:T(8,128)(2,1)} %get-tuple-element.126.refs_1_.grad_hidden, bf16[1024,1536]{1,0:T(8,128)(2,1)} %get-tuple-element.128.refs_2_, ...), custom_call_target="tpu_custom_call" | custom-call | bytes 33554432 | tf_op jit(solution)/shard_map/pallas_call | solution.py:1025
  687.9 0.8 slice_reduce_fusion
  688.7 0.6 slice.35
  689.2 0.7 slice_bitcast_fusion
  690.0 0.6 dynamic_slice.7
  690.6 0.6 dynamic_slice.6
  691.9 0.5 divide_sqrt_fusion
  692.4 1.3 slice_bitcast_fusion.2
  693.7 0.0 reduce-scatter.3.cloned.1.call-done.refs_5_
  693.7 44.6 %reduce-scatter.5.cloned.1.call-done.refs_6_ = bf16[256,1536]{1,0:T(8,128)(2,1)} async-done(((bf16[2048,1536]{1,0:T(8,128)(2,1)}), bf16[256,1536]{1,0:T(8,128)(2,1)}) %reduce-scatter.5.cloned.1.call-update) | async-done | bytes 786448 | tf_op jit(solution)/shard_map/reduce_scatter | solution.py:1105
  738.3 12.1 %finish.1 = (bf16[1024,2048]{1,0:T(8,128)(2,1)}, f32[256,512]{1,0:T(8,128)}, f32[256,512]{1,0:T(8,128)}, f32[256,256]{1,0:T(8,128)}, f32[256,256]{1,0:T(8,128)},...) custom-call(bf16[1024,2048]{1,0:T(8,128)(2,1)} %x.7, ...), custom_call_target="tpu_custom_call" | custom-call | flops 41943040 | bytes 31457280 | tf_op jit(solution)/shard_map/finish/pallas_call | solution.py:711
Async XLA Ops:
  7.2 310.3 %all-gather.3.cloned.1.call-start = ((), (), s32[]{:S(2)}) async-start(), calls=%async_computation.2 | async-start | bytes 3538944 | tf_op jit(solution)/shard_map/all_gather | solution.py:1086
  103.5 234.6 %all-gather.5.cloned.1.call-start = ((), (), s32[]{:S(2)}) async-start(), calls=%async_computation.3 | async-start | bytes 3538944 | tf_op jit(solution)/shard_map/all_gather | solution.py:1099
  277.8 415.9 %reduce-scatter.3.cloned.1.call-start = ((), (), s32[]{:S(2)}) async-start(), calls=%async_computation.4 | async-start | bytes 3538944 | tf_op jit(solution)/shard_map/reduce_scatter | solution.py:1121
  477.6 260.7 %reduce-scatter.5.cloned.1.call-start = ((), (), s32[]{:S(2)}) async-start(), calls=%async_computation.5 | async-start | bytes 7077888 | tf_op jit(solution)/shard_map/reduce_scatter | solution.py:1105
Sparse Core Ops, SparseCore 0:
  103.6 82.4 all-gather.2
  277.9 60.1 all-gather.4
  477.7 88.5 reduce-scatter.2
  569.7 168.4 reduce-scatter.4
